TPU v7x, 128 devices: a whole 4x4x4 slice. The times are simulated.
128 devices in a mesh: dp: 8 (over y, core), prompt: 16 (over x, z).
Axes of the slice: x: 4, y: 4, z: 4, core: 2. Of those that a mesh axis runs over, the one named last changes fastest.
Arguments:
- cand_hidden: bfloat16 [16, 8, 128, 1024], P('prompt', 'dp')
- ref_hidden: bfloat16 [32, 16, 128, 1024], P('dp', 'prompt')
- cand_ids: int32 [16, 8, 128], P('prompt', 'dp'), may hold values from 0 to 50264
- ref_ids: int32 [32, 16, 128], P('dp', 'prompt'), may hold values from 0 to 50264
- cand_len: int32 [16, 8], P('prompt', 'dp'), may hold values from 32 to 128
- reference_length: int32 [32, 16], P('dp', 'prompt'), may hold values from 32 to 128
- idf_table: float32 [50265], replicated, may hold values from 1 to 10
- up_weight: bfloat16 [1024, 4096], replicated, may hold values from -0.1875 to 0.1875
- up_bias: float32 [4096], replicated, may hold values from -3 to 3
- down_weight: bfloat16 [4096, 1024], replicated, may hold values from -0.09375 to 0.09375
- down_bias: float32 [1024], replicated, may hold values from -3 to 3
- norm_gain: float32 [1024], replicated, may hold values from 0.3 to 3
- norm_bias: float32 [1024], replicated, may hold values from -3 to 3
- pair_cand: int32 [8, 16, 32], P('dp', 'prompt'), may hold values from 0 to 7
- pair_ref: int32 [8, 16, 32], P('dp', 'prompt'), may hold values from 0 to 63
- pair_count: int32 [8, 16], P('dp', 'prompt'), may hold values from 8 to 32, as said below
Outputs:
- pair_scores: float32 [3, 8, 16, 32], P(None, 'dp', 'prompt')
- totals: float32 [3], replicated
Inputs may be any that keep to these rules, and one draw needn't show every extreme that they name: Slots from pair_count on are not live; some device has all 32 slots live.
All inputs are finite; a program needn't handle non-finite values.
Results may differ from a plain program's by a relative error of at most 0.0003.
Values may be sent and summed in bfloat16 or wider, within the bound.
No kernel may reach another device: no remote copies, remote signals or barrier semaphores. Data moves between devices by JAX's collectives and lax.ppermute only.
A program may use at most 128 MiB of HBM per device.

v0:
```python
import jax
import jax.numpy as jnp
from jax import lax
from jax.sharding import PartitionSpec as P


def encode_rows(hidden, up_weight, up_bias, down_weight, down_bias, norm_gain, norm_bias):
    preactivation_hidden = jnp.dot(hidden, up_weight, preferred_element_type=jnp.float32) + up_bias
    activated = jax.nn.gelu(preactivation_hidden, approximate=False).astype(jnp.bfloat16)
    summed = (
        hidden.astype(jnp.float32)
        + jnp.dot(activated, down_weight, preferred_element_type=jnp.float32)
        + down_bias
    )
    center = jnp.mean(summed, axis=-1, keepdims=True)
    spread = jnp.mean(jnp.square(summed - center), axis=-1, keepdims=True)
    normed = (summed - center) * lax.rsqrt(spread + 1e-05) * norm_gain + norm_bias
    magnitude = jnp.sum(jnp.square(normed), axis=-1, keepdims=True)
    return (normed * lax.rsqrt(magnitude + 1e-06)).astype(jnp.bfloat16)


def token_idf_weights(ids, lengths, idf_table):
    positions = jnp.arange(ids.shape[-1], dtype=jnp.int32)
    live_tokens = positions[None, :] < lengths[:, None]
    return jnp.where(live_tokens, jnp.take(idf_table, ids, axis=0), 0.0).astype(jnp.bfloat16)


def on_device(
    cand_hidden,
    ref_hidden,
    cand_ids,
    ref_ids,
    cand_len,
    reference_length,
    idf_table,
    up_weight,
    up_bias,
    down_weight,
    down_bias,
    norm_gain,
    norm_bias,
    pair_cand,
    pair_ref,
    pair_count,
):
    seq_len = cand_hidden.shape[2]
    width = cand_hidden.shape[3]

    def encode_side(hidden, ids, lengths):
        units = encode_rows(
            hidden.reshape(-1, width),
            up_weight,
            up_bias,
            down_weight,
            down_bias,
            norm_gain,
            norm_bias,
        )
        weights = token_idf_weights(ids.reshape(-1, seq_len), lengths.reshape(-1), idf_table)
        return (units.reshape(hidden.shape), weights.reshape(hidden.shape[:3]))

    ref_unit, ref_weight = encode_side(ref_hidden, ref_ids, reference_length)
    candidate_normalized, cand_weight = encode_side(cand_hidden, cand_ids, cand_len)
    cand_all, cand_wall = (
        lax.all_gather(candidate_normalized, "dp", axis=1, tiled=True),
        lax.all_gather(cand_weight, "dp", axis=1, tiled=True),
    )
    cand_all = cand_all.reshape(-1, seq_len, width)
    cand_wall = cand_wall.reshape(-1, seq_len)
    cand_pick = pair_cand.reshape(-1)
    slot_total = cand_pick.shape[0]
    ref_pick = pair_ref.reshape(-1)
    groups = lax.axis_size("prompt")
    ref_major = ref_pick // groups
    ref_minor = ref_pick % groups
    order = jnp.argsort(ref_minor, stable=True)
    sorted_minor = jnp.take(ref_minor, order, axis=0)
    sorted_major = jnp.take(ref_major, order, axis=0)
    sorted_cand = jnp.take(cand_pick, order, axis=0)
    paired_normalized = jnp.take(cand_all, sorted_cand, axis=0)
    pair_weight = jnp.take(cand_wall, sorted_cand, axis=0)
    initial = (
        jnp.zeros((slot_total, seq_len), jnp.float32),
        jnp.zeros((slot_total, seq_len), jnp.float32),
        jnp.zeros((slot_total, seq_len), jnp.bfloat16),
    )
    ref_all, ref_wall = (
        lax.all_gather(ref_unit, "prompt", axis=1, tiled=True),
        lax.all_gather(ref_weight, "prompt", axis=1, tiled=True),
    )
    shard_span = ref_all.shape[1]
    inside = (sorted_minor >= 0) & (sorted_minor < 0 + shard_span)
    within = sorted_major * shard_span + jnp.clip(sorted_minor - 0, 0, shard_span - 1)
    selected_normalized = jnp.take(ref_all.reshape(-1, seq_len, width), within, axis=0)
    chosen_weight = jnp.take(ref_wall.reshape(-1, seq_len), within, axis=0)
    cosine_similarity = jnp.einsum(
        "uqg,uog->uqo", paired_normalized, selected_normalized, preferred_element_type=jnp.float32
    )
    row_best = jnp.max(
        jnp.where(chosen_weight[:, None, :] > 0, cosine_similarity, -10000.0), axis=2
    )
    col_best = jnp.max(jnp.where(pair_weight[:, :, None] > 0, cosine_similarity, -10000.0), axis=1)
    keeper = inside[:, None]
    updated = []
    for stored, fresh in zip(initial, (row_best, col_best, chosen_weight)):
        updated.append(jnp.where(keeper, fresh, stored))
    row_best, col_best, ref_chosen = tuple(updated)
    cand_float = pair_weight.astype(jnp.float32)
    ref_float = ref_chosen.astype(jnp.float32)
    precision_sorted = jnp.sum(cand_float * row_best, axis=1) / jnp.sum(cand_float, axis=1)
    recall_sorted = jnp.sum(ref_float * col_best, axis=1) / jnp.sum(ref_float, axis=1)
    inverse = jnp.argsort(order)
    precision = jnp.take(precision_sorted, inverse, axis=0)
    recall = jnp.take(recall_sorted, inverse, axis=0)
    fmeasure = 2.0 * precision * recall / jnp.maximum(precision + recall, 0.7)
    live_slots = jnp.arange(slot_total, dtype=jnp.int32) < pair_count.reshape(1)
    stacked = jnp.where(live_slots[None, :], jnp.stack([precision, recall, fmeasure]), 0.0)
    score_sums, live_total = lax.psum(
        (jnp.sum(stacked, axis=1), jnp.sum(live_slots.astype(jnp.float32))), ("dp", "prompt")
    )
    return (stacked.reshape(3, 1, 1, slot_total), score_sums / live_total)


def solution(mesh):
    placed = (
        P("prompt", "dp", None, None),
        P("dp", "prompt", None, None),
        P("prompt", "dp", None),
        P("dp", "prompt", None),
        P("prompt", "dp"),
        P("dp", "prompt"),
        P(),
        P(),
        P(),
        P(),
        P(),
        P(),
        P(),
        P("dp", "prompt", None),
        P("dp", "prompt", None),
        P("dp", "prompt"),
    )
    return jax.shard_map(
        on_device,
        mesh=mesh,
        in_specs=placed,
        out_specs=(P(None, "dp", "prompt", None), P()),
        check_vma=False,
    )
```

profile of v0, /device:TPU:1, one launch (start us, length us, event | category | flops | bytes accessed | tf_op | source)
XLA Modules:
  0.0 263.4 jit_solution(12290140118969234346)
XLA Ops:
  7.2 0.0 copy-start
  7.2 0.0 copy-start.2
  7.2 0.0 copy-start.3
  7.2 0.0 all-gather.6.cloned.1.call-start
  7.2 13.2 %fusion.169 = (f32[128]{0:T(128)S(1)}, f32[128,1024]{1,0:T(8,128)S(1)}) fusion(f32[1024]{0:T(1024)} %param.30, bf16[4096,1024]{1,0:T(8,128)(2,1)} %param.29, bf16[1024,4096]{1,0:T(8,128)(2,1)} %param.27, f32[4096]{0:T(1024)} %param.28, bf16[1,1,128,1024]{3,2,1,0:T(8,128)(2,1)} %param.20), kind=kOutput, calls=%fused_computation.264 | convolution fusion | flops 2182610944 | bytes 17584640 | tf_op jit(solution)/shard_map/dot_general | solution.py:12
  20.5 0.0 copy-start.7
  20.5 0.0 copy-start.8
  20.5 0.0 copy-start.9
  20.5 0.2 multiply_reduce_fusion.3
  20.7 0.0 copy-done.2
  20.7 0.0 copy-done.3
  20.7 0.3 multiply_reduce_fusion.2
  21.0 0.9 multiply_convert_fusion.1
  21.9 0.0 all-gather.6.cloned.1.call-update
  21.9 0.2 all-gather.4.cloned.1.call-start
  22.1 0.0 copy-done.7
  22.2 0.0 copy-done.8
  22.2 0.0 copy-done.9
  22.2 30.3 %fusion.168 = (f32[512]{0:T(512)S(1)}, f32[512,1024]{1,0:T(8,128)S(1)}) fusion(f32[1024]{0:T(1024)S(1)} %copy-done.9, bf16[4096,1024]{1,0:T(8,128)(2,1)} %param.29, bf16[512,1024]{1,0:T(8,128)(2,1)S(1)} %bitcast.84, bf16[1024,4096]{1,0:T(8,128)(2,1)} %param.27, f32[4096]{0:T(1024)S(1)} %copy-done.8), kind=kOutput, calls=%fused_computation.263 | convolution fusion | flops 8730443776 | bytes 19945472 | tf_op jit(solution)/shard_map/dot_general | solution.py:12
  52.5 0.4 multiply_reduce_fusion.1
  52.8 0.9 multiply_reduce_fusion
  53.7 0.0 copy-start.6
  53.7 0.0 copy-start.10
  53.8 1.5 multiply_convert_fusion
  55.2 0.0 copy-start.1
  55.2 0.0 copy-start.4
  55.2 0.0 copy-start.5
  55.2 0.0 all-gather.4.cloned.1.call-update
  56.6 0.0 copy-done.6
  56.6 0.0 copy-done
  56.6 1.1 gather_fusion
  57.8 12.1 %all_gather.12 = bf16[1,8,128]{2,0,1:T(2,128)(2,1)S(1)} all-gather(bf16[1,1,128]{2,0,1:T(2,128)(2,1)S(1)} %fusion.100), channel_id=1, replica_groups=mesh['dp'=8,'prompt'=16] {'dp'}, dimensions={1}, use_global_device_ids=true | all-gather | bytes 2304 | tf_op jit(solution)/shard_map/all_gather | solution.py:66
  69.8 0.0 copy-done.10
  69.9 1.6 sort.34
  71.5 0.7 gather_fusion.7
  72.2 0.7 gather_fusion.8
  72.9 0.0 copy-done.1
  72.9 0.7 gather_fusion.6
  73.6 0.0 copy-done.4
  73.6 3.1 %gather_fusion.2 = bf16[512]{0:T(512)(128)(2,1)S(1)} fusion(f32[50265]{0:T(1024)S(1)} %copy-done, s32[1024]{0:T(1024)S(1)} %pad_clamp_fusion.2), kind=kCustom, calls=%fused_computation.7 | custom fusion | bytes 4096 | tf_op jit(solution)/shard_map/jit(_take)/gather | solution.py:25
  76.8 0.0 copy-done.5
  76.8 0.1 fusion.98
  76.8 20.3 %all_gather.13 = bf16[4,16,128]{2,0,1:T(4,128)(2,1)S(1)} all-gather(bf16[4,1,128]{2,0,1:T(4,128)(2,1)S(1)} %fusion.98), channel_id=1, replica_groups=mesh['dp'=8,'prompt'=16] {'prompt'}, dimensions={1}, use_global_device_ids=true | all-gather | bytes 17408 | tf_op jit(solution)/shard_map/all_gather | solution.py:89
  97.2 1.6 sort.35
  98.8 0.6 convert_reduce_fusion.2
  99.4 0.6 gather_fusion.1
  100.0 0.6 gather_fusion.3
  100.6 0.1 broadcast_compare_fusion
  100.7 0.1 broadcast_compare_fusion.1
  100.8 0.0 all-gather.6.cloned.1.call-done
  100.8 6.9 %gather_fusion.4 = bf16[32,128,1024]{2,1,0:T(8,128)(2,1)} fusion(bf16[8,128,1024]{2,1,0:T(8,128)(2,1)} %bitcast.74, s32[1024]{0:T(1024)S(1)} %get-tuple-element.39), kind=kCustom, calls=%fused_computation.9 | custom fusion | bytes 16777344 | tf_op jit(solution)/shard_map/jit(_take)/gather | solution.py:80
  107.7 62.4 %all-gather.4.cloned.1.call-done = bf16[4,16,128,1024]{3,2,1,0:T(8,128)(2,1)} async-done(((bf16[4,1,128,1024]{3,2,1,0:T(8,128)(2,1)}), bf16[4,16,128,1024]{3,2,1,0:T(8,128)(2,1)}) %all-gather.4.cloned.1.call-update) | async-done | bytes 16777232 | tf_op jit(solution)/shard_map/all_gather | solution.py:88
  170.1 10.8 %gather_fusion.5 = bf16[32,128,1024]{2,1,0:T(8,128)(2,1)} fusion(bf16[64,128,1024]{2,1,0:T(8,128)(2,1)} %bitcast.75, s32[1024]{0:T(1024)S(1)} %get-tuple-element.38), kind=kCustom, calls=%fused_computation.10 | custom fusion | bytes 16777344 | tf_op jit(solution)/shard_map/jit(_take)/gather | solution.py:94
  180.8 7.5 %select_reduce_fusion = (f32[32,128]{1,0:T(8,128)S(1)}, f32[32,128]{1,0:T(8,128)S(1)}) fusion(pred[32,128]{1,0:T(8,128)(4,1)S(1)} %broadcast_compare_fusion, pred[32,128]{1,0:T(8,128)(4,1)S(1)} %broadcast_compare_fusion.1, bf16[32,128,1024]{2,1,0:T(8,128)(2,1)} %gather_fusion.5, pred[32]{0:T(512)(128)(4,1)S(1)} %get-tuple-element.22, ...), kind=kOutput, calls=%fused_computation.73 | convolution fusion | flops 1084219392 | bytes 16818240 | tf_op jit(solution)/shard_map/uqg,uog->uqo/dot_general | solution.py:96
  188.4 0.2 convert_reduce_fusion.1
  188.6 0.7 gather_fusion.9
  189.3 0.7 gather_fusion.10
  190.1 0.1 fusion.96
  190.2 64.7 %all-reduce = (f32[3]{0:T(128)S(1)}, f32[]{:T(128)}) all-reduce(f32[3]{0:T(128)S(1)} %fusion.96, f32[]{:T(128)} %convert_reduce_fusion.2), channel_id=1, replica_groups=mesh['dp'=8,'prompt'=16] {'dp','prompt'}, use_global_device_ids=true, to_apply=%region_15.18 | all-reduce | flops 4 | bytes 32 | tf_op jit(solution)/shard_map/psum | solution.py:118
  254.9 1.2 broadcast_divide_fusion
  256.0 0.6 broadcast_select_fusion.3
  (28 shorter events, 0.2 us)
Async XLA Ops:
  7.2 49.4 %copy-start = (f32[50265]{0:T(1024)S(1)}, f32[50265]{0:T(1024)}, u32[]{:S(2)}) copy-start(f32[50265]{0:T(1024)} %param.26) | copy-start | bytes 603184
  7.2 13.5 %copy-start.2 = (f32[1024]{0:T(1024)S(1)}, f32[1024]{0:T(1024)}, u32[]{:S(2)}) copy-start(f32[1024]{0:T(1024)} %param.32) | copy-start | bytes 12292
  7.2 13.5 %copy-start.3 = (f32[1024]{0:T(1024)S(1)}, f32[1024]{0:T(1024)}, u32[]{:S(2)}) copy-start(f32[1024]{0:T(1024)} %param.31) | copy-start | bytes 12292
  7.2 93.6 %all-gather.6.cloned.1.call-start = ((), (), s32[]{:S(2)}) async-start(), calls=%async_computation.1 | async-start | bytes 2359296 | tf_op jit(solution)/shard_map/all_gather | solution.py:65
  20.5 1.7 copy-start.7
  20.5 1.7 copy-start.8
  20.5 1.7 copy-start.9
  21.9 148.1 %all-gather.4.cloned.1.call-start = ((), (), s32[]{:S(2)}) async-start(), calls=%async_computation | async-start | bytes 17825792 | tf_op jit(solution)/shard_map/all_gather | solution.py:88
  53.7 2.8 %copy-start.6 = (s32[1,1,128]{2,1,0:T(1,128)S(1)}, s32[1,1,128]{2,1,0:T(1,128)}, u32[]{:S(2)}) copy-start(s32[1,1,128]{2,1,0:T(1,128)} %param.22) | copy-start | bytes 1540
  53.7 16.1 %copy-start.10 = (s32[1,1,32]{2,1,0:T(1,128)S(1)}, s32[1,1,32]{2,1,0:T(1,128)}, u32[]{:S(2)}) copy-start(s32[1,1,32]{2,1,0:T(1,128)} %param.34) | copy-start | bytes 388
  55.2 17.7 %copy-start.1 = (s32[1,1,32]{2,1,0:T(1,128)S(1)}, s32[1,1,32]{2,1,0:T(1,128)}, u32[]{:S(2)}) copy-start(s32[1,1,32]{2,1,0:T(1,128)} %param.33) | copy-start | bytes 388
  55.2 18.4 %copy-start.4 = (s32[4,1,128]{2,1,0:T(1,128)S(1)}, s32[4,1,128]{2,1,0:T(1,128)}, u32[]{:S(2)}) copy-start(s32[4,1,128]{2,1,0:T(1,128)} %param.23) | copy-start | bytes 6148
  55.2 21.6 %copy-start.5 = (s32[4,1]{0,1:T(1,128)S(1)}, s32[4,1]{0,1:T(1,128)}, u32[]{:S(2)}) copy-start(s32[4,1]{0,1:T(1,128)} %param.25) | copy-start | bytes 52
Sparse Core Ops, SparseCore 0:
  22.0 28.8 all-gather.5
  55.4 114.6 all-gather.3
where the time goes:
time: 264 us; the launch traced here: 263 us
  blocking collectives  97 us (37%)
  waiting for transfers between devices  62.4 us (24%)
  matrix products  51 us (19%)
  local copies, waits for them, and re-layouts  26.7 us (10%)
  between operations  15.6 us (6%)
  other arithmetic  10.3 us (4%)
    psum x1, blocking collectives, on_device(): lax.psum((jnp.sum(stacked, axis=1), jnp.sum(live_slots.astype(jnp.float32...  64.7 us
    all_gather x1, waiting for transfers between devices, on_device(): lax.all_gather(ref_unit, 'prompt', axis=1, tiled=True)  62.4 us
    dot_general x2, matrix products, encode_rows(): jnp.dot(activated, down_weight, preferred_element_type=jnp.float32)  43.5 us
    all_gather x1, blocking collectives, on_device(): lax.all_gather(ref_weight, 'prompt', axis=1, tiled=True)  20.3 us
    all_gather x1, blocking collectives, on_device(): lax.all_gather(cand_weight, 'dp', axis=1, tiled=True)  12.1 us
    gather x1, local copies, waits for them, and re-layouts, on_device(): jnp.take(ref_all.reshape(-1, seq_len, width), within, axis=0)  10.8 us
    dot_general x1, matrix products, on_device(): jnp.einsum('uqg,uog->uqo', paired_normalized, selected_normalized, prefer...  7.55 us
    gather x1, local copies, waits for them, and re-layouts, on_device(): paired_normalized = jnp.take(cand_all, sorted_cand, axis=0)  6.89 us
  transfers between devices with their start and end apart: 2, of which 1 were waited for; matrix products, arithmetic and copies ran while one was open for 20% of the time, Pallas kernels for 0%

commit v1 on v0

v1 whole, which is shorter than its diff:
```python
import functools

import jax
import jax.numpy as jnp
from jax import lax
from jax.experimental import pallas as pl
from jax.experimental.pallas import tpu as pltpu
from jax.sharding import PartitionSpec as P

D = 1024
L = 128
SLOTS = 32
TABLE_ROWS = 400
AXES = ("dp", "prompt")
GRID = [(y, c, x, z) for y in range(4) for c in range(2) for x in range(4) for z in range(4)]


def number(y, c, x, z):
    return (((y % 4) * 2 + c) * 4 + x % 4) * 4 + z % 4


def send(value, where):
    return lax.ppermute(value, AXES, [(number(*a), number(*where(*a))) for a in GRID])


def along_x(step):
    return lambda y, c, x, z: (y, c, x + (step if c == 0 else -step), z)


def along_first(step):
    return lambda y, c, x, z: (y + step, c, x, z) if c == 0 else (y, c, x, z + step)


def along_second(step):
    return lambda y, c, x, z: (y, c, x, z + step) if c == 0 else (y + step, c, x, z)


def along_z(step):
    return lambda y, c, x, z: (y, c, x, z + step)


def to_other_core(y, c, x, z):
    return (y, 1 - c, x, z)


def encode_kernel(
    sub, clen_ref, rlen_ref, cid_ref, rid_ref, tbl_ref, ch_ref, rh_ref, up, upb, dn, dnb, gain, bias,
    co_ref, ro_ref, x_ref, acc_ref,
):
    step = pl.program_id(0)

    def token_weights(ids, length):
        high, low = ids >> 7, ids & 127
        hot = (lax.broadcasted_iota(jnp.int32, (TABLE_ROWS, L), 0) == high).astype(jnp.bfloat16)
        rows = lax.dot_general(
            tbl_ref[...], hot, (((0,), (0,)), ((), ())), preferred_element_type=jnp.float32
        )
        mine = lax.broadcasted_iota(jnp.int32, (128, L), 0) == low
        value = jnp.sum(jnp.where(mine, rows, 0.0), axis=0, keepdims=True)
        live = lax.broadcasted_iota(jnp.int32, (1, L), 1) < length
        return jnp.where(live, value, 0.0)

    @pl.when(step == 0)
    def _():
        x_ref[0:L, :] = ch_ref[0]
        for q in range(4):
            x_ref[L * (q + 1) : L * (q + 2), :] = rh_ref[q]
        row = lax.broadcasted_iota(jnp.int32, (16, L), 0)
        co_ref[L:, :] = jnp.zeros((16, D), jnp.bfloat16)
        ro_ref[4 * L :, :] = jnp.zeros((16, D), jnp.bfloat16)
        w = token_weights(cid_ref[...], clen_ref[0])
        co_ref[L:, 0:L] = jnp.where(row == 0, w, 0.0).astype(jnp.bfloat16)
        block = jnp.zeros((16, L), jnp.float32)
        for q in range(4):
            block = jnp.where(row == q, token_weights(rid_ref[q : q + 1, :], rlen_ref[q]), block)
        ro_ref[4 * L :, 0:L] = block.astype(jnp.bfloat16)

    w = up.shape[1] // sub
    x = x_ref[...]
    pre = [
        jnp.dot(x, up[:, k * w : (k + 1) * w], preferred_element_type=jnp.float32)
        + upb[:, k * w : (k + 1) * w]
        for k in range(sub)
    ]
    part = None
    for k in range(sub):
        h = pre[k]
        act = (0.5 * h * (lax.erf(h * 0.7071067811865476) + 1.0)).astype(jnp.bfloat16)
        d = jnp.dot(act, dn[k * w : (k + 1) * w, :], preferred_element_type=jnp.float32)
        part = d if part is None else part + d

    @pl.when(step == 0)
    def _():
        acc_ref[...] = part

    @pl.when(step > 0)
    def _():
        acc_ref[...] += part

    @pl.when(step == pl.num_programs(0) - 1)
    def _():
        for c in range(0, 5 * L, 64):
            r = slice(c, c + 64)
            s = x_ref[r, :].astype(jnp.float32) + acc_ref[r, :] + dnb[...]
            center = jnp.mean(s, axis=-1, keepdims=True)
            e = s - center
            spread = jnp.mean(e * e, axis=-1, keepdims=True)
            y = e * lax.rsqrt(spread + 1e-5) * gain[...] + bias[...]
            m = jnp.sum(y * y, axis=-1, keepdims=True)
            unit = (y * lax.rsqrt(m + 1e-6)).astype(jnp.bfloat16)
            if c < L:
                co_ref[r, :] = unit
            else:
                ro_ref[c - L : c - L + 64, :] = unit


def encode(ch, rh, cids, rids, clen, rlen, table, up, upb, dn, dnb, gain, bias, f=1024, sub=4):
    def full(a):
        return pl.BlockSpec(a.shape, lambda i: (0,) * a.ndim, pipeline_mode=pl.Buffered(1))

    smem = pl.BlockSpec(memory_space=pltpu.SMEM)
    outs = [
        jax.ShapeDtypeStruct((L + 16, D), jnp.bfloat16),
        jax.ShapeDtypeStruct((4 * L + 16, D), jnp.bfloat16),
    ]
    return pl.pallas_call(
        functools.partial(encode_kernel, sub),
        grid=(up.shape[1] // f,),
        in_specs=[smem, smem, full(cids), full(rids), full(table), full(ch), full(rh)]
        + [
            pl.BlockSpec((D, f), lambda i: (0, i)),
            pl.BlockSpec((1, f), lambda i: (0, i)),
            pl.BlockSpec((f, D), lambda i: (i, 0)),
            full(dnb),
            full(gain),
            full(bias),
        ],
        out_specs=[pl.BlockSpec(o.shape, lambda i: (0, 0)) for o in outs],
        out_shape=outs,
        scratch_shapes=[pltpu.VMEM((5 * L, D), jnp.bfloat16), pltpu.VMEM((5 * L, D), jnp.float32)],
        compiler_params=pltpu.CompilerParams(
            dimension_semantics=("arbitrary",), vmem_limit_bytes=60 << 20
        ),
        name="encode",
    )(clen, rlen, cids, rids, table, ch, rh, up, upb, dn, dnb, gain, bias)


SLOT_BUFS = 4


def pair_kernel(
    pos_ref, l0, l1, l2, l3,
    own4, d1, d2, d3, d4, e0, e1, e2, e3, e4, r0, ra1, ra2, rb,
    out_ref, cbuf, rbuf, wbuf, todo, sem_c, sem_r, sem_w,
):
    y, core, x, z = pos_ref[0], pos_ref[1], pos_ref[2], pos_ref[3]
    n = jnp.int32(0)
    for lst, dz in ((l0, 0), (l1, 3), (l2, 1), (l3, 2)):
        zj = (z + dz) & 3

        def scan(s, n, lst=lst, dz=dz, zj=zj):
            c = lst[0, s]
            r = lst[0, SLOTS + s]
            mine = (r & 3) == z

            @pl.when(mine)
            def _():
                kc = c & 1
                dy = ((c >> 1) - y) & 3
                u1 = jnp.where(kc == 0, dy, dz)
                u2 = jnp.where(kc == 0, dz, dy)
                i1 = (u1 == 3) * 1 + (u1 == 1) * 2 + (u1 == 2) * 3
                g2 = (u2 == 3) * 1 + (u2 == 1) * 2 + (u2 == 2) * 3
                g2 = jnp.where((g2 == 3) & (i1 >= 2), 4, g2)
                src = g2 + jnp.where(kc == core, 0, 5)
                row = jnp.where(g2 == 4, i1 - 2, i1)
                dx = (((r & 15) >> 2) - x) & 3
                back = jnp.where(core == 0, 3, 1)
                rs = jnp.where(dx == 0, 0, jnp.where(dx == 2, 3, jnp.where(dx == back, 1, 2)))
                todo[0, n] = src
                todo[1, n] = row
                todo[2, n] = rs
                todo[3, n] = r >> 4
                todo[4, n] = zj * SLOTS + s

            return n + jnp.where(mine, 1, 0)

        n = lax.fori_loop(0, lst[0, 2 * SLOTS], scan, n)

    def start(t, b):
        row, i = todo[1, t], todo[3, t]
        for k, buf in enumerate((own4, d1, d2, d3, d4, e0, e1, e2, e3, e4)):
            @pl.when(todo[0, t] == k)
            def _():
                pltpu.make_async_copy(buf.at[row], cbuf.at[b], sem_c.at[b]).start()
        at = pl.multiple_of(i * L, L)
        for k, buf in enumerate((r0, ra1, ra2, rb)):
            @pl.when(todo[2, t] == k)
            def _():
                pltpu.make_async_copy(buf.at[pl.ds(at, L), :], rbuf.at[b], sem_r.at[b]).start()
                pltpu.make_async_copy(
                    buf.at[pl.ds(4 * L, 16), pl.ds(0, L)], wbuf.at[b], sem_w.at[b]
                ).start()

    for t in range(SLOT_BUFS - 1):
        @pl.when(t < n)
        def _(t=t):
            start(t, t)

    lane = lax.broadcasted_iota(jnp.int32, (8, L), 1)
    sub = lax.broadcasted_iota(jnp.int32, (8, L), 0)
    eye = lax.broadcasted_iota(jnp.int32, (L, L), 0) == lax.broadcasted_iota(jnp.int32, (L, L), 1)

    def score(t, carry):
        acc, total = carry
        b = t % SLOT_BUFS

        @pl.when(t + SLOT_BUFS - 1 < n)
        def _():
            start(t + SLOT_BUFS - 1, (t + SLOT_BUFS - 1) % SLOT_BUFS)

        pltpu.make_async_copy(own4.at[0], cbuf.at[b], sem_c.at[b]).wait()
        pltpu.make_async_copy(r0.at[pl.ds(0, L), :], rbuf.at[b], sem_r.at[b]).wait()
        pltpu.make_async_copy(r0.at[pl.ds(4 * L, 16), pl.ds(0, L)], wbuf.at[b], sem_w.at[b]).wait()
        similar = lax.dot_general(
            cbuf[b, 0:L, :], rbuf[b], (((1,), (1,)), ((), ())), preferred_element_type=jnp.float32
        )
        cw = cbuf[b, L:, 0:L].astype(jnp.float32)[0:1, :]
        wide = wbuf[b].astype(jnp.float32)
        rsub = lax.broadcasted_iota(jnp.int32, (16, L), 0)
        rw = jnp.sum(jnp.where(rsub == todo[3, t], wide, 0.0), axis=0, keepdims=True)
        cw_col = jnp.sum(jnp.where(eye, cw, 0.0), axis=1, keepdims=True)
        row_best = jnp.max(jnp.where(rw > 0, similar, -10000.0), axis=1, keepdims=True)
        col_best = jnp.max(jnp.where(cw_col > 0, similar, -10000.0), axis=0, keepdims=True)
        precision = jnp.sum(cw_col * row_best, axis=0, keepdims=True) / jnp.sum(
            cw, axis=1, keepdims=True
        )
        recall = jnp.sum(rw * col_best, axis=1, keepdims=True) / jnp.sum(rw, axis=1, keepdims=True)
        fmeasure = 2.0 * precision * recall / jnp.maximum(precision + recall, 0.7)
        three = jnp.where(
            sub == 0, precision, jnp.where(sub == 1, recall, jnp.where(sub == 2, fmeasure, 0.0))
        )
        return jnp.where(lane == todo[4, t], three, acc), total + three

    zero = jnp.zeros((8, L), jnp.float32)
    acc, total = lax.fori_loop(0, n, score, (zero, zero))
    count = l0[0, 2 * SLOTS].astype(jnp.float32)
    sums = jnp.where(
        lane == 0, total[0:1, :], jnp.where(lane == 1, total[1:2, :], jnp.where(lane == 2, total[2:3, :], count))
    )
    sums = jnp.where((sub == 3) & (lane < 4), sums, 0.0)
    for q in range(out_ref.shape[0]):
        out_ref[q] = sums
    mine = (y * 2 + core) * 4 + x
    for q in range(4):
        out_ref[mine * 4 + q] = jnp.where(sub < 3, acc, sums)


def score_pairs(pos, lists, bufs):
    smem = pl.BlockSpec(memory_space=pltpu.SMEM)
    hbm = pl.BlockSpec(memory_space=pl.ANY)
    return pl.pallas_call(
        pair_kernel,
        in_specs=[smem] * 5 + [hbm] * len(bufs),
        out_specs=pl.BlockSpec(memory_space=pltpu.VMEM),
        out_shape=jax.ShapeDtypeStruct((128, 8, L), jnp.float32),
        scratch_shapes=[
            pltpu.VMEM((SLOT_BUFS, L + 16, D), jnp.bfloat16),
            pltpu.VMEM((SLOT_BUFS, L, D), jnp.bfloat16),
            pltpu.VMEM((SLOT_BUFS, 16, L), jnp.bfloat16),
            pltpu.SMEM((5, 4 * SLOTS), jnp.int32),
            pltpu.SemaphoreType.DMA((SLOT_BUFS,)),
            pltpu.SemaphoreType.DMA((SLOT_BUFS,)),
            pltpu.SemaphoreType.DMA((SLOT_BUFS,)),
        ],
        compiler_params=pltpu.CompilerParams(vmem_limit_bytes=60 << 20),
        name="score_pairs",
    )(pos, *lists, *bufs)


def on_device(
    cand_hidden, ref_hidden, cand_ids, ref_ids, cand_len, reference_length, idf_table, up_weight,
    up_bias, down_weight, down_bias, norm_gain, norm_bias, pair_cand, pair_ref, pair_count,
):
    table = jnp.pad(idf_table, (0, TABLE_ROWS * 128 - idf_table.shape[0]))
    table = table.reshape(TABLE_ROWS, 128).astype(jnp.bfloat16)
    cand, refs = encode(
        cand_hidden.reshape(1, L, D),
        ref_hidden.reshape(4, L, D),
        cand_ids.reshape(1, L),
        ref_ids.reshape(4, L),
        cand_len.reshape(1),
        reference_length.reshape(4),
        table,
        up_weight,
        up_bias.reshape(1, -1),
        down_weight,
        down_bias.reshape(1, -1),
        norm_gain.reshape(1, -1),
        norm_bias.reshape(1, -1),
    )
    ref_back = send(refs, along_x(1))
    ref_ahead = send(refs, along_x(-1))
    c1 = send(cand, along_first(1))
    c2 = send(cand, along_first(-1))
    c3 = send(c1, along_first(1))
    own4 = jnp.stack([cand, c1, c2, c3])
    d1 = send(own4, along_second(1))
    d2 = send(own4, along_second(-1))
    d3 = send(d1[:2], along_second(1))
    d4 = send(d2[2:], along_second(-1))
    others = [send(v, to_other_core) for v in (own4, d1, d2, d3, d4)]
    ref_far = send(ref_back, along_x(1))
    slots = jnp.concatenate(
        [
            pair_cand.reshape(-1),
            pair_ref.reshape(-1),
            jnp.broadcast_to(pair_count.reshape(1), (2 * SLOTS,)),
        ]
    ).reshape(1, 4 * SLOTS)
    lists = [slots] + [send(slots, along_z(k)) for k in (1, -1, 2)]
    dp, prompt = lax.axis_index("dp"), lax.axis_index("prompt")
    z = prompt & 3
    pos = jnp.stack([dp >> 1, dp & 1, prompt >> 2, z]).astype(jnp.int32)
    payload = score_pairs(
        pos, lists, [own4, d1, d2, d3, d4, *others, refs, ref_back, ref_ahead, ref_far]
    )
    got = jnp.sum(lax.all_to_all(payload, AXES, 0, 0), axis=0)
    scores = lax.dynamic_slice(got, (0, z * SLOTS), (3, SLOTS))
    return scores.reshape(3, 1, 1, SLOTS), got[3, :3] / got[3, 3]


def solution(mesh):
    placed = (
        P("prompt", "dp", None, None),
        P("dp", "prompt", None, None),
        P("prompt", "dp", None),
        P("dp", "prompt", None),
        P("prompt", "dp"),
        P("dp", "prompt"),
        P(),
        P(),
        P(),
        P(),
        P(),
        P(),
        P(),
        P("dp", "prompt", None),
        P("dp", "prompt", None),
        P("dp", "prompt"),
    )
    return jax.shard_map(
        on_device,
        mesh=mesh,
        in_specs=placed,
        out_specs=(P(None, "dp", "prompt", None), P()),
        check_vma=False,
    )
```

time: 264 us -> 129 us (0.49)
  blocking collectives: 97 us -> 0 us
  matrix products: 51 us -> 0 us
  starting transfers between devices: 0.26 us -> 42.1 us
  Pallas kernels: 0 us -> 31.4 us
  local copies, waits for them, and re-layouts: 26.7 us -> 2 us
  waiting for transfers between devices: 62.4 us -> 46 us
  between operations: 15.6 us -> 2.12 us
  other arithmetic: 10.3 us -> 4.09 us
    psum x1 -> x0, blocking collectives: 64.7 us -> none  [on_device(): lax.psum((jnp.sum(stacked, axis=1), jnp.sum(live_slots.astype(jnp.float32...]
    all_gather x2 -> x0, waiting for transfers between devices: 62.4 us -> none  [the longest x1 62.4 us: on_device(): lax.all_gather(ref_unit, 'prompt', axis=1, tiled=True)]
    dot_general x3 -> x0, matrix products: 51 us -> none  [the longest x2 43.5 us: encode_rows(): jnp.dot(activated, down_weight, preferred_element_type=jnp.float32)]
    ppermute x0 -> x18, starting transfers between devices: none -> 34.8 us  [send(): lax.ppermute(value, AXES, [(number(*a), number(*where(*a))) for a in GRID])]
    ppermute x0 -> x18, waiting for transfers between devices: none -> 32.6 us  [send(): lax.ppermute(value, AXES, [(number(*a), number(*where(*a))) for a in GRID])]
    all_gather x2 -> x0, blocking collectives: 32.4 us -> none  [the longest x1 20.3 us: on_device(): lax.all_gather(ref_weight, 'prompt', axis=1, tiled=True)]
    pallas_call x0 -> x2, Pallas kernels: none -> 31.4 us  [the longest x1 18.5 us: encode(): pl.pallas_call(functools.partial(encode_kernel, sub), grid=(up.shape[1] /...]
    gather x11 -> x0, local copies, waits for them, and re-layouts: 26.6 us -> none  [the longest x1 10.8 us: on_device(): jnp.take(ref_all.reshape(-1, seq_len, width), within, axis=0)]
  transfers between devices with their start and end apart: 2 -> 19, of which waited for: 1 -> 7; matrix products, arithmetic and copies ran while one was open for 20% -> 1% of each run, Pallas kernels for 0% -> 0%
where the time goes in v1:
time: 129 us; the launch traced here: 128 us
  waiting for transfers between devices  46 us (36%)
  starting transfers between devices  42.1 us (33%)
  Pallas kernels  31.4 us (24%)
  other arithmetic  4.09 us (3%)
  between operations  2.12 us (2%)
  local copies, waits for them, and re-layouts  2 us (2%)
    ppermute x18, starting transfers between devices, send(): lax.ppermute(value, AXES, [(number(*a), number(*where(*a))) for a in GRID])  34.8 us
    ppermute x18, waiting for transfers between devices, send(): lax.ppermute(value, AXES, [(number(*a), number(*where(*a))) for a in GRID])  32.6 us
    pallas_call x1, Pallas kernels, encode(): pl.pallas_call(functools.partial(encode_kernel, sub), grid=(up.shape[1] /...  18.5 us
    all_to_all x1, waiting for transfers between devices, on_device(): got = jnp.sum(lax.all_to_all(payload, AXES, 0, 0), axis=0)  13.4 us
    pallas_call x1, Pallas kernels, score_pairs(): pl.pallas_call(pair_kernel, in_specs=[smem] * 5 + [hbm] * len(bufs), out_...  12.9 us
    all_to_all x1, starting transfers between devices, on_device(): got = jnp.sum(lax.all_to_all(payload, AXES, 0, 0), axis=0)  7.35 us
  transfers between devices with their start and end apart: 19, of which 7 were waited for; matrix products, arithmetic and copies ran while one was open for 1% of the time, Pallas kernels for 0%

profile of v1, /device:TPU:1, one launch (start us, length us, event | category | flops | bytes accessed | tf_op | source)
XLA Modules:
  0.0 127.7 jit_solution(4558184483832553042)
XLA Ops:
  1.3 0.9 convert.4
  2.2 0.7 pad_bitcast_fusion.tbl_ref
  2.9 18.5 %encode.1 = (bf16[144,1024]{1,0:T(8,128)(2,1)}, bf16[528,1024]{1,0:T(8,128)(2,1)}) custom-call(s32[1]{0:T(128)} %bitcast.30.clen_ref, s32[4]{0:T(128)} %bitcast.43, s32[1,128]{1,0:T(1,128)} %bitcast.44, s32[4,128]{1,0:T(4,128)} %bitcast.42, bf16[400,128]{1,0:T(8,128)(2,1)} %pad_bitcast_fusion.tbl_ref, bf16[1,128,1024]{2,1,0:T(8,128)(2,1)} %bitcast.37, ...), custom_call_target="tpu_custom_call" | custom-call | tf_op jit(solution)/shard_map/encode/pallas_call | solution.py:126
  21.3 2.5 %collective-permute-start.3 = (bf16[144,1024]{1,0:T(8,128)(2,1)}, bf16[144,1024]{1,0:T(8,128)(2,1)S(1)}, u32[]{:S(2)}, u32[]{:S(2)}) collective-permute-start(bf16[144,1024]{1,0:T(8,128)(2,1)} %get-tuple-element.4), channel_id=1, source_target_pairs={{0,32},{1,33},{2,34},{3,35},{4,36},{5,37},{6,38},{7,39},{8,40},{9,... | collective-permute-start | bytes 884744 | tf_op jit(solution)/shard_map/ppermute | solution.py:23
  23.8 2.2 %collective-permute-start.4 = (bf16[144,1024]{1,0:T(8,128)(2,1)}, bf16[144,1024]{1,0:T(8,128)(2,1)S(1)}, u32[]{:S(2)}, u32[]{:S(2)}) collective-permute-start(bf16[144,1024]{1,0:T(8,128)(2,1)} %get-tuple-element.4), channel_id=1, source_target_pairs={{0,96},{1,97},{2,98},{3,99},{4,100},{5,101},{6,102},{7,103},{8,104... | collective-permute-start | bytes 884744 | tf_op jit(solution)/shard_map/ppermute | solution.py:23
  26.0 4.5 %collective-permute-done.3 = bf16[144,1024]{1,0:T(8,128)(2,1)S(1)} collective-permute-done((bf16[144,1024]{1,0:T(8,128)(2,1)}, bf16[144,1024]{1,0:T(8,128)(2,1)S(1)}, u32[]{:S(2)}, u32[]{:S(2)}) %collective-permute-start.3) | collective-permute-done | bytes 294944 | tf_op jit(solution)/shard_map/ppermute | solution.py:23
  30.5 0.0 collective-permute-start.5
  31.2 0.0 collective-permute-done.4
  31.2 6.4 %collective-permute-done.5 = bf16[144,1024]{1,0:T(8,128)(2,1)S(1)} collective-permute-done((bf16[144,1024]{1,0:T(8,128)(2,1)S(1)}, bf16[144,1024]{1,0:T(8,128)(2,1)S(1)}, u32[]{:S(2)}, u32[]{:S(2)}) %collective-permute-start.5) | collective-permute-done | bytes 294944 | tf_op jit(solution)/shard_map/ppermute | solution.py:23
  37.6 1.2 pad_maximum_fusion.own4
  38.8 0.0 copy-start
  38.8 2.5 %collective-permute-start.7 = (bf16[4,144,1024]{2,1,0:T(8,128)(2,1)S(1)}, bf16[4,144,1024]{2,1,0:T(8,128)(2,1)S(1)}, u32[]{:S(2)}, u32[]{:S(2)}) collective-permute-start(bf16[4,144,1024]{2,1,0:T(8,128)(2,1)S(1)} %pad_maximum_fusion.own4), channel_id=1, source_target_pairs={{0,3},{1,0},{2,1},{3,2},{4,7},{5,4},{6,5},{7,6},{8,11},{9,8},{10,9... | collective-permute-start | bytes 3538952 | tf_op jit(solution)/shard_map/ppermute | solution.py:23
  41.3 0.0 collective-permute-start.6
  41.3 0.0 copy-done.10
  41.3 0.0 copy-done.11
  41.4 0.1 add_bitcast_fusion.l0
  41.4 0.4 collective-permute-start.2
  41.8 4.4 %collective-permute-start.10 = (bf16[4,144,1024]{2,1,0:T(8,128)(2,1)S(1)}, bf16[4,144,1024]{2,1,0:T(8,128)(2,1)S(1)}, u32[]{:S(2)}, u32[]{:S(2)}) collective-permute-start(bf16[4,144,1024]{2,1,0:T(8,128)(2,1)S(1)} %pad_maximum_fusion.own4), channel_id=1, source_target_pairs={{0,16},{1,17},{2,18},{3,19},{4,20},{5,21},{6,22},{7,23},{8,24},{9,... | collective-permute-start | bytes 3538952 | tf_op jit(solution)/shard_map/ppermute | solution.py:23
  46.2 0.0 copy-done.4
  46.2 1.2 collective-permute-start.16
  47.4 0.0 collective-permute-done.2.l3
  47.4 1.5 %collective-permute-start.15 = (bf16[528,1024]{1,0:T(8,128)(2,1)S(1)}, bf16[528,1024]{1,0:T(8,128)(2,1)}, u32[]{:S(2)}, u32[]{:S(2)}) collective-permute-start(bf16[528,1024]{1,0:T(8,128)(2,1)S(1)} %copy-done.4), channel_id=1, source_target_pairs={{0,4},{1,5},{2,6},{3,7},{4,8},{5,9},{6,10},{7,11},{8,12},{9,13},{1... | collective-permute-start | bytes 3244040 | tf_op jit(solution)/shard_map/ppermute | solution.py:23
  48.9 5.6 %collective-permute-done.7.d2 = bf16[4,144,1024]{2,1,0:T(8,128)(2,1)S(1)} collective-permute-done((bf16[4,144,1024]{2,1,0:T(8,128)(2,1)S(1)}, bf16[4,144,1024]{2,1,0:T(8,128)(2,1)S(1)}, u32[]{:S(2)}, u32[]{:S(2)}) %collective-permute-start.7) | collective-permute-done | bytes 1179680 | tf_op jit(solution)/shard_map/ppermute | solution.py:23
  54.5 0.5 collective-permute-start.1
  55.0 2.9 %collective-permute-done.6.d1 = bf16[4,144,1024]{2,1,0:T(8,128)(2,1)S(1)} collective-permute-done((bf16[4,144,1024]{2,1,0:T(8,128)(2,1)S(1)}, bf16[4,144,1024]{2,1,0:T(8,128)(2,1)S(1)}, u32[]{:S(2)}, u32[]{:S(2)}) %collective-permute-start.6) | collective-permute-done | bytes 1179680 | tf_op jit(solution)/shard_map/ppermute | solution.py:23
  57.9 0.0 collective-permute-start
  58.0 0.0 copy-done
  58.0 0.0 copy-done.6
  58.0 0.0 copy-done.7
  58.0 0.0 collective-permute-done.1.l2
  58.0 0.0 copy-start.8
  58.0 2.5 %collective-permute-start.9 = (bf16[2,144,1024]{2,1,0:T(8,128)(2,1)S(1)}, bf16[2,144,1024]{2,1,0:T(8,128)(2,1)}, u32[]{:S(2)}, u32[]{:S(2)}) collective-permute-start(bf16[2,144,1024]{2,1,0:T(8,128)(2,1)S(1)} %slice.17), channel_id=1, source_target_pairs={{0,3},{1,0},{2,1},{3,2},{4,7},{5,4},{6,5},{7,6},{8,11},{9,8},{10,9... | collective-permute-start | bytes 1769480 | tf_op jit(solution)/shard_map/ppermute | solution.py:23
  60.6 0.9 collective-permute-done.l1
  61.5 0.0 collective-permute-start.8
  61.5 0.0 collective-permute-done.16.ra2
  61.5 0.0 copy-done.1
  61.5 0.0 copy-start.5
  61.5 11.4 %collective-permute-start.12 = (bf16[4,144,1024]{2,1,0:T(8,128)(2,1)S(1)}, bf16[4,144,1024]{2,1,0:T(8,128)(2,1)}, u32[]{:S(2)}, u32[]{:S(2)}) collective-permute-start(bf16[4,144,1024]{2,1,0:T(8,128)(2,1)S(1)} %collective-permute-done.7.d2), channel_id=1, source_target_pairs={{0,16},{1,17},{2,18},{3,19},{4,20},{5,21},{6,22},{7,23},{8,24},{9,... | collective-permute-start | bytes 3538952 | tf_op jit(solution)/shard_map/ppermute | solution.py:23
  73.0 0.0 collective-permute-done.15.ra1
  73.0 3.7 %collective-permute-start.11 = (bf16[4,144,1024]{2,1,0:T(8,128)(2,1)S(1)}, bf16[4,144,1024]{2,1,0:T(8,128)(2,1)}, u32[]{:S(2)}, u32[]{:S(2)}) collective-permute-start(bf16[4,144,1024]{2,1,0:T(8,128)(2,1)S(1)} %collective-permute-done.6.d1), channel_id=1, source_target_pairs={{0,16},{1,17},{2,18},{3,19},{4,20},{5,21},{6,22},{7,23},{8,24},{9,... | collective-permute-start | bytes 3538952 | tf_op jit(solution)/shard_map/ppermute | solution.py:23
  76.7 0.0 collective-permute-done.10.e0
  76.7 0.0 copy-done.5
  76.7 1.3 %collective-permute-start.17 = (bf16[528,1024]{1,0:T(8,128)(2,1)}, bf16[528,1024]{1,0:T(8,128)(2,1)}, u32[]{:S(2)}, u32[]{:S(2)}) collective-permute-start(bf16[528,1024]{1,0:T(8,128)(2,1)} %collective-permute-done.15.ra1), channel_id=1, source_target_pairs={{0,4},{1,5},{2,6},{3,7},{4,8},{5,9},{6,10},{7,11},{8,12},{9,13},{1... | collective-permute-start | bytes 3244040 | tf_op jit(solution)/shard_map/ppermute | solution.py:23
  78.1 0.0 collective-permute-done.9.d4
  78.1 0.0 collective-permute-start.14
  78.1 0.0 collective-permute-done.8.d3
  78.1 0.5 collective-permute-start.13
  78.6 0.6 pad_add_fusion.pos_ref
  79.2 12.2 %collective-permute-done.17.rb = bf16[528,1024]{1,0:T(8,128)(2,1)} collective-permute-done((bf16[528,1024]{1,0:T(8,128)(2,1)}, bf16[528,1024]{1,0:T(8,128)(2,1)}, u32[]{:S(2)}, u32[]{:S(2)}) %collective-permute-start.17) | collective-permute-done | bytes 1081376 | tf_op jit(solution)/shard_map/ppermute | solution.py:23
  91.4 0.0 collective-permute-done.14.e4
  91.4 0.0 collective-permute-done.12.e2
  91.4 0.0 collective-permute-done.13.e3
  91.4 0.0 collective-permute-done.11.e1
  91.4 0.0 copy-done.2
  91.4 0.0 copy-done.8
  91.5 0.0 copy-done.9
  91.5 12.9 %score_pairs.1 = f32[128,8,128]{2,1,0:T(8,128)} custom-call(s32[4]{0:T(128)} %pad_add_fusion.pos_ref, s32[1,128]{1,0:T(1,128)} %copy-done.6, s32[1,128]{1,0:T(1,128)} %copy-done.9, s32[1,128]{1,0:T(1,128)} %copy-done.8, s32[1,128]{1,0:T(1,128)} %copy-done.7, bf16[4,144,1024]{2,1,0:T(8,128)(2,1)} %copy-done, bf16[4,144,1024]{2,1,0:T(8,128)(2,1)} %copy-done.2, ...), custom_call_target="tpu_custom_call" | custom-call | tf_op jit(solution)/shard_map/score_pairs/pallas_call | solution.py:262
  104.4 7.3 %all-to-all-start = ((f32[128,8,128]{2,1,0:T(8,128)}), f32[128,8,128]{2,1,0:T(8,128)S(1)}, u32[]{:S(2)}, u32[]{:S(2)}) async-start(f32[128,8,128]{2,1,0:T(8,128)} %score_pairs.1), calls=%async_computation | async-start | bytes 1048576 | tf_op jit(solution)/shard_map/all_to_all | solution.py:328
  111.8 13.4 %all-to-all-done = f32[128,8,128]{2,1,0:T(8,128)S(1)} async-done(((f32[128,8,128]{2,1,0:T(8,128)}), f32[128,8,128]{2,1,0:T(8,128)S(1)}, u32[]{:S(2)}, u32[]{:S(2)}) %all-to-all-start) | async-done | bytes 524320 | tf_op jit(solution)/shard_map/all_to_all | solution.py:328
  125.2 0.1 reduce_sum.9
  125.3 0.6 slice.15
  125.9 1.2 divide_bitcast_fusion
  127.1 0.1 dynamic-slice_bitcast_fusion
  127.1 0.6 copy.18
  (13 shorter events, 0.1 us)
Async XLA Ops:
  21.3 9.2 %collective-permute-start.3 = (bf16[144,1024]{1,0:T(8,128)(2,1)}, bf16[144,1024]{1,0:T(8,128)(2,1)S(1)}, u32[]{:S(2)}, u32[]{:S(2)}) collective-permute-start(bf16[144,1024]{1,0:T(8,128)(2,1)} %get-tuple-element.4), channel_id=1, source_target_pairs={{0,32},{1,33},{2,34},{3,35},{4,36},{5,37},{6,38},{7,39},{8,40},{9,... | collective-permute-start | bytes 884744 | tf_op jit(solution)/shard_map/ppermute | solution.py:23
  23.8 7.4 %collective-permute-start.4 = (bf16[144,1024]{1,0:T(8,128)(2,1)}, bf16[144,1024]{1,0:T(8,128)(2,1)S(1)}, u32[]{:S(2)}, u32[]{:S(2)}) collective-permute-start(bf16[144,1024]{1,0:T(8,128)(2,1)} %get-tuple-element.4), channel_id=1, source_target_pairs={{0,96},{1,97},{2,98},{3,99},{4,100},{5,101},{6,102},{7,103},{8,104... | collective-permute-start | bytes 884744 | tf_op jit(solution)/shard_map/ppermute | solution.py:23
  30.5 7.1 %collective-permute-start.5 = (bf16[144,1024]{1,0:T(8,128)(2,1)S(1)}, bf16[144,1024]{1,0:T(8,128)(2,1)S(1)}, u32[]{:S(2)}, u32[]{:S(2)}) collective-permute-start(bf16[144,1024]{1,0:T(8,128)(2,1)S(1)} %collective-permute-done.3), channel_id=1, source_target_pairs={{0,32},{1,33},{2,34},{3,35},{4,36},{5,37},{6,38},{7,39},{8,40},{9,... | collective-permute-start | bytes 884744 | tf_op jit(solution)/shard_map/ppermute | solution.py:23
  37.6 3.8 %copy-start.10 = (s32[1,1,32]{2,1,0:T(1,128)S(1)}, s32[1,1,32]{2,1,0:T(1,128)}, u32[]{:S(2)}) copy-start(s32[1,1,32]{2,1,0:T(1,128)} %param.30) | copy-start | bytes 388
  37.6 3.8 %copy-start.11 = (s32[1,1,32]{2,1,0:T(1,128)S(1)}, s32[1,1,32]{2,1,0:T(1,128)}, u32[]{:S(2)}) copy-start(s32[1,1,32]{2,1,0:T(1,128)} %param.29) | copy-start | bytes 388
  37.6 8.6 %copy-start.4 = (bf16[528,1024]{1,0:T(8,128)(2,1)S(1)}, bf16[528,1024]{1,0:T(8,128)(2,1)}, u32[]{:S(2)}) copy-start(bf16[528,1024]{1,0:T(8,128)(2,1)} %get-tuple-element.5.r0) | copy-start | bytes 3244036
  38.8 19.2 %copy-start = (bf16[4,144,1024]{2,1,0:T(8,128)(2,1)}, bf16[4,144,1024]{2,1,0:T(8,128)(2,1)S(1)}, u32[]{:S(2)}) copy-start(bf16[4,144,1024]{2,1,0:T(8,128)(2,1)S(1)} %pad_maximum_fusion.own4) | copy-start | bytes 3538948
  38.8 15.7 %collective-permute-start.7 = (bf16[4,144,1024]{2,1,0:T(8,128)(2,1)S(1)}, bf16[4,144,1024]{2,1,0:T(8,128)(2,1)S(1)}, u32[]{:S(2)}, u32[]{:S(2)}) collective-permute-start(bf16[4,144,1024]{2,1,0:T(8,128)(2,1)S(1)} %pad_maximum_fusion.own4), channel_id=1, source_target_pairs={{0,3},{1,0},{2,1},{3,2},{4,7},{5,4},{6,5},{7,6},{8,11},{9,8},{10,9... | collective-permute-start | bytes 3538952 | tf_op jit(solution)/shard_map/ppermute | solution.py:23
  41.3 16.6 %collective-permute-start.6 = (bf16[4,144,1024]{2,1,0:T(8,128)(2,1)S(1)}, bf16[4,144,1024]{2,1,0:T(8,128)(2,1)S(1)}, u32[]{:S(2)}, u32[]{:S(2)}) collective-permute-start(bf16[4,144,1024]{2,1,0:T(8,128)(2,1)S(1)} %pad_maximum_fusion.own4), channel_id=1, source_target_pairs={{0,1},{1,2},{2,3},{3,0},{4,5},{5,6},{6,7},{7,4},{8,9},{9,10},{10,1... | collective-permute-start | bytes 3538952 | tf_op jit(solution)/shard_map/ppermute | solution.py:23
  41.4 16.6 %copy-start.6 = (s32[1,128]{1,0:T(1,128)}, s32[1,128]{1,0:T(1,128)S(1)}, u32[]{:S(2)}) copy-start(s32[1,128]{1,0:T(1,128)S(1)} %add_bitcast_fusion.l0) | copy-start | bytes 1540
  41.4 6.0 %collective-permute-start.2 = (s32[1,128]{1,0:T(1,128)S(1)}, s32[1,128]{1,0:T(1,128)S(1)}, u32[]{:S(2)}, u32[]{:S(2)}) collective-permute-start(s32[1,128]{1,0:T(1,128)S(1)} %add_bitcast_fusion.l0), channel_id=1, source_target_pairs={{0,2},{1,3},{2,0},{3,1},{4,6},{5,7},{6,4},{7,5},{8,10},{9,11},{10,... | collective-permute-start | bytes 1544 | tf_op jit(solution)/shard_map/ppermute | solution.py:23
  41.8 34.9 %collective-permute-start.10 = (bf16[4,144,1024]{2,1,0:T(8,128)(2,1)S(1)}, bf16[4,144,1024]{2,1,0:T(8,128)(2,1)S(1)}, u32[]{:S(2)}, u32[]{:S(2)}) collective-permute-start(bf16[4,144,1024]{2,1,0:T(8,128)(2,1)S(1)} %pad_maximum_fusion.own4), channel_id=1, source_target_pairs={{0,16},{1,17},{2,18},{3,19},{4,20},{5,21},{6,22},{7,23},{8,24},{9,... | collective-permute-start | bytes 3538952 | tf_op jit(solution)/shard_map/ppermute | solution.py:23
  46.2 15.3 %collective-permute-start.16 = (bf16[528,1024]{1,0:T(8,128)(2,1)S(1)}, bf16[528,1024]{1,0:T(8,128)(2,1)S(1)}, u32[]{:S(2)}, u32[]{:S(2)}) collective-permute-start(bf16[528,1024]{1,0:T(8,128)(2,1)S(1)} %copy-done.4), channel_id=1, source_target_pairs={{0,12},{1,13},{2,14},{3,15},{4,0},{5,1},{6,2},{7,3},{8,4},{9,5},{1... | collective-permute-start | bytes 3244040 | tf_op jit(solution)/shard_map/ppermute | solution.py:23
  47.4 10.6 %copy-start.7 = (s32[1,128]{1,0:T(1,128)}, s32[1,128]{1,0:T(1,128)S(1)}, u32[]{:S(2)}) copy-start(s32[1,128]{1,0:T(1,128)S(1)} %collective-permute-done.2.l3) | copy-start | bytes 1540
  47.4 25.5 %collective-permute-start.15 = (bf16[528,1024]{1,0:T(8,128)(2,1)S(1)}, bf16[528,1024]{1,0:T(8,128)(2,1)}, u32[]{:S(2)}, u32[]{:S(2)}) collective-permute-start(bf16[528,1024]{1,0:T(8,128)(2,1)S(1)} %copy-done.4), channel_id=1, source_target_pairs={{0,4},{1,5},{2,6},{3,7},{4,8},{5,9},{6,10},{7,11},{8,12},{9,13},{1... | collective-permute-start | bytes 3244040 | tf_op jit(solution)/shard_map/ppermute | solution.py:23
  54.5 7.0 %copy-start.1 = (bf16[4,144,1024]{2,1,0:T(8,128)(2,1)}, bf16[4,144,1024]{2,1,0:T(8,128)(2,1)S(1)}, u32[]{:S(2)}) copy-start(bf16[4,144,1024]{2,1,0:T(8,128)(2,1)S(1)} %collective-permute-done.7.d2) | copy-start | bytes 3538948
  54.5 3.5 %collective-permute-start.1 = (s32[1,128]{1,0:T(1,128)S(1)}, s32[1,128]{1,0:T(1,128)S(1)}, u32[]{:S(2)}, u32[]{:S(2)}) collective-permute-start(s32[1,128]{1,0:T(1,128)S(1)} %add_bitcast_fusion.l0), channel_id=1, source_target_pairs={{0,3},{1,0},{2,1},{3,2},{4,7},{5,4},{6,5},{7,6},{8,11},{9,8},{10,9... | collective-permute-start | bytes 1544 | tf_op jit(solution)/shard_map/ppermute | solution.py:23
  57.9 33.5 %copy-start.2 = (bf16[4,144,1024]{2,1,0:T(8,128)(2,1)}, bf16[4,144,1024]{2,1,0:T(8,128)(2,1)S(1)}, u32[]{:S(2)}) copy-start(bf16[4,144,1024]{2,1,0:T(8,128)(2,1)S(1)} %collective-permute-done.6.d1) | copy-start | bytes 3538948
  57.9 3.6 %collective-permute-start = (s32[1,128]{1,0:T(1,128)S(1)}, s32[1,128]{1,0:T(1,128)S(1)}, u32[]{:S(2)}, u32[]{:S(2)}) collective-permute-start(s32[1,128]{1,0:T(1,128)S(1)} %add_bitcast_fusion.l0), channel_id=1, source_target_pairs={{0,1},{1,2},{2,3},{3,0},{4,5},{5,6},{6,7},{7,4},{8,9},{9,10},{10,1... | collective-permute-start | bytes 1544 | tf_op jit(solution)/shard_map/ppermute | solution.py:23
  58.0 33.4 %copy-start.8 = (s32[1,128]{1,0:T(1,128)}, s32[1,128]{1,0:T(1,128)S(1)}, u32[]{:S(2)}) copy-start(s32[1,128]{1,0:T(1,128)S(1)} %collective-permute-done.1.l2) | copy-start | bytes 1540
  58.0 20.0 %collective-permute-start.9 = (bf16[2,144,1024]{2,1,0:T(8,128)(2,1)S(1)}, bf16[2,144,1024]{2,1,0:T(8,128)(2,1)}, u32[]{:S(2)}, u32[]{:S(2)}) collective-permute-start(bf16[2,144,1024]{2,1,0:T(8,128)(2,1)S(1)} %slice.17), channel_id=1, source_target_pairs={{0,3},{1,0},{2,1},{3,2},{4,7},{5,4},{6,5},{7,6},{8,11},{9,8},{10,9... | collective-permute-start | bytes 1769480 | tf_op jit(solution)/shard_map/ppermute | solution.py:23
  61.5 30.0 %copy-start.9 = (s32[1,128]{1,0:T(1,128)}, s32[1,128]{1,0:T(1,128)S(1)}, u32[]{:S(2)}) copy-start(s32[1,128]{1,0:T(1,128)S(1)} %collective-permute-done.l1) | copy-start | bytes 1540
  61.5 16.6 %collective-permute-start.8 = (bf16[2,144,1024]{2,1,0:T(8,128)(2,1)S(1)}, bf16[2,144,1024]{2,1,0:T(8,128)(2,1)}, u32[]{:S(2)}, u32[]{:S(2)}) collective-permute-start(bf16[2,144,1024]{2,1,0:T(8,128)(2,1)S(1)} %slice.16), channel_id=1, source_target_pairs={{0,1},{1,2},{2,3},{3,0},{4,5},{5,6},{6,7},{7,4},{8,9},{9,10},{10,1... | collective-permute-start | bytes 1769480 | tf_op jit(solution)/shard_map/ppermute | solution.py:23
  61.5 15.2 %copy-start.5 = (bf16[528,1024]{1,0:T(8,128)(2,1)}, bf16[528,1024]{1,0:T(8,128)(2,1)S(1)}, u32[]{:S(2)}) copy-start(bf16[528,1024]{1,0:T(8,128)(2,1)S(1)} %collective-permute-done.16.ra2) | copy-start | bytes 3244036
  61.5 29.9 %collective-permute-start.12 = (bf16[4,144,1024]{2,1,0:T(8,128)(2,1)S(1)}, bf16[4,144,1024]{2,1,0:T(8,128)(2,1)}, u32[]{:S(2)}, u32[]{:S(2)}) collective-permute-start(bf16[4,144,1024]{2,1,0:T(8,128)(2,1)S(1)} %collective-permute-done.7.d2), channel_id=1, source_target_pairs={{0,16},{1,17},{2,18},{3,19},{4,20},{5,21},{6,22},{7,23},{8,24},{9,... | collective-permute-start | bytes 3538952 | tf_op jit(solution)/shard_map/ppermute | solution.py:23
  73.0 18.4 %collective-permute-start.11 = (bf16[4,144,1024]{2,1,0:T(8,128)(2,1)S(1)}, bf16[4,144,1024]{2,1,0:T(8,128)(2,1)}, u32[]{:S(2)}, u32[]{:S(2)}) collective-permute-start(bf16[4,144,1024]{2,1,0:T(8,128)(2,1)S(1)} %collective-permute-done.6.d1), channel_id=1, source_target_pairs={{0,16},{1,17},{2,18},{3,19},{4,20},{5,21},{6,22},{7,23},{8,24},{9,... | collective-permute-start | bytes 3538952 | tf_op jit(solution)/shard_map/ppermute | solution.py:23
  76.7 14.7 %copy-start.3 = (bf16[4,144,1024]{2,1,0:T(8,128)(2,1)}, bf16[4,144,1024]{2,1,0:T(8,128)(2,1)S(1)}, u32[]{:S(2)}) copy-start(bf16[4,144,1024]{2,1,0:T(8,128)(2,1)S(1)} %collective-permute-done.10.e0) | copy-start | bytes 3538948
  76.7 14.7 %collective-permute-start.17 = (bf16[528,1024]{1,0:T(8,128)(2,1)}, bf16[528,1024]{1,0:T(8,128)(2,1)}, u32[]{:S(2)}, u32[]{:S(2)}) collective-permute-start(bf16[528,1024]{1,0:T(8,128)(2,1)} %collective-permute-done.15.ra1), channel_id=1, source_target_pairs={{0,4},{1,5},{2,6},{3,7},{4,8},{5,9},{6,10},{7,11},{8,12},{9,13},{1... | collective-permute-start | bytes 3244040 | tf_op jit(solution)/shard_map/ppermute | solution.py:23
  78.1 13.3 %collective-permute-start.14 = (bf16[2,144,1024]{2,1,0:T(8,128)(2,1)}, bf16[2,144,1024]{2,1,0:T(8,128)(2,1)}, u32[]{:S(2)}, u32[]{:S(2)}) collective-permute-start(bf16[2,144,1024]{2,1,0:T(8,128)(2,1)} %collective-permute-done.9.d4), channel_id=1, source_target_pairs={{0,16},{1,17},{2,18},{3,19},{4,20},{5,21},{6,22},{7,23},{8,24},{9,... | collective-permute-start | bytes 1769480 | tf_op jit(solution)/shard_map/ppermute | solution.py:23
  78.1 13.3 %collective-permute-start.13 = (bf16[2,144,1024]{2,1,0:T(8,128)(2,1)}, bf16[2,144,1024]{2,1,0:T(8,128)(2,1)}, u32[]{:S(2)}, u32[]{:S(2)}) collective-permute-start(bf16[2,144,1024]{2,1,0:T(8,128)(2,1)} %collective-permute-done.8.d3), channel_id=1, source_target_pairs={{0,16},{1,17},{2,18},{3,19},{4,20},{5,21},{6,22},{7,23},{8,24},{9,... | collective-permute-start | bytes 1769480 | tf_op jit(solution)/shard_map/ppermute | solution.py:23
  104.4 20.8 %all-to-all-start = ((f32[128,8,128]{2,1,0:T(8,128)}), f32[128,8,128]{2,1,0:T(8,128)S(1)}, u32[]{:S(2)}, u32[]{:S(2)}) async-start(f32[128,8,128]{2,1,0:T(8,128)} %score_pairs.1), calls=%async_computation | async-start | bytes 1048576 | tf_op jit(solution)/shard_map/all_to_all | solution.py:328

commit v2 on v1

v2 whole, which is shorter than its diff:
```python
import functools

import jax
import jax.numpy as jnp
from jax import lax
from jax.experimental import pallas as pl
from jax.experimental.pallas import tpu as pltpu
from jax.sharding import PartitionSpec as P

D = 1024
L = 128
SLOTS = 32
TABLE_ROWS = 400
AXES = ("dp", "prompt")
GRID = [(y, c, x, z) for y in range(4) for c in range(2) for x in range(4) for z in range(4)]


def number(y, c, x, z):
    return (((y % 4) * 2 + c) * 4 + x % 4) * 4 + z % 4


def send(value, where):
    return lax.ppermute(value, AXES, [(number(*a), number(*where(*a))) for a in GRID])


def along_x(step):
    return lambda y, c, x, z: (y, c, x + (step if c == 0 else -step), z)


def along_first(step):
    return lambda y, c, x, z: (y + step, c, x, z) if c == 0 else (y, c, x, z + step)


def along_second(step):
    return lambda y, c, x, z: (y, c, x, z + step) if c == 0 else (y + step, c, x, z)


def along_z(step):
    return lambda y, c, x, z: (y, c, x, z + step)


def to_other_core(y, c, x, z):
    return (y, 1 - c, x, z)


def encode_kernel(n_cand, picks, weights, sub, *refs):
    refs = list(refs)
    if weights:
        clen_ref, rlen_ref, cid_ref, rid_ref, tbl_ref = refs[:5]
        refs = refs[5:]
    ch_ref = refs.pop(0) if n_cand else None
    rh_ref, up, upb, dn, dnb, gain, bias = refs[:7]
    refs = refs[7:]
    co_ref = refs.pop(0) if n_cand else None
    ro_ref, x_ref, acc_ref = refs
    step = pl.program_id(0)
    seqs = n_cand + len(picks)

    def token_weights(ids, length):
        high, low = ids >> 7, ids & 127
        hot = (lax.broadcasted_iota(jnp.int32, (TABLE_ROWS, L), 0) == high).astype(jnp.bfloat16)
        rows = lax.dot_general(
            tbl_ref[...], hot, (((0,), (0,)), ((), ())), preferred_element_type=jnp.float32
        )
        mine = lax.broadcasted_iota(jnp.int32, (128, L), 0) == low
        value = jnp.sum(jnp.where(mine, rows, 0.0), axis=0, keepdims=True)
        live = lax.broadcasted_iota(jnp.int32, (1, L), 1) < length
        return jnp.where(live, value, 0.0)

    @pl.when(step == 0)
    def _():
        if n_cand:
            x_ref[0:L, :] = ch_ref[0]
        for k, q in enumerate(picks):
            x_ref[L * (n_cand + k) : L * (n_cand + k + 1), :] = rh_ref[q]
        if weights:
            row = lax.broadcasted_iota(jnp.int32, (16, L), 0)
            co_ref[L:, :] = jnp.zeros((16, D), jnp.bfloat16)
            ro_ref[len(picks) * L :, :] = jnp.zeros((16, D), jnp.bfloat16)
            w = token_weights(cid_ref[...], clen_ref[0])
            co_ref[L:, 0:L] = jnp.where(row == 0, w, 0.0).astype(jnp.bfloat16)
            block = jnp.zeros((16, L), jnp.float32)
            for q in range(4):
                block = jnp.where(row == q, token_weights(rid_ref[q : q + 1, :], rlen_ref[q]), block)
            ro_ref[len(picks) * L :, 0:L] = block.astype(jnp.bfloat16)

    w = up.shape[1] // sub
    x = x_ref[...]
    pre = [
        jnp.dot(x, up[:, k * w : (k + 1) * w], preferred_element_type=jnp.float32)
        + upb[:, k * w : (k + 1) * w]
        for k in range(sub)
    ]
    part = None
    for k in range(sub):
        h = pre[k]
        act = (0.5 * h * (lax.erf(h * 0.7071067811865476) + 1.0)).astype(jnp.bfloat16)
        d = jnp.dot(act, dn[k * w : (k + 1) * w, :], preferred_element_type=jnp.float32)
        part = d if part is None else part + d

    @pl.when(step == 0)
    def _():
        acc_ref[...] = part

    @pl.when(step > 0)
    def _():
        acc_ref[...] += part

    @pl.when(step == pl.num_programs(0) - 1)
    def _():
        for c in range(0, seqs * L, 64):
            r = slice(c, c + 64)
            s = x_ref[r, :].astype(jnp.float32) + acc_ref[r, :] + dnb[...]
            center = jnp.mean(s, axis=-1, keepdims=True)
            e = s - center
            spread = jnp.mean(e * e, axis=-1, keepdims=True)
            y = e * lax.rsqrt(spread + 1e-5) * gain[...] + bias[...]
            m = jnp.sum(y * y, axis=-1, keepdims=True)
            unit = (y * lax.rsqrt(m + 1e-6)).astype(jnp.bfloat16)
            if c < L * n_cand:
                co_ref[r, :] = unit
            else:
                ro_ref[c - L * n_cand : c - L * n_cand + 64, :] = unit


def encode(picks, cand, rh, words, layer, f=1024, sub=4):
    def full(a):
        return pl.BlockSpec(a.shape, lambda i: (0,) * a.ndim, pipeline_mode=pl.Buffered(1))

    up, upb, dn, dnb, gain, bias = layer
    n_cand = 0 if cand is None else 1
    extra = 16 if words else 0
    seqs = n_cand + len(picks)
    smem = pl.BlockSpec(memory_space=pltpu.SMEM)
    outs = [jax.ShapeDtypeStruct((L + extra, D), jnp.bfloat16)] * n_cand + [
        jax.ShapeDtypeStruct((len(picks) * L + extra, D), jnp.bfloat16)
    ]
    first = list(words) + ([cand] if n_cand else []) + [rh]
    return pl.pallas_call(
        functools.partial(encode_kernel, n_cand, picks, bool(words), sub),
        grid=(up.shape[1] // f,),
        in_specs=[smem if k < 2 and words else full(a) for k, a in enumerate(first)]
        + [
            pl.BlockSpec((D, f), lambda i: (0, i)),
            pl.BlockSpec((1, f), lambda i: (0, i)),
            pl.BlockSpec((f, D), lambda i: (i, 0)),
            full(dnb),
            full(gain),
            full(bias),
        ],
        out_specs=[pl.BlockSpec(o.shape, lambda i: (0, 0)) for o in outs],
        out_shape=outs,
        scratch_shapes=[
            pltpu.VMEM((seqs * L, D), jnp.bfloat16),
            pltpu.VMEM((seqs * L, D), jnp.float32),
        ],
        compiler_params=pltpu.CompilerParams(
            dimension_semantics=("arbitrary",), vmem_limit_bytes=60 << 20
        ),
        cost_estimate=pl.CostEstimate(
            flops=4 * seqs * L * D * up.shape[1], bytes_accessed=17 << 20, transcendentals=0
        ),
        name="encode",
    )(*first, up, upb, dn, dnb, gain, bias)


GROUP = 4


def score_listed(todo, n, acc, total, cands, refs, cbuf, rbuf, wbuf, sem):
    def start(t, b):
        for k, buf in enumerate(cands):
            @pl.when(todo[0, t] == k)
            def _():
                pltpu.make_async_copy(buf.at[todo[1, t]], cbuf.at[b], sem.at[0, b]).start()
        at = pl.multiple_of(todo[3, t] * L, L)
        for k, buf in enumerate(refs):
            @pl.when(todo[2, t] == k)
            def _():
                words = refs[k - k % 2]
                pltpu.make_async_copy(buf.at[pl.ds(at, L), :], rbuf.at[b], sem.at[1, b]).start()
                pltpu.make_async_copy(
                    words.at[pl.ds(2 * L, 16), pl.ds(0, L)], wbuf.at[b], sem.at[2, b]
                ).start()

    def start_group(g):
        for k in range(GROUP):
            t = g * GROUP + k

            @pl.when(t < n)
            def _(t=t, k=k):
                start(t, (g % 2) * GROUP + k)

    start_group(0)
    lane = lax.broadcasted_iota(jnp.int32, (8, L), 1)
    sub = lax.broadcasted_iota(jnp.int32, (8, L), 0)
    eye = lax.broadcasted_iota(jnp.int32, (L, L), 0) == lax.broadcasted_iota(jnp.int32, (L, L), 1)

    def one(t, b):
        similar = lax.dot_general(
            cbuf[b, 0:L, :], rbuf[b], (((1,), (1,)), ((), ())), preferred_element_type=jnp.float32
        )
        cw = cbuf[b, L:, 0:L].astype(jnp.float32)[0:1, :]
        wide = wbuf[b].astype(jnp.float32)
        rsub = lax.broadcasted_iota(jnp.int32, (16, L), 0)
        rw = jnp.sum(jnp.where(rsub == todo[4, t], wide, 0.0), axis=0, keepdims=True)
        cw_col = jnp.sum(jnp.where(eye, cw, 0.0), axis=1, keepdims=True)
        row_best = jnp.max(jnp.where(rw > 0, similar, -10000.0), axis=1, keepdims=True)
        col_best = jnp.max(jnp.where(cw_col > 0, similar, -10000.0), axis=0, keepdims=True)
        precision = jnp.sum(cw_col * row_best, axis=0, keepdims=True) / jnp.sum(
            cw, axis=1, keepdims=True
        )
        recall = jnp.sum(rw * col_best, axis=1, keepdims=True) / jnp.sum(rw, axis=1, keepdims=True)
        fmeasure = 2.0 * precision * recall / jnp.maximum(precision + recall, 0.7)
        return precision, recall, fmeasure

    def group(g, carry):
        acc, total = carry
        start_group(g + 1)
        for k in range(GROUP):
            b = (g % 2) * GROUP + k

            @pl.when(g * GROUP + k < n)
            def _(b=b):
                pltpu.make_async_copy(cands[0].at[0], cbuf.at[b], sem.at[0, b]).wait()
                pltpu.make_async_copy(refs[0].at[pl.ds(0, L), :], rbuf.at[b], sem.at[1, b]).wait()
                pltpu.make_async_copy(
                    refs[0].at[pl.ds(2 * L, 16), pl.ds(0, L)], wbuf.at[b], sem.at[2, b]
                ).wait()

        scores = []
        for k in range(GROUP):
            t = jnp.minimum(g * GROUP + k, n - 1)
            scores.append((t, g * GROUP + k < n, one(t, (g % 2) * GROUP + k)))
        for t, real, (p, r, f) in scores:
            three = jnp.where(lane < 32, p, jnp.where(lane < 64, r, f))
            here = (sub == todo[5, t]) & ((lane & 31) == todo[6, t]) & (lane < 96) & real
            acc = jnp.where(here, three, acc)
            rows = jnp.where(sub == 0, p, jnp.where(sub == 1, r, f))
            total = total + jnp.where(real, rows, 0.0)
        return acc, total

    return lax.fori_loop(0, (n + GROUP - 1) // GROUP, group, (acc, total))


def early_kernel(pos_ref, l0, l1, l2, l3, *refs):
    cands, refs_, (out_ref, later, cbuf, rbuf, wbuf, todo, sem) = refs[:10], refs[10:16], refs[16:]
    y, core, x, z = pos_ref[0], pos_ref[1], pos_ref[2], pos_ref[3]
    n = m = jnp.int32(0)
    for lst, dz in ((l0, 0), (l1, 3), (l2, 1), (l3, 2)):
        zj = (z + dz) & 3

        def scan(s, counts, lst=lst, dz=dz, zj=zj):
            n, m = counts
            c = lst[0, s]
            r = lst[0, SLOTS + s]
            mine = (r & 3) == z
            dx = (((r & 15) >> 2) - x) & 3
            late = mine & (dx == 2)
            soon = mine & (dx != 2)
            kc = c & 1
            dy = ((c >> 1) - y) & 3
            u1 = jnp.where(kc == 0, dy, dz)
            u2 = jnp.where(kc == 0, dz, dy)
            i1 = (4 - u1) & 3
            g2 = (u2 == 3) * 1 + (u2 == 1) * 2 + (u2 == 2) * 3
            g2 = jnp.where((g2 == 3) & (i1 >= 2), 4, g2)
            src = g2 + jnp.where(kc == core, 0, 5)
            row = jnp.where(g2 == 4, i1 - 2, i1)
            i = r >> 4
            back = jnp.where(core == 0, 3, 1)
            rs = jnp.where(dx == 0, 0, jnp.where(dx == 2, 3, jnp.where(dx == back, 1, 2)))

            def put(where, k, rs):
                where[0, k] = src
                where[1, k] = row
                where[2, k] = rs * 2 + (i >> 1)
                where[3, k] = i & 1
                where[4, k] = i
                where[5, k] = zj
                where[6, k] = s

            @pl.when(soon)
            def _():
                put(todo, n, rs)

            @pl.when(late)
            def _():
                put(later, m, 0)

            return n + jnp.where(soon, 1, 0), m + jnp.where(late, 1, 0)

        n, m = lax.fori_loop(0, lst[0, 2 * SLOTS], scan, (n, m))
    later[7, 0] = m
    zero = jnp.zeros((8, L), jnp.float32)
    acc, total = score_listed(todo, n, zero, zero, cands, refs_, cbuf, rbuf, wbuf, sem)
    out_ref[0] = acc
    out_ref[1] = total


def late_kernel(pos_ref, l0, todo, *refs):
    cands, refs_, (part, out_ref, cbuf, rbuf, wbuf, sem) = refs[:10], refs[10:12], refs[12:]
    y, core, x = pos_ref[0], pos_ref[1], pos_ref[2]
    acc, total = score_listed(todo, todo[7, 0], part[0], part[1], cands, refs_, cbuf, rbuf, wbuf, sem)
    lane = lax.broadcasted_iota(jnp.int32, (1, L), 1)
    count = l0[0, 2 * SLOTS].astype(jnp.float32)
    sums = jnp.where(
        lane == 96,
        total[0:1, :],
        jnp.where(lane == 97, total[1:2, :], jnp.where(lane == 98, total[2:3, :], count)),
    )
    sums = jnp.where((lane >= 96) & (lane < 100), sums, 0.0)
    for q in range(out_ref.shape[0]):
        out_ref[q] = sums
    mine = (y * 2 + core) * 4 + x
    for q in range(4):
        out_ref[mine * 4 + q] = acc[q : q + 1, :] + sums


def pair_call(kernel, name, smem_args, hbm_args, vmem_args, out_specs, out_shape, scratch):
    smem = pl.BlockSpec(memory_space=pltpu.SMEM)
    hbm = pl.BlockSpec(memory_space=pl.ANY)
    vmem = pl.BlockSpec(memory_space=pltpu.VMEM)
    return pl.pallas_call(
        kernel,
        in_specs=[smem] * len(smem_args) + [hbm] * len(hbm_args) + [vmem] * len(vmem_args),
        out_specs=out_specs,
        out_shape=out_shape,
        scratch_shapes=[
            pltpu.VMEM((2 * GROUP, L + 16, D), jnp.bfloat16),
            pltpu.VMEM((2 * GROUP, L, D), jnp.bfloat16),
            pltpu.VMEM((2 * GROUP, 16, L), jnp.bfloat16),
            *scratch,
            pltpu.SemaphoreType.DMA((3, 2 * GROUP)),
        ],
        compiler_params=pltpu.CompilerParams(vmem_limit_bytes=60 << 20),
        cost_estimate=pl.CostEstimate(
            flops=1 << 30, bytes_accessed=16 << 20, transcendentals=0
        ),
        name=name,
    )(*smem_args, *hbm_args, *vmem_args)


def on_device(
    cand_hidden, ref_hidden, cand_ids, ref_ids, cand_len, reference_length, idf_table, up_weight,
    up_bias, down_weight, down_bias, norm_gain, norm_bias, pair_cand, pair_ref, pair_count,
):
    table = jnp.pad(idf_table, (0, TABLE_ROWS * 128 - idf_table.shape[0]))
    table = table.reshape(TABLE_ROWS, 128).astype(jnp.bfloat16)
    layer = (
        up_weight,
        up_bias.reshape(1, -1),
        down_weight,
        down_bias.reshape(1, -1),
        norm_gain.reshape(1, -1),
        norm_bias.reshape(1, -1),
    )
    hidden = ref_hidden.reshape(4, L, D)
    words = (
        cand_len.reshape(1),
        reference_length.reshape(4),
        cand_ids.reshape(1, L),
        ref_ids.reshape(4, L),
        table,
    )
    cand, refs_a = encode((0, 1), cand_hidden.reshape(1, L, D), hidden, words, layer)
    back_a = send(refs_a, along_x(1))
    ahead_a = send(refs_a, along_x(-1))
    c1 = send(cand, along_first(1))
    c3 = send(cand, along_first(-1))
    c2 = send(cand, along_first(2))
    (refs_b,) = encode((2, 3), None, hidden, (), layer)
    back_a, ahead_a, c1, c2, c3, refs_b = lax.optimization_barrier(
        (back_a, ahead_a, c1, c2, c3, refs_b)
    )
    back_b = send(refs_b, along_x(1))
    ahead_b = send(refs_b, along_x(-1))
    far_a = send(back_a, along_x(1))
    own4 = jnp.stack([cand, c1, c2, c3])
    d1 = send(own4, along_second(1))
    d2 = send(own4, along_second(-1))
    d3 = send(d1[:2], along_second(1))
    d4 = send(d2[2:], along_second(-1))
    d3, d4, far_a, back_b, ahead_b = lax.optimization_barrier((d3, d4, far_a, back_b, ahead_b))
    far_b = send(back_b, along_x(1))
    others = [send(v, to_other_core) for v in (own4, d1, d2, d3, d4)]
    cands = [own4, d1, d2, d3, d4, *others]
    slots = jnp.concatenate(
        [
            pair_cand.reshape(-1),
            pair_ref.reshape(-1),
            jnp.broadcast_to(pair_count.reshape(1), (2 * SLOTS,)),
        ]
    ).reshape(1, 4 * SLOTS)
    lists = [slots] + [send(slots, along_z(k)) for k in (1, -1, 2)]
    dp, prompt = lax.axis_index("dp"), lax.axis_index("prompt")
    pos = jnp.stack([dp >> 1, dp & 1, prompt >> 2, prompt & 3]).astype(jnp.int32)
    part, later = pair_call(
        early_kernel,
        "score_early",
        [pos, *lists],
        [*cands, refs_a, refs_b, back_a, back_b, ahead_a, ahead_b],
        [],
        [pl.BlockSpec(memory_space=pltpu.VMEM), pl.BlockSpec(memory_space=pltpu.SMEM)],
        [
            jax.ShapeDtypeStruct((2, 8, L), jnp.float32),
            jax.ShapeDtypeStruct((8, 4 * SLOTS), jnp.int32),
        ],
        [pltpu.SMEM((8, 4 * SLOTS), jnp.int32)],
    )
    payload = pair_call(
        late_kernel,
        "score_late",
        [pos, slots, later],
        [*cands, far_a, far_b],
        [part],
        pl.BlockSpec(memory_space=pltpu.VMEM),
        jax.ShapeDtypeStruct((128, 1, L), jnp.float32),
        [],
    )
    got = jnp.sum(lax.all_to_all(payload, AXES, 0, 0), axis=0)
    scores = got[:, : 3 * SLOTS].reshape(3, 1, 1, SLOTS)
    return scores, got[0, 96:99] / got[0, 99]


def solution(mesh):
    placed = (
        P("prompt", "dp", None, None),
        P("dp", "prompt", None, None),
        P("prompt", "dp", None),
        P("dp", "prompt", None),
        P("prompt", "dp"),
        P("dp", "prompt"),
        P(),
        P(),
        P(),
        P(),
        P(),
        P(),
        P(),
        P("dp", "prompt", None),
        P("dp", "prompt", None),
        P("dp", "prompt"),
    )
    return jax.shard_map(
        on_device,
        mesh=mesh,
        in_specs=placed,
        out_specs=(P(None, "dp", "prompt", None), P()),
        check_vma=False,
    )
```

time: 129 us -> 114 us (0.88)
  waiting for transfers between devices: 46 us -> 14.1 us
  blocking collectives: 0 us -> 16.8 us
  starting transfers between devices: 42.1 us -> 33.5 us
  Pallas kernels: 31.4 us -> 39 us
  local copies, waits for them, and re-layouts: 2 us -> 4.71 us
    ppermute x18 -> x21, waiting for transfers between devices: 32.6 us -> 14.1 us  [send(): lax.ppermute(value, AXES, [(number(*a), number(*where(*a))) for a in GRID])]
    all_to_all x0 -> x1, blocking collectives: none -> 16.8 us  [on_device(): got = jnp.sum(lax.all_to_all(payload, AXES, 0, 0), axis=0)]
    all_to_all x1 -> x0, waiting for transfers between devices: 13.4 us -> none  [on_device(): got = jnp.sum(lax.all_to_all(payload, AXES, 0, 0), axis=0)]
    pallas_call x2 -> x4, Pallas kernels: 31.4 us -> 39 us  [the longest x2 24 us: encode(): pl.pallas_call(functools.partial(encode_kernel, n_cand, picks, bool(words...]
    all_to_all x1 -> x0, starting transfers between devices: 7.35 us -> none  [on_device(): got = jnp.sum(lax.all_to_all(payload, AXES, 0, 0), axis=0)]
    unnamed x25 -> x34, local copies, waits for them, and re-layouts: 0.61 us -> 2.72 us
    ppermute x18 -> x21, starting transfers between devices: 34.8 us -> 33.5 us  [send(): lax.ppermute(value, AXES, [(number(*a), number(*where(*a))) for a in GRID])]
  transfers between devices with their start and end apart: 19 -> 21, of which waited for: 7 -> 6; matrix products, arithmetic and copies ran while one was open for 1% -> 1% of each run, Pallas kernels for 0% -> 19%
where the time goes in v2:
time: 114 us; the launch traced here: 113 us
  Pallas kernels  39 us (34%)
  starting transfers between devices  33.5 us (29%)
  blocking collectives  16.8 us (15%)
  waiting for transfers between devices  14.1 us (12%)
  local copies, waits for them, and re-layouts  4.71 us (4%)
  other arithmetic  3.14 us (3%)
  between operations  2.15 us (2%)
    ppermute x21, starting transfers between devices, send(): lax.ppermute(value, AXES, [(number(*a), number(*where(*a))) for a in GRID])  33.5 us
    pallas_call x2, Pallas kernels, encode(): pl.pallas_call(functools.partial(encode_kernel, n_cand, picks, bool(words...  24 us
    all_to_all x1, blocking collectives, on_device(): got = jnp.sum(lax.all_to_all(payload, AXES, 0, 0), axis=0)  16.8 us
    pallas_call x2, Pallas kernels, pair_call(): pl.pallas_call(kernel, in_specs=[smem] * len(smem_args) + [hbm] * len(hbm...  15 us
    ppermute x21, waiting for transfers between devices, send(): lax.ppermute(value, AXES, [(number(*a), number(*where(*a))) for a in GRID])  14.1 us
    unnamed x34, local copies, waits for them, and re-layouts  2.72 us
  transfers between devices with their start and end apart: 21, of which 6 were waited for; matrix products, arithmetic and copies ran while one was open for 1% of the time, Pallas kernels for 19%

profile of v2, /device:TPU:1, one launch (start us, length us, event | category | flops | bytes accessed | tf_op | source)
XLA Modules:
  0.0 113.4 jit_solution(11568650180873847687)
XLA Ops:
  0.6 0.9 convert.4
  1.6 0.7 pad_bitcast_fusion.refs_4_
  2.9 13.3 %encode.2 = (bf16[144,1024]{1,0:T(8,128)(2,1)}, bf16[272,1024]{1,0:T(8,128)(2,1)}) custom-call(s32[1]{0:T(128)} %bitcast.29.refs_0_, s32[4]{0:T(128)} %bitcast.52, s32[1,128]{1,0:T(1,128)} %bitcast.53, s32[4,128]{1,0:T(4,128)} %bitcast.51, bf16[400,128]{1,0:T(8,128)(2,1)} %pad_bitcast_fusion.refs_4_, bf16[1,128,1024]{2,1,0:T(8,128)(2,1)} %bitcast.50, ...), custom_call_target="tpu_custom_call" | custom-call | flops 6442450944 | bytes 17825792 | tf_op jit(solution)/shard_map/encode/pallas_call | solution.py:139
  16.1 3.3 %collective-permute-start.3 = (bf16[272,1024]{1,0:T(8,128)(2,1)}, bf16[272,1024]{1,0:T(8,128)(2,1)S(1)}, u32[]{:S(2)}, u32[]{:S(2)}) collective-permute-start(bf16[272,1024]{1,0:T(8,128)(2,1)} %get-tuple-element.18.refs_10_), channel_id=1, source_target_pairs={{0,4},{1,5},{2,6},{3,7},{4,8},{5,9},{6,10},{7,11},{8,12},{9,13},{1... | collective-permute-start | bytes 1671176 | tf_op jit(solution)/shard_map/ppermute | solution.py:23
  19.5 0.0 collective-permute-start.4
  19.5 1.6 %collective-permute-start.5 = (bf16[144,1024]{1,0:T(8,128)(2,1)}, bf16[144,1024]{1,0:T(8,128)(2,1)S(1)}, u32[]{:S(2)}, u32[]{:S(2)}) collective-permute-start(bf16[144,1024]{1,0:T(8,128)(2,1)} %get-tuple-element.17), channel_id=1, source_target_pairs={{0,32},{1,33},{2,34},{3,35},{4,36},{5,37},{6,38},{7,39},{8,40},{9,... | collective-permute-start | bytes 884744 | tf_op jit(solution)/shard_map/ppermute | solution.py:23
  21.1 3.3 %collective-permute-start.6 = (bf16[144,1024]{1,0:T(8,128)(2,1)}, bf16[144,1024]{1,0:T(8,128)(2,1)S(1)}, u32[]{:S(2)}, u32[]{:S(2)}) collective-permute-start(bf16[144,1024]{1,0:T(8,128)(2,1)} %get-tuple-element.17), channel_id=1, source_target_pairs={{0,64},{1,65},{2,66},{3,67},{4,68},{5,69},{6,70},{7,71},{8,72},{9,... | collective-permute-start | bytes 884744 | tf_op jit(solution)/shard_map/ppermute | solution.py:23
  24.4 0.7 collective-permute-start.7
  25.1 10.7 %encode.3.refs_11_ = bf16[256,1024]{1,0:T(8,128)(2,1)} custom-call(bf16[4,128,1024]{2,1,0:T(8,128)(2,1)} %bitcast.32, bf16[1024,4096]{1,0:T(8,128)(2,1)} %refs_1_.1, f32[1,4096]{1,0:T(1,128)} %bitcast.38, bf16[4096,1024]{1,0:T(8,128)(2,1)} %refs_3_.1, f32[1,1024]{1,0:T(1,128)} %bitcast.40, f32[1,1024]{1,0:T(1,128)} %bitcast.42, f32[1,1024]{1,0:T(1,128)} %bitcast.44), custom_call_target="tpu_custom_call" | custom-call | flops 4294967296 | bytes 17825792 | tf_op jit(solution)/shard_map/encode/pallas_call | solution.py:139
  35.9 0.0 collective-permute-done.5
  35.9 0.0 collective-permute-done.6
  35.9 0.0 collective-permute-done.7
  35.9 0.0 collective-permute-done.3.refs_12_
  35.9 0.0 copy-start.6
  35.9 0.0 collective-permute-done.4.refs_14_
  35.9 0.0 copy-start.7
  35.9 0.8 copy-done.7
  36.8 0.0 copy-done.10
  36.8 0.2 pad_maximum_fusion.refs_0_
  37.0 0.0 copy-start
  37.0 1.4 %collective-permute-start.8 = (bf16[4,144,1024]{2,1,0:T(8,128)(2,1)S(1)}, bf16[4,144,1024]{2,1,0:T(8,128)(2,1)S(1)}, u32[]{:S(2)}, u32[]{:S(2)}) collective-permute-start(bf16[4,144,1024]{2,1,0:T(8,128)(2,1)S(1)} %pad_maximum_fusion.refs_0_), channel_id=1, source_target_pairs={{0,1},{1,2},{2,3},{3,0},{4,5},{5,6},{6,7},{7,4},{8,9},{9,10},{10,1... | collective-permute-start | bytes 3538952 | tf_op jit(solution)/shard_map/ppermute | solution.py:23
  38.3 1.5 %collective-permute-start.9 = (bf16[4,144,1024]{2,1,0:T(8,128)(2,1)S(1)}, bf16[4,144,1024]{2,1,0:T(8,128)(2,1)S(1)}, u32[]{:S(2)}, u32[]{:S(2)}) collective-permute-start(bf16[4,144,1024]{2,1,0:T(8,128)(2,1)S(1)} %pad_maximum_fusion.refs_0_), channel_id=1, source_target_pairs={{0,3},{1,0},{2,1},{3,2},{4,7},{5,4},{6,5},{7,6},{8,11},{9,8},{10,9... | collective-permute-start | bytes 3538952 | tf_op jit(solution)/shard_map/ppermute | solution.py:23
  40.5 2.7 %collective-permute-start.13 = (bf16[256,1024]{1,0:T(8,128)(2,1)S(1)}, bf16[256,1024]{1,0:T(8,128)(2,1)}, u32[]{:S(2)}, u32[]{:S(2)}) collective-permute-start(bf16[256,1024]{1,0:T(8,128)(2,1)S(1)} %copy-done.4), channel_id=1, source_target_pairs={{0,4},{1,5},{2,6},{3,7},{4,8},{5,9},{6,10},{7,11},{8,12},{9,13},{1... | collective-permute-start | bytes 1572872 | tf_op jit(solution)/shard_map/ppermute | solution.py:23
  43.3 0.1 collective-permute-start.12
  43.4 0.1 add_bitcast_fusion.l0
  43.4 0.7 collective-permute-start
  44.2 3.2 %collective-permute-done.l1 = s32[1,128]{1,0:T(1,128)S(1)} collective-permute-done((s32[1,128]{1,0:T(1,128)S(1)}, s32[1,128]{1,0:T(1,128)S(1)}, u32[]{:S(2)}, u32[]{:S(2)}) %collective-permute-start) | collective-permute-done | bytes 544 | tf_op jit(solution)/shard_map/ppermute | solution.py:23
  47.4 1.4 %collective-permute-start.14 = (bf16[256,1024]{1,0:T(8,128)(2,1)S(1)}, bf16[256,1024]{1,0:T(8,128)(2,1)S(1)}, u32[]{:S(2)}, u32[]{:S(2)}) collective-permute-start(bf16[256,1024]{1,0:T(8,128)(2,1)S(1)} %copy-done.4), channel_id=1, source_target_pairs={{0,12},{1,13},{2,14},{3,15},{4,0},{5,1},{6,2},{7,3},{8,4},{9,5},{1... | collective-permute-start | bytes 1572872 | tf_op jit(solution)/shard_map/ppermute | solution.py:23
  48.8 5.0 %collective-permute-done.8.refs_1_ = bf16[4,144,1024]{2,1,0:T(8,128)(2,1)S(1)} collective-permute-done((bf16[4,144,1024]{2,1,0:T(8,128)(2,1)S(1)}, bf16[4,144,1024]{2,1,0:T(8,128)(2,1)S(1)}, u32[]{:S(2)}, u32[]{:S(2)}) %collective-permute-start.8) | collective-permute-done | bytes 1179680 | tf_op jit(solution)/shard_map/ppermute | solution.py:23
  53.8 4.7 %collective-permute-start.15 = (bf16[4,144,1024]{2,1,0:T(8,128)(2,1)S(1)}, bf16[4,144,1024]{2,1,0:T(8,128)(2,1)S(1)}, u32[]{:S(2)}, u32[]{:S(2)}) collective-permute-start(bf16[4,144,1024]{2,1,0:T(8,128)(2,1)S(1)} %pad_maximum_fusion.refs_0_), channel_id=1, source_target_pairs={{0,16},{1,17},{2,18},{3,19},{4,20},{5,21},{6,22},{7,23},{8,24},{9,... | collective-permute-start | bytes 3538952 | tf_op jit(solution)/shard_map/ppermute | solution.py:23
  58.5 0.0 collective-permute-done.9.refs_2_
  58.5 0.5 collective-permute-start.10
  59.1 0.0 collective-permute-done.13.refs_13_
  59.1 2.3 %collective-permute-start.11 = (bf16[2,144,1024]{2,1,0:T(8,128)(2,1)S(1)}, bf16[2,144,1024]{2,1,0:T(8,128)(2,1)}, u32[]{:S(2)}, u32[]{:S(2)}) collective-permute-start(bf16[2,144,1024]{2,1,0:T(8,128)(2,1)S(1)} %slice.21), channel_id=1, source_target_pairs={{0,3},{1,0},{2,1},{3,2},{4,7},{5,4},{6,5},{7,6},{8,11},{9,8},{10,9... | collective-permute-start | bytes 1769480 | tf_op jit(solution)/shard_map/ppermute | solution.py:23
  61.4 1.2 %collective-permute-done.14.refs_15_ = bf16[256,1024]{1,0:T(8,128)(2,1)S(1)} collective-permute-done((bf16[256,1024]{1,0:T(8,128)(2,1)S(1)}, bf16[256,1024]{1,0:T(8,128)(2,1)S(1)}, u32[]{:S(2)}, u32[]{:S(2)}) %collective-permute-start.14) | collective-permute-done | bytes 524320 | tf_op jit(solution)/shard_map/ppermute | solution.py:23
  62.6 3.5 %collective-permute-start.16 = (bf16[4,144,1024]{2,1,0:T(8,128)(2,1)S(1)}, bf16[4,144,1024]{2,1,0:T(8,128)(2,1)}, u32[]{:S(2)}, u32[]{:S(2)}) collective-permute-start(bf16[4,144,1024]{2,1,0:T(8,128)(2,1)S(1)} %collective-permute-done.8.refs_1_), channel_id=1, source_target_pairs={{0,16},{1,17},{2,18},{3,19},{4,20},{5,21},{6,22},{7,23},{8,24},{9,... | collective-permute-start | bytes 3538952 | tf_op jit(solution)/shard_map/ppermute | solution.py:23
  66.1 0.0 collective-permute-done.12.refs_10_
  66.1 0.1 collective-permute-start.17
  66.2 2.8 %collective-permute-done.10.refs_3_ = bf16[2,144,1024]{2,1,0:T(8,128)(2,1)} collective-permute-done((bf16[2,144,1024]{2,1,0:T(8,128)(2,1)S(1)}, bf16[2,144,1024]{2,1,0:T(8,128)(2,1)}, u32[]{:S(2)}, u32[]{:S(2)}) %collective-permute-start.10) | collective-permute-done | bytes 589856 | tf_op jit(solution)/shard_map/ppermute | solution.py:23
  69.0 1.7 %collective-permute-start.1 = (s32[1,128]{1,0:T(1,128)S(1)}, s32[1,128]{1,0:T(1,128)S(1)}, u32[]{:S(2)}, u32[]{:S(2)}) collective-permute-start(s32[1,128]{1,0:T(1,128)S(1)} %add_bitcast_fusion.l0), channel_id=1, source_target_pairs={{0,3},{1,0},{2,1},{3,2},{4,7},{5,4},{6,5},{7,6},{8,11},{9,8},{10,9... | collective-permute-start | bytes 1544 | tf_op jit(solution)/shard_map/ppermute | solution.py:23
  70.7 0.0 collective-permute-done.11.refs_4_
  70.7 0.0 copy-done.11
  70.7 0.0 collective-permute-start.2
  70.7 0.7 collective-permute-done.1.l2
  71.4 1.9 %collective-permute-start.18 = (bf16[2,144,1024]{2,1,0:T(8,128)(2,1)}, bf16[2,144,1024]{2,1,0:T(8,128)(2,1)}, u32[]{:S(2)}, u32[]{:S(2)}) collective-permute-start(bf16[2,144,1024]{2,1,0:T(8,128)(2,1)} %collective-permute-done.10.refs_3_), channel_id=1, source_target_pairs={{0,16},{1,17},{2,18},{3,19},{4,20},{5,21},{6,22},{7,23},{8,24},{9,... | collective-permute-start | bytes 1769480 | tf_op jit(solution)/shard_map/ppermute | solution.py:23
  73.4 1.2 %collective-permute-done.2.l3 = s32[1,128]{1,0:T(1,128)S(1)} collective-permute-done((s32[1,128]{1,0:T(1,128)S(1)}, s32[1,128]{1,0:T(1,128)S(1)}, u32[]{:S(2)}, u32[]{:S(2)}) %collective-permute-start.2) | collective-permute-done | bytes 544 | tf_op jit(solution)/shard_map/ppermute | solution.py:23
  74.6 1.1 collective-permute-start.19
  75.7 0.0 collective-permute-done.15.refs_5_
  75.7 1.0 copy-done.3
  76.7 0.8 collective-permute-start.20
  77.5 0.6 pad_add_fusion.pos_ref
  78.1 0.0 collective-permute-done.18.refs_8_
  78.1 0.0 collective-permute-done.19.refs_9_
  78.1 0.0 collective-permute-done.16.refs_6_
  78.1 0.0 collective-permute-done.17.refs_7_
  78.2 11.3 %score_early.1 = (f32[2,8,128]{2,1,0:T(8,128)}, s32[8,128]{1,0:T(8,128)}) custom-call(s32[4]{0:T(128)} %pad_add_fusion.pos_ref, s32[1,128]{1,0:T(1,128)} %copy-done.11, s32[1,128]{1,0:T(1,128)} %copy-done.12, s32[1,128]{1,0:T(1,128)} %copy-done.13, s32[1,128]{1,0:T(1,128)} %copy-done.14, bf16[4,144,1024]{2,1,0:T(8,128)(2,1)} %copy-done, ...), custom_call_target="tpu_custom_call" | custom-call | flops 1073741824 | bytes 16777216 | tf_op jit(solution)/shard_map/score_early/pallas_call | solution.py:324
  89.5 0.0 collective-permute-done.20.refs_11_
  89.5 0.8 copy-done.8
  90.3 3.7 %score_late.1 = f32[128,1,128]{2,1,0:T(1,128)} custom-call(s32[4]{0:T(128)} %pad_add_fusion.pos_ref, s32[1,128]{1,0:T(1,128)} %copy-done.11, s32[8,128]{1,0:T(8,128)} %get-tuple-element.29.todo, bf16[4,144,1024]{2,1,0:T(8,128)(2,1)} %copy-done, bf16[4,144,1024]{2,1,0:T(8,128)(2,1)} %copy-done.1, bf16[4,144,1024]{2,1,0:T(8,128)(2,1)} %copy-done.2, ...), custom_call_target="tpu_custom_call" | custom-call | flops 1073741824 | bytes 16777216 | tf_op jit(solution)/shard_map/score_late/pallas_call | solution.py:324
  94.0 16.8 %all_to_all.5 = f32[128,1,128]{2,1,0:T(1,128)S(1)} all-to-all(f32[128,1,128]{2,1,0:T(1,128)} %score_late.1), channel_id=1, replica_groups=mesh['dp'=8,'prompt'=16] {'dp','prompt'}, dimensions={0} | all-to-all | bytes 131072 | tf_op jit(solution)/shard_map/all_to_all | solution.py:421
  110.8 0.2 reduce_sum.11
  110.9 0.6 slice.19
  111.5 1.2 %divide_bitcast_fusion = f32[3]{0:T(128)} fusion(f32[1,128]{1,0:T(1,128)S(1)} %bitcast.47, f32[]{:T(128)} %bitcast.24), kind=kLoop, calls=%fused_computation.4 | loop fusion | flops 3 | bytes 28 | tf_op jit(solution)/shard_map/div | solution.py:423
  112.8 0.6 reshape.67
  (30 shorter events, 0.1 us)
Async XLA Ops:
  16.1 19.8 %collective-permute-start.3 = (bf16[272,1024]{1,0:T(8,128)(2,1)}, bf16[272,1024]{1,0:T(8,128)(2,1)S(1)}, u32[]{:S(2)}, u32[]{:S(2)}) collective-permute-start(bf16[272,1024]{1,0:T(8,128)(2,1)} %get-tuple-element.18.refs_10_), channel_id=1, source_target_pairs={{0,4},{1,5},{2,6},{3,7},{4,8},{5,9},{6,10},{7,11},{8,12},{9,13},{1... | collective-permute-start | bytes 1671176 | tf_op jit(solution)/shard_map/ppermute | solution.py:23
  19.5 16.5 %collective-permute-start.4 = (bf16[272,1024]{1,0:T(8,128)(2,1)}, bf16[272,1024]{1,0:T(8,128)(2,1)S(1)}, u32[]{:S(2)}, u32[]{:S(2)}) collective-permute-start(bf16[272,1024]{1,0:T(8,128)(2,1)} %get-tuple-element.18.refs_10_), channel_id=1, source_target_pairs={{0,12},{1,13},{2,14},{3,15},{4,0},{5,1},{6,2},{7,3},{8,4},{9,5},{1... | collective-permute-start | bytes 1671176 | tf_op jit(solution)/shard_map/ppermute | solution.py:23
  19.5 17.3 %copy-start.10 = (bf16[144,1024]{1,0:T(8,128)(2,1)S(1)}, bf16[144,1024]{1,0:T(8,128)(2,1)}, u32[]{:S(2)}) copy-start(bf16[144,1024]{1,0:T(8,128)(2,1)} %get-tuple-element.17) | copy-start | bytes 884740
  19.5 16.4 %collective-permute-start.5 = (bf16[144,1024]{1,0:T(8,128)(2,1)}, bf16[144,1024]{1,0:T(8,128)(2,1)S(1)}, u32[]{:S(2)}, u32[]{:S(2)}) collective-permute-start(bf16[144,1024]{1,0:T(8,128)(2,1)} %get-tuple-element.17), channel_id=1, source_target_pairs={{0,32},{1,33},{2,34},{3,35},{4,36},{5,37},{6,38},{7,39},{8,40},{9,... | collective-permute-start | bytes 884744 | tf_op jit(solution)/shard_map/ppermute | solution.py:23
  21.1 14.8 %collective-permute-start.6 = (bf16[144,1024]{1,0:T(8,128)(2,1)}, bf16[144,1024]{1,0:T(8,128)(2,1)S(1)}, u32[]{:S(2)}, u32[]{:S(2)}) collective-permute-start(bf16[144,1024]{1,0:T(8,128)(2,1)} %get-tuple-element.17), channel_id=1, source_target_pairs={{0,64},{1,65},{2,66},{3,67},{4,68},{5,69},{6,70},{7,71},{8,72},{9,... | collective-permute-start | bytes 884744 | tf_op jit(solution)/shard_map/ppermute | solution.py:23
  24.4 11.5 %collective-permute-start.7 = (bf16[144,1024]{1,0:T(8,128)(2,1)}, bf16[144,1024]{1,0:T(8,128)(2,1)S(1)}, u32[]{:S(2)}, u32[]{:S(2)}) collective-permute-start(bf16[144,1024]{1,0:T(8,128)(2,1)} %get-tuple-element.17), channel_id=1, source_target_pairs={{0,96},{1,97},{2,98},{3,99},{4,100},{5,101},{6,102},{7,103},{8,104... | collective-permute-start | bytes 884744 | tf_op jit(solution)/shard_map/ppermute | solution.py:23
  35.9 7.3 %copy-start.6 = (bf16[272,1024]{1,0:T(8,128)(2,1)}, bf16[272,1024]{1,0:T(8,128)(2,1)S(1)}, u32[]{:S(2)}) copy-start(bf16[272,1024]{1,0:T(8,128)(2,1)S(1)} %collective-permute-done.3.refs_12_) | copy-start | bytes 1671172
  35.9 0.8 copy-start.7
  36.8 3.7 %copy-start.4 = (bf16[256,1024]{1,0:T(8,128)(2,1)S(1)}, bf16[256,1024]{1,0:T(8,128)(2,1)}, u32[]{:S(2)}) copy-start(bf16[256,1024]{1,0:T(8,128)(2,1)} %encode.3.refs_11_) | copy-start | bytes 1572868
  36.8 6.6 %copy-start.15 = (s32[1,1,32]{2,1,0:T(1,128)S(1)}, s32[1,1,32]{2,1,0:T(1,128)}, u32[]{:S(2)}) copy-start(s32[1,1,32]{2,1,0:T(1,128)} %param.30) | copy-start | bytes 388
  36.8 6.6 %copy-start.16 = (s32[1,1,32]{2,1,0:T(1,128)S(1)}, s32[1,1,32]{2,1,0:T(1,128)}, u32[]{:S(2)}) copy-start(s32[1,1,32]{2,1,0:T(1,128)} %param.29) | copy-start | bytes 388
  37.0 22.1 %copy-start = (bf16[4,144,1024]{2,1,0:T(8,128)(2,1)}, bf16[4,144,1024]{2,1,0:T(8,128)(2,1)S(1)}, u32[]{:S(2)}) copy-start(bf16[4,144,1024]{2,1,0:T(8,128)(2,1)S(1)} %pad_maximum_fusion.refs_0_) | copy-start | bytes 3538948
  37.0 16.8 %collective-permute-start.8 = (bf16[4,144,1024]{2,1,0:T(8,128)(2,1)S(1)}, bf16[4,144,1024]{2,1,0:T(8,128)(2,1)S(1)}, u32[]{:S(2)}, u32[]{:S(2)}) collective-permute-start(bf16[4,144,1024]{2,1,0:T(8,128)(2,1)S(1)} %pad_maximum_fusion.refs_0_), channel_id=1, source_target_pairs={{0,1},{1,2},{2,3},{3,0},{4,5},{5,6},{6,7},{7,4},{8,9},{9,10},{10,1... | collective-permute-start | bytes 3538952 | tf_op jit(solution)/shard_map/ppermute | solution.py:23
  38.3 20.2 %collective-permute-start.9 = (bf16[4,144,1024]{2,1,0:T(8,128)(2,1)S(1)}, bf16[4,144,1024]{2,1,0:T(8,128)(2,1)S(1)}, u32[]{:S(2)}, u32[]{:S(2)}) collective-permute-start(bf16[4,144,1024]{2,1,0:T(8,128)(2,1)S(1)} %pad_maximum_fusion.refs_0_), channel_id=1, source_target_pairs={{0,3},{1,0},{2,1},{3,2},{4,7},{5,4},{6,5},{7,6},{8,11},{9,8},{10,9... | collective-permute-start | bytes 3538952 | tf_op jit(solution)/shard_map/ppermute | solution.py:23
  40.5 18.6 %collective-permute-start.13 = (bf16[256,1024]{1,0:T(8,128)(2,1)S(1)}, bf16[256,1024]{1,0:T(8,128)(2,1)}, u32[]{:S(2)}, u32[]{:S(2)}) collective-permute-start(bf16[256,1024]{1,0:T(8,128)(2,1)S(1)} %copy-done.4), channel_id=1, source_target_pairs={{0,4},{1,5},{2,6},{3,7},{4,8},{5,9},{6,10},{7,11},{8,12},{9,13},{1... | collective-permute-start | bytes 1572872 | tf_op jit(solution)/shard_map/ppermute | solution.py:23
  43.3 22.8 %collective-permute-start.12 = (bf16[272,1024]{1,0:T(8,128)(2,1)S(1)}, bf16[272,1024]{1,0:T(8,128)(2,1)S(1)}, u32[]{:S(2)}, u32[]{:S(2)}) collective-permute-start(bf16[272,1024]{1,0:T(8,128)(2,1)S(1)} %collective-permute-done.3.refs_12_), channel_id=1, source_target_pairs={{0,4},{1,5},{2,6},{3,7},{4,8},{5,9},{6,10},{7,11},{8,12},{9,13},{1... | collective-permute-start | bytes 1671176 | tf_op jit(solution)/shard_map/ppermute | solution.py:23
  43.4 27.3 %copy-start.11 = (s32[1,128]{1,0:T(1,128)}, s32[1,128]{1,0:T(1,128)S(1)}, u32[]{:S(2)}) copy-start(s32[1,128]{1,0:T(1,128)S(1)} %add_bitcast_fusion.l0) | copy-start | bytes 1540
  43.4 4.0 %collective-permute-start = (s32[1,128]{1,0:T(1,128)S(1)}, s32[1,128]{1,0:T(1,128)S(1)}, u32[]{:S(2)}, u32[]{:S(2)}) collective-permute-start(s32[1,128]{1,0:T(1,128)S(1)} %add_bitcast_fusion.l0), channel_id=1, source_target_pairs={{0,1},{1,2},{2,3},{3,0},{4,5},{5,6},{6,7},{7,4},{8,9},{9,10},{10,1... | collective-permute-start | bytes 1544 | tf_op jit(solution)/shard_map/ppermute | solution.py:23
  47.4 11.6 %copy-start.12 = (s32[1,128]{1,0:T(1,128)}, s32[1,128]{1,0:T(1,128)S(1)}, u32[]{:S(2)}) copy-start(s32[1,128]{1,0:T(1,128)S(1)} %collective-permute-done.l1) | copy-start | bytes 1540
  47.4 15.2 %collective-permute-start.14 = (bf16[256,1024]{1,0:T(8,128)(2,1)S(1)}, bf16[256,1024]{1,0:T(8,128)(2,1)S(1)}, u32[]{:S(2)}, u32[]{:S(2)}) collective-permute-start(bf16[256,1024]{1,0:T(8,128)(2,1)S(1)} %copy-done.4), channel_id=1, source_target_pairs={{0,12},{1,13},{2,14},{3,15},{4,0},{5,1},{6,2},{7,3},{8,4},{9,5},{1... | collective-permute-start | bytes 1572872 | tf_op jit(solution)/shard_map/ppermute | solution.py:23
  53.8 8.9 %copy-start.1 = (bf16[4,144,1024]{2,1,0:T(8,128)(2,1)}, bf16[4,144,1024]{2,1,0:T(8,128)(2,1)S(1)}, u32[]{:S(2)}) copy-start(bf16[4,144,1024]{2,1,0:T(8,128)(2,1)S(1)} %collective-permute-done.8.refs_1_) | copy-start | bytes 3538948
  53.8 21.9 %collective-permute-start.15 = (bf16[4,144,1024]{2,1,0:T(8,128)(2,1)S(1)}, bf16[4,144,1024]{2,1,0:T(8,128)(2,1)S(1)}, u32[]{:S(2)}, u32[]{:S(2)}) collective-permute-start(bf16[4,144,1024]{2,1,0:T(8,128)(2,1)S(1)} %pad_maximum_fusion.refs_0_), channel_id=1, source_target_pairs={{0,16},{1,17},{2,18},{3,19},{4,20},{5,21},{6,22},{7,23},{8,24},{9,... | collective-permute-start | bytes 3538952 | tf_op jit(solution)/shard_map/ppermute | solution.py:23
  58.5 19.6 %copy-start.2 = (bf16[4,144,1024]{2,1,0:T(8,128)(2,1)}, bf16[4,144,1024]{2,1,0:T(8,128)(2,1)S(1)}, u32[]{:S(2)}) copy-start(bf16[4,144,1024]{2,1,0:T(8,128)(2,1)S(1)} %collective-permute-done.9.refs_2_) | copy-start | bytes 3538948
  58.5 10.4 %collective-permute-start.10 = (bf16[2,144,1024]{2,1,0:T(8,128)(2,1)S(1)}, bf16[2,144,1024]{2,1,0:T(8,128)(2,1)}, u32[]{:S(2)}, u32[]{:S(2)}) collective-permute-start(bf16[2,144,1024]{2,1,0:T(8,128)(2,1)S(1)} %slice.20), channel_id=1, source_target_pairs={{0,1},{1,2},{2,3},{3,0},{4,5},{5,6},{6,7},{7,4},{8,9},{9,10},{10,1... | collective-permute-start | bytes 1769480 | tf_op jit(solution)/shard_map/ppermute | solution.py:23
  59.1 11.6 %collective-permute-start.11 = (bf16[2,144,1024]{2,1,0:T(8,128)(2,1)S(1)}, bf16[2,144,1024]{2,1,0:T(8,128)(2,1)}, u32[]{:S(2)}, u32[]{:S(2)}) collective-permute-start(bf16[2,144,1024]{2,1,0:T(8,128)(2,1)S(1)} %slice.21), channel_id=1, source_target_pairs={{0,3},{1,0},{2,1},{3,2},{4,7},{5,4},{6,5},{7,6},{8,11},{9,8},{10,9... | collective-permute-start | bytes 1769480 | tf_op jit(solution)/shard_map/ppermute | solution.py:23
  62.6 14.9 %copy-start.9 = (bf16[256,1024]{1,0:T(8,128)(2,1)}, bf16[256,1024]{1,0:T(8,128)(2,1)S(1)}, u32[]{:S(2)}) copy-start(bf16[256,1024]{1,0:T(8,128)(2,1)S(1)} %collective-permute-done.14.refs_15_) | copy-start | bytes 1572868
  62.6 15.5 %collective-permute-start.16 = (bf16[4,144,1024]{2,1,0:T(8,128)(2,1)S(1)}, bf16[4,144,1024]{2,1,0:T(8,128)(2,1)}, u32[]{:S(2)}, u32[]{:S(2)}) collective-permute-start(bf16[4,144,1024]{2,1,0:T(8,128)(2,1)S(1)} %collective-permute-done.8.refs_1_), channel_id=1, source_target_pairs={{0,16},{1,17},{2,18},{3,19},{4,20},{5,21},{6,22},{7,23},{8,24},{9,... | collective-permute-start | bytes 3538952 | tf_op jit(solution)/shard_map/ppermute | solution.py:23
  66.1 11.4 %copy-start.5 = (bf16[272,1024]{1,0:T(8,128)(2,1)}, bf16[272,1024]{1,0:T(8,128)(2,1)S(1)}, u32[]{:S(2)}) copy-start(bf16[272,1024]{1,0:T(8,128)(2,1)S(1)} %collective-permute-done.12.refs_10_) | copy-start | bytes 1671172
  66.1 12.0 %collective-permute-start.17 = (bf16[4,144,1024]{2,1,0:T(8,128)(2,1)S(1)}, bf16[4,144,1024]{2,1,0:T(8,128)(2,1)}, u32[]{:S(2)}, u32[]{:S(2)}) collective-permute-start(bf16[4,144,1024]{2,1,0:T(8,128)(2,1)S(1)} %collective-permute-done.9.refs_2_), channel_id=1, source_target_pairs={{0,16},{1,17},{2,18},{3,19},{4,20},{5,21},{6,22},{7,23},{8,24},{9,... | collective-permute-start | bytes 3538952 | tf_op jit(solution)/shard_map/ppermute | solution.py:23
  69.0 2.5 %collective-permute-start.1 = (s32[1,128]{1,0:T(1,128)S(1)}, s32[1,128]{1,0:T(1,128)S(1)}, u32[]{:S(2)}, u32[]{:S(2)}) collective-permute-start(s32[1,128]{1,0:T(1,128)S(1)} %add_bitcast_fusion.l0), channel_id=1, source_target_pairs={{0,3},{1,0},{2,1},{3,2},{4,7},{5,4},{6,5},{7,6},{8,11},{9,8},{10,9... | collective-permute-start | bytes 1544 | tf_op jit(solution)/shard_map/ppermute | solution.py:23
  70.7 3.9 %collective-permute-start.2 = (s32[1,128]{1,0:T(1,128)S(1)}, s32[1,128]{1,0:T(1,128)S(1)}, u32[]{:S(2)}, u32[]{:S(2)}) collective-permute-start(s32[1,128]{1,0:T(1,128)S(1)} %add_bitcast_fusion.l0), channel_id=1, source_target_pairs={{0,2},{1,3},{2,0},{3,1},{4,6},{5,7},{6,4},{7,5},{8,10},{9,11},{10,... | collective-permute-start | bytes 1544 | tf_op jit(solution)/shard_map/ppermute | solution.py:23
  71.4 6.7 %copy-start.13 = (s32[1,128]{1,0:T(1,128)}, s32[1,128]{1,0:T(1,128)S(1)}, u32[]{:S(2)}) copy-start(s32[1,128]{1,0:T(1,128)S(1)} %collective-permute-done.1.l2) | copy-start | bytes 1540
  71.4 6.7 %collective-permute-start.18 = (bf16[2,144,1024]{2,1,0:T(8,128)(2,1)}, bf16[2,144,1024]{2,1,0:T(8,128)(2,1)}, u32[]{:S(2)}, u32[]{:S(2)}) collective-permute-start(bf16[2,144,1024]{2,1,0:T(8,128)(2,1)} %collective-permute-done.10.refs_3_), channel_id=1, source_target_pairs={{0,16},{1,17},{2,18},{3,19},{4,20},{5,21},{6,22},{7,23},{8,24},{9,... | collective-permute-start | bytes 1769480 | tf_op jit(solution)/shard_map/ppermute | solution.py:23
  74.6 3.6 %copy-start.14 = (s32[1,128]{1,0:T(1,128)}, s32[1,128]{1,0:T(1,128)S(1)}, u32[]{:S(2)}) copy-start(s32[1,128]{1,0:T(1,128)S(1)} %collective-permute-done.2.l3) | copy-start | bytes 1540
  74.6 3.5 %collective-permute-start.19 = (bf16[2,144,1024]{2,1,0:T(8,128)(2,1)}, bf16[2,144,1024]{2,1,0:T(8,128)(2,1)}, u32[]{:S(2)}, u32[]{:S(2)}) collective-permute-start(bf16[2,144,1024]{2,1,0:T(8,128)(2,1)} %collective-permute-done.11.refs_4_), channel_id=1, source_target_pairs={{0,16},{1,17},{2,18},{3,19},{4,20},{5,21},{6,22},{7,23},{8,24},{9,... | collective-permute-start | bytes 1769480 | tf_op jit(solution)/shard_map/ppermute | solution.py:23
  75.7 1.0 copy-start.3
  76.7 12.7 %collective-permute-start.20 = (bf16[256,1024]{1,0:T(8,128)(2,1)}, bf16[256,1024]{1,0:T(8,128)(2,1)S(1)}, u32[]{:S(2)}, u32[]{:S(2)}) collective-permute-start(bf16[256,1024]{1,0:T(8,128)(2,1)} %collective-permute-done.13.refs_13_), channel_id=1, source_target_pairs={{0,4},{1,5},{2,6},{3,7},{4,8},{5,9},{6,10},{7,11},{8,12},{9,13},{1... | collective-permute-start | bytes 1572872 | tf_op jit(solution)/shard_map/ppermute | solution.py:23
  89.5 0.8 copy-start.8

commit v3 on v2

--- a/solution.py
+++ b/solution.py
@@ -46,8 +46,8 @@
 def encode_kernel(n_cand, picks, weights, sub, *refs):
     refs = list(refs)
     if weights:
-        clen_ref, rlen_ref, cid_ref, rid_ref, tbl_ref = refs[:5]
-        refs = refs[5:]
+        clen_ref, rlen_ref, count_ref, cid_ref, rid_ref, pc_ref, pr_ref, tbl_ref = refs[:8]
+        refs = refs[8:]
     ch_ref = refs.pop(0) if n_cand else None
     rh_ref, up, upb, dn, dnb, gain, bias = refs[:7]
     refs = refs[7:]
@@ -60,7 +60,7 @@
         high, low = ids >> 7, ids & 127
         hot = (lax.broadcasted_iota(jnp.int32, (TABLE_ROWS, L), 0) == high).astype(jnp.bfloat16)
         rows = lax.dot_general(
-            tbl_ref[...], hot, (((0,), (0,)), ((), ())), preferred_element_type=jnp.float32
+            tbl_ref[...].astype(jnp.bfloat16), hot, (((0,), (0,)), ((), ())), preferred_element_type=jnp.float32
         )
         mine = lax.broadcasted_iota(jnp.int32, (128, L), 0) == low
         value = jnp.sum(jnp.where(mine, rows, 0.0), axis=0, keepdims=True)
@@ -78,7 +78,10 @@
             co_ref[L:, :] = jnp.zeros((16, D), jnp.bfloat16)
             ro_ref[len(picks) * L :, :] = jnp.zeros((16, D), jnp.bfloat16)
             w = token_weights(cid_ref[...], clen_ref[0])
-            co_ref[L:, 0:L] = jnp.where(row == 0, w, 0.0).astype(jnp.bfloat16)
+            count = jnp.full((1, 2 * SLOTS), count_ref[0], jnp.int32)
+            slots = jnp.concatenate([pc_ref[...], pr_ref[...], count], axis=1).astype(jnp.float32)
+            words = jnp.where(row == 0, w, jnp.where(row == 1, slots, 0.0))
+            co_ref[L:, 0:L] = words.astype(jnp.bfloat16)
             block = jnp.zeros((16, L), jnp.float32)
             for q in range(4):
                 block = jnp.where(row == q, token_weights(rid_ref[q : q + 1, :], rlen_ref[q]), block)
@@ -139,7 +142,7 @@
     return pl.pallas_call(
         functools.partial(encode_kernel, n_cand, picks, bool(words), sub),
         grid=(up.shape[1] // f,),
-        in_specs=[smem if k < 2 and words else full(a) for k, a in enumerate(first)]
+        in_specs=[smem if k < 3 and words else full(a) for k, a in enumerate(first)]
         + [
             pl.BlockSpec((D, f), lambda i: (0, i)),
             pl.BlockSpec((1, f), lambda i: (0, i)),
@@ -243,17 +246,33 @@
     return lax.fori_loop(0, (n + GROUP - 1) // GROUP, group, (acc, total))
 
 
-def early_kernel(pos_ref, l0, l1, l2, l3, *refs):
-    cands, refs_, (out_ref, later, cbuf, rbuf, wbuf, todo, sem) = refs[:10], refs[10:16], refs[16:]
+def early_kernel(pos_ref, *refs):
+    cands, refs_, refs = refs[:10], refs[10:16], refs[16:]
+    out_ref, later, cbuf, rbuf, wbuf, todo, lbuf, lint, lists, lsem, sem = refs
     y, core, x, z = pos_ref[0], pos_ref[1], pos_ref[2], pos_ref[3]
+
+    for own, places in ((0, ((0, 0), (1, 0), (2, 0), (3, 0))), (1, ((0, 0), (0, 1), (0, 3), (0, 2)))):
+        @pl.when(core == own)
+        def _(places=places):
+            for k, (buf, row) in enumerate(places):
+                words = cands[buf].at[row, pl.ds(L, 16), pl.ds(0, L)]
+                pltpu.make_async_copy(words, lbuf.at[k], lsem.at[k]).start()
+
+    for k in range(4):
+        words = cands[0].at[0, pl.ds(L, 16), pl.ds(0, L)]
+        pltpu.make_async_copy(words, lbuf.at[k], lsem.at[k]).wait()
+        lint[k : k + 1, :] = lbuf[k].astype(jnp.float32)[1:2, :].astype(jnp.int32)
+    move = pltpu.make_async_copy(lint, lists, lsem.at[0])
+    move.start()
+    move.wait()
     n = m = jnp.int32(0)
-    for lst, dz in ((l0, 0), (l1, 3), (l2, 1), (l3, 2)):
+    for k, dz in enumerate((0, 3, 1, 2)):
         zj = (z + dz) & 3
 
-        def scan(s, counts, lst=lst, dz=dz, zj=zj):
+        def scan(s, counts, k=k, dz=dz, zj=zj):
             n, m = counts
-            c = lst[0, s]
-            r = lst[0, SLOTS + s]
+            c = lists[k, s]
+            r = lists[k, SLOTS + s]
             mine = (r & 3) == z
             dx = (((r & 15) >> 2) - x) & 3
             late = mine & (dx == 2)
@@ -271,14 +290,14 @@
             back = jnp.where(core == 0, 3, 1)
             rs = jnp.where(dx == 0, 0, jnp.where(dx == 2, 3, jnp.where(dx == back, 1, 2)))
 
-            def put(where, k, rs):
-                where[0, k] = src
-                where[1, k] = row
-                where[2, k] = rs * 2 + (i >> 1)
-                where[3, k] = i & 1
-                where[4, k] = i
-                where[5, k] = zj
-                where[6, k] = s
+            def put(where, at, rs):
+                where[0, at] = src
+                where[1, at] = row
+                where[2, at] = rs * 2 + (i >> 1)
+                where[3, at] = i & 1
+                where[4, at] = i
+                where[5, at] = zj
+                where[6, at] = s
 
             @pl.when(soon)
             def _():
@@ -290,7 +309,7 @@
 
             return n + jnp.where(soon, 1, 0), m + jnp.where(late, 1, 0)
 
-        n, m = lax.fori_loop(0, lst[0, 2 * SLOTS], scan, (n, m))
+        n, m = lax.fori_loop(0, lists[k, 2 * SLOTS], scan, (n, m))
     later[7, 0] = m
     zero = jnp.zeros((8, L), jnp.float32)
     acc, total = score_listed(todo, n, zero, zero, cands, refs_, cbuf, rbuf, wbuf, sem)
@@ -298,12 +317,12 @@
     out_ref[1] = total
 
 
-def late_kernel(pos_ref, l0, todo, *refs):
+def late_kernel(pos_ref, count_ref, todo, *refs):
     cands, refs_, (part, out_ref, cbuf, rbuf, wbuf, sem) = refs[:10], refs[10:12], refs[12:]
     y, core, x = pos_ref[0], pos_ref[1], pos_ref[2]
     acc, total = score_listed(todo, todo[7, 0], part[0], part[1], cands, refs_, cbuf, rbuf, wbuf, sem)
     lane = lax.broadcasted_iota(jnp.int32, (1, L), 1)
-    count = l0[0, 2 * SLOTS].astype(jnp.float32)
+    count = count_ref[0].astype(jnp.float32)
     sums = jnp.where(
         lane == 96,
         total[0:1, :],
@@ -317,7 +336,14 @@
         out_ref[mine * 4 + q] = acc[q : q + 1, :] + sums
 
 
-def pair_call(kernel, name, smem_args, hbm_args, vmem_args, out_specs, out_shape, scratch):
+def finish_kernel(got_ref, scores_ref, totals_ref):
+    s = jnp.sum(got_ref[...], axis=0)
+    for k in range(3):
+        scores_ref[k, 0] = s[:, k * SLOTS : (k + 1) * SLOTS]
+    totals_ref[...] = s[:, 96:99] / s[:, 99:100]
+
+
+def pair_call(kernel, name, cost, smem_args, hbm_args, vmem_args, out_specs, out_shape, scratch):
     smem = pl.BlockSpec(memory_space=pltpu.SMEM)
     hbm = pl.BlockSpec(memory_space=pl.ANY)
     vmem = pl.BlockSpec(memory_space=pltpu.VMEM)
@@ -333,9 +359,9 @@
             *scratch,
             pltpu.SemaphoreType.DMA((3, 2 * GROUP)),
         ],
-        compiler_params=pltpu.CompilerParams(vmem_limit_bytes=60 << 20),
+        compiler_params=pltpu.CompilerParams(vmem_limit_bytes=12 << 20),
         cost_estimate=pl.CostEstimate(
-            flops=1 << 30, bytes_accessed=16 << 20, transcendentals=0
+            flops=cost << 10, bytes_accessed=cost, transcendentals=0
         ),
         name=name,
     )(*smem_args, *hbm_args, *vmem_args)
@@ -345,8 +371,10 @@
     cand_hidden, ref_hidden, cand_ids, ref_ids, cand_len, reference_length, idf_table, up_weight,
     up_bias, down_weight, down_bias, norm_gain, norm_bias, pair_cand, pair_ref, pair_count,
 ):
-    table = jnp.pad(idf_table, (0, TABLE_ROWS * 128 - idf_table.shape[0]))
-    table = table.reshape(TABLE_ROWS, 128).astype(jnp.bfloat16)
+    table = jnp.pad(idf_table, (0, TABLE_ROWS * 128 - idf_table.shape[0])).reshape(TABLE_ROWS, 128)
+    count = pair_count.reshape(1)
+    dp, prompt = lax.axis_index("dp"), lax.axis_index("prompt")
+    pos = jnp.stack([dp >> 1, dp & 1, prompt >> 2, prompt & 3]).astype(jnp.int32)
     layer = (
         up_weight,
         up_bias.reshape(1, -1),
@@ -359,8 +387,11 @@
     words = (
         cand_len.reshape(1),
         reference_length.reshape(4),
+        count,
         cand_ids.reshape(1, L),
         ref_ids.reshape(4, L),
+        pair_cand.reshape(1, SLOTS),
+        pair_ref.reshape(1, SLOTS),
         table,
     )
     cand, refs_a = encode((0, 1), cand_hidden.reshape(1, L, D), hidden, words, layer)
@@ -370,8 +401,8 @@
     c3 = send(cand, along_first(-1))
     c2 = send(cand, along_first(2))
     (refs_b,) = encode((2, 3), None, hidden, (), layer)
-    back_a, ahead_a, c1, c2, c3, refs_b = lax.optimization_barrier(
-        (back_a, ahead_a, c1, c2, c3, refs_b)
+    back_a, ahead_a, c1, c2, c3, refs_b, pos = lax.optimization_barrier(
+        (back_a, ahead_a, c1, c2, c3, refs_b, pos)
     )
     back_b = send(refs_b, along_x(1))
     ahead_b = send(refs_b, along_x(-1))
@@ -385,20 +416,11 @@
     far_b = send(back_b, along_x(1))
     others = [send(v, to_other_core) for v in (own4, d1, d2, d3, d4)]
     cands = [own4, d1, d2, d3, d4, *others]
-    slots = jnp.concatenate(
-        [
-            pair_cand.reshape(-1),
-            pair_ref.reshape(-1),
-            jnp.broadcast_to(pair_count.reshape(1), (2 * SLOTS,)),
-        ]
-    ).reshape(1, 4 * SLOTS)
-    lists = [slots] + [send(slots, along_z(k)) for k in (1, -1, 2)]
-    dp, prompt = lax.axis_index("dp"), lax.axis_index("prompt")
-    pos = jnp.stack([dp >> 1, dp & 1, prompt >> 2, prompt & 3]).astype(jnp.int32)
     part, later = pair_call(
         early_kernel,
         "score_early",
-        [pos, *lists],
+        1 << 10,
+        [pos],
         [*cands, refs_a, refs_b, back_a, back_b, ahead_a, ahead_b],
         [],
         [pl.BlockSpec(memory_space=pltpu.VMEM), pl.BlockSpec(memory_space=pltpu.SMEM)],
@@ -406,21 +428,35 @@
             jax.ShapeDtypeStruct((2, 8, L), jnp.float32),
             jax.ShapeDtypeStruct((8, 4 * SLOTS), jnp.int32),
         ],
-        [pltpu.SMEM((8, 4 * SLOTS), jnp.int32)],
+        [
+            pltpu.SMEM((8, 4 * SLOTS), jnp.int32),
+            pltpu.VMEM((4, 16, L), jnp.bfloat16),
+            pltpu.VMEM((8, L), jnp.int32),
+            pltpu.SMEM((8, L), jnp.int32),
+            pltpu.SemaphoreType.DMA((4,)),
+        ],
     )
     payload = pair_call(
         late_kernel,
         "score_late",
-        [pos, slots, later],
+        1 << 20,
+        [pos, count, later],
         [*cands, far_a, far_b],
         [part],
         pl.BlockSpec(memory_space=pltpu.VMEM),
         jax.ShapeDtypeStruct((128, 1, L), jnp.float32),
         [],
     )
-    got = jnp.sum(lax.all_to_all(payload, AXES, 0, 0), axis=0)
-    scores = got[:, : 3 * SLOTS].reshape(3, 1, 1, SLOTS)
-    return scores, got[0, 96:99] / got[0, 99]
+    got = lax.all_to_all(payload, AXES, 0, 0)
+    scores, totals = pl.pallas_call(
+        finish_kernel,
+        out_shape=[
+            jax.ShapeDtypeStruct((3, 1, 1, SLOTS), jnp.float32),
+            jax.ShapeDtypeStruct((1, 3), jnp.float32),
+        ],
+        name="finish",
+    )(got)
+    return scores, totals.reshape(3)
 
 
 def solution(mesh):

time: 114 us -> 111 us (0.974)
  waiting for transfers between devices: 14.1 us -> 19.8 us
  starting transfers between devices: 33.5 us -> 28.6 us
  local copies, waits for them, and re-layouts: 4.71 us -> 1.72 us
  other arithmetic: 3.14 us -> 0.23 us
  blocking collectives: 16.8 us -> 19.2 us
    ppermute x21 -> x18, waiting for transfers between devices: 14.1 us -> 19.8 us  [send(): lax.ppermute(value, AXES, [(number(*a), number(*where(*a))) for a in GRID])]
    ppermute x21 -> x18, starting transfers between devices: 33.5 us -> 28.6 us  [send(): lax.ppermute(value, AXES, [(number(*a), number(*where(*a))) for a in GRID])]
    unnamed x34 -> x6, local copies, waits for them, and re-layouts: 2.72 us -> 0.01 us
    all_to_all x1, blocking collectives: 16.8 us -> 19.2 us  [on_device(): got = lax.all_to_all(payload, AXES, 0, 0)]
    pallas_call x0 -> x1, Pallas kernels: none -> 1.63 us  [on_device(): pl.pallas_call(finish_kernel, out_shape=[jax.ShapeDtypeStruct((3, 1, 1, S...]
    div x1 -> x0, other arithmetic: 1.23 us -> none  [on_device(): return (scores, got[0, 96:99] / got[0, 99])]
  transfers between devices with their start and end apart: 21 -> 18, of which waited for: 6 -> 6; matrix products, arithmetic and copies ran while one was open for 1% -> 0% of each run, Pallas kernels for 19% -> 19%
where the time goes in v3:
time: 111 us; the launch traced here: 112 us
  Pallas kernels  40 us (36%)
  starting transfers between devices  28.6 us (26%)
  waiting for transfers between devices  19.8 us (18%)
  blocking collectives  19.2 us (17%)
  between operations  2.05 us (2%)
  local copies, waits for them, and re-layouts  1.72 us (2%)
    ppermute x18, starting transfers between devices, send(): lax.ppermute(value, AXES, [(number(*a), number(*where(*a))) for a in GRID])  28.6 us
    pallas_call x2, Pallas kernels, encode(): pl.pallas_call(functools.partial(encode_kernel, n_cand, picks, bool(words...  24.1 us
    ppermute x18, waiting for transfers between devices, send(): lax.ppermute(value, AXES, [(number(*a), number(*where(*a))) for a in GRID])  19.8 us
    all_to_all x1, blocking collectives, on_device(): got = lax.all_to_all(payload, AXES, 0, 0)  19.2 us
    pallas_call x2, Pallas kernels, pair_call(): pl.pallas_call(kernel, in_specs=[smem] * len(smem_args) + [hbm] * len(hbm...  14.3 us
  transfers between devices with their start and end apart: 18, of which 6 were waited for; matrix products, arithmetic and copies ran while one was open for 0% of the time, Pallas kernels for 19%

profile of v3, /device:TPU:1, one launch (start us, length us, event | category | flops | bytes accessed | tf_op | source)
XLA Modules:
  0.0 111.5 jit_solution(9836229760344407137)
XLA Ops:
  1.3 1.6 %pad_bitcast_fusion.refs_7_ = f32[400,128]{1,0:T(8,128)} fusion(f32[50265]{0:T(1024)} %param.22), kind=kLoop, calls=%fused_computation.1 | loop fusion | bytes 405860 | tf_op jit(solution)/shard_map/reshape | solution.py:374
  3.6 13.3 %encode.2 = (bf16[144,1024]{1,0:T(8,128)(2,1)}, bf16[272,1024]{1,0:T(8,128)(2,1)}) custom-call(s32[1]{0:T(128)} %bitcast.24.refs_0_, s32[4]{0:T(128)} %bitcast.43, s32[1]{0:T(128)} %bitcast.25.refs_2_, s32[1,128]{1,0:T(1,128)} %bitcast.44, s32[4,128]{1,0:T(4,128)} %bitcast.42, s32[1,32]{1,0:T(1,128)} %bitcast.45, s32[1,32]{1,0:T(1,128)} %bitcast.46, ...), custom_call_target="tpu_custom_call" | custom-call | flops 6442450944 | bytes 17825792 | tf_op jit(solution)/shard_map/encode/pallas_call | solution.py:142
  16.8 3.3 %collective-permute-start = (bf16[272,1024]{1,0:T(8,128)(2,1)}, bf16[272,1024]{1,0:T(8,128)(2,1)S(1)}, u32[]{:S(2)}, u32[]{:S(2)}) collective-permute-start(bf16[272,1024]{1,0:T(8,128)(2,1)} %get-tuple-element.20.refs_10_), channel_id=1, source_target_pairs={{0,4},{1,5},{2,6},{3,7},{4,8},{5,9},{6,10},{7,11},{8,12},{9,13},{1... | collective-permute-start | bytes 1671176 | tf_op jit(solution)/shard_map/ppermute | solution.py:23
  20.1 0.0 collective-permute-start.1
  20.1 1.6 %collective-permute-start.2 = (bf16[144,1024]{1,0:T(8,128)(2,1)}, bf16[144,1024]{1,0:T(8,128)(2,1)S(1)}, u32[]{:S(2)}, u32[]{:S(2)}) collective-permute-start(bf16[144,1024]{1,0:T(8,128)(2,1)} %get-tuple-element.21), channel_id=1, source_target_pairs={{0,32},{1,33},{2,34},{3,35},{4,36},{5,37},{6,38},{7,39},{8,40},{9,... | collective-permute-start | bytes 884744 | tf_op jit(solution)/shard_map/ppermute | solution.py:23
  21.8 3.3 %collective-permute-start.3 = (bf16[144,1024]{1,0:T(8,128)(2,1)}, bf16[144,1024]{1,0:T(8,128)(2,1)S(1)}, u32[]{:S(2)}, u32[]{:S(2)}) collective-permute-start(bf16[144,1024]{1,0:T(8,128)(2,1)} %get-tuple-element.21), channel_id=1, source_target_pairs={{0,64},{1,65},{2,66},{3,67},{4,68},{5,69},{6,70},{7,71},{8,72},{9,... | collective-permute-start | bytes 884744 | tf_op jit(solution)/shard_map/ppermute | solution.py:23
  25.1 0.7 collective-permute-start.4
  25.8 0.1 pad_add_fusion.pos_ref
  25.9 0.0 copy-start.2
  25.9 10.8 %encode.3.refs_11_ = bf16[256,1024]{1,0:T(8,128)(2,1)} custom-call(bf16[4,128,1024]{2,1,0:T(8,128)(2,1)} %bitcast.28, bf16[1024,4096]{1,0:T(8,128)(2,1)} %refs_1_.1, f32[1,4096]{1,0:T(1,128)} %bitcast.34, bf16[4096,1024]{1,0:T(8,128)(2,1)} %refs_3_.1, f32[1,1024]{1,0:T(1,128)} %bitcast.36, f32[1,1024]{1,0:T(1,128)} %bitcast.38, f32[1,1024]{1,0:T(1,128)} %bitcast.40), custom_call_target="tpu_custom_call" | custom-call | flops 4294967296 | bytes 17825792 | tf_op jit(solution)/shard_map/encode/pallas_call | solution.py:142
  36.7 0.0 collective-permute-done.2
  36.7 0.0 collective-permute-done.3
  36.7 0.0 collective-permute-done.4
  36.7 0.0 collective-permute-done.refs_12_
  36.7 0.0 collective-permute-done.1.refs_14_
  36.7 0.0 copy-done.2
  36.7 0.0 copy-start
  36.7 0.2 pad_maximum_fusion.refs_0_
  36.9 0.0 copy-start.1
  36.9 1.4 %collective-permute-start.5 = (bf16[4,144,1024]{2,1,0:T(8,128)(2,1)S(1)}, bf16[4,144,1024]{2,1,0:T(8,128)(2,1)S(1)}, u32[]{:S(2)}, u32[]{:S(2)}) collective-permute-start(bf16[4,144,1024]{2,1,0:T(8,128)(2,1)S(1)} %pad_maximum_fusion.refs_0_), channel_id=1, source_target_pairs={{0,1},{1,2},{2,3},{3,0},{4,5},{5,6},{6,7},{7,4},{8,9},{9,10},{10,1... | collective-permute-start | bytes 3538952 | tf_op jit(solution)/shard_map/ppermute | solution.py:23
  38.3 1.5 %collective-permute-start.6 = (bf16[4,144,1024]{2,1,0:T(8,128)(2,1)S(1)}, bf16[4,144,1024]{2,1,0:T(8,128)(2,1)S(1)}, u32[]{:S(2)}, u32[]{:S(2)}) collective-permute-start(bf16[4,144,1024]{2,1,0:T(8,128)(2,1)S(1)} %pad_maximum_fusion.refs_0_), channel_id=1, source_target_pairs={{0,3},{1,0},{2,1},{3,2},{4,7},{5,4},{6,5},{7,6},{8,11},{9,8},{10,9... | collective-permute-start | bytes 3538952 | tf_op jit(solution)/shard_map/ppermute | solution.py:23
  39.8 2.7 %collective-permute-start.9 = (bf16[272,1024]{1,0:T(8,128)(2,1)S(1)}, bf16[272,1024]{1,0:T(8,128)(2,1)S(1)}, u32[]{:S(2)}, u32[]{:S(2)}) collective-permute-start(bf16[272,1024]{1,0:T(8,128)(2,1)S(1)} %collective-permute-done.refs_12_), channel_id=1, source_target_pairs={{0,4},{1,5},{2,6},{3,7},{4,8},{5,9},{6,10},{7,11},{8,12},{9,13},{1... | collective-permute-start | bytes 1671176 | tf_op jit(solution)/shard_map/ppermute | solution.py:23
  42.5 0.0 copy-done
  42.5 0.0 collective-permute-start.10
  42.5 1.4 %collective-permute-start.11 = (bf16[256,1024]{1,0:T(8,128)(2,1)S(1)}, bf16[256,1024]{1,0:T(8,128)(2,1)S(1)}, u32[]{:S(2)}, u32[]{:S(2)}) collective-permute-start(bf16[256,1024]{1,0:T(8,128)(2,1)S(1)} %copy-done), channel_id=1, source_target_pairs={{0,12},{1,13},{2,14},{3,15},{4,0},{5,1},{6,2},{7,3},{8,4},{9,5},{1... | collective-permute-start | bytes 1572872 | tf_op jit(solution)/shard_map/ppermute | solution.py:23
  43.9 9.7 %collective-permute-done.5.refs_1_ = bf16[4,144,1024]{2,1,0:T(8,128)(2,1)S(1)} collective-permute-done((bf16[4,144,1024]{2,1,0:T(8,128)(2,1)S(1)}, bf16[4,144,1024]{2,1,0:T(8,128)(2,1)S(1)}, u32[]{:S(2)}, u32[]{:S(2)}) %collective-permute-start.5) | collective-permute-done | bytes 1179680 | tf_op jit(solution)/shard_map/ppermute | solution.py:23
  53.6 3.2 %collective-permute-start.12 = (bf16[4,144,1024]{2,1,0:T(8,128)(2,1)S(1)}, bf16[4,144,1024]{2,1,0:T(8,128)(2,1)S(1)}, u32[]{:S(2)}, u32[]{:S(2)}) collective-permute-start(bf16[4,144,1024]{2,1,0:T(8,128)(2,1)S(1)} %pad_maximum_fusion.refs_0_), channel_id=1, source_target_pairs={{0,16},{1,17},{2,18},{3,19},{4,20},{5,21},{6,22},{7,23},{8,24},{9,... | collective-permute-start | bytes 3538952 | tf_op jit(solution)/shard_map/ppermute | solution.py:23
  56.8 0.0 collective-permute-done.6.refs_2_
  56.8 0.5 collective-permute-start.7
  57.3 2.8 %collective-permute-done.10.refs_13_ = bf16[256,1024]{1,0:T(8,128)(2,1)S(1)} collective-permute-done((bf16[256,1024]{1,0:T(8,128)(2,1)S(1)}, bf16[256,1024]{1,0:T(8,128)(2,1)S(1)}, u32[]{:S(2)}, u32[]{:S(2)}) %collective-permute-start.10) | collective-permute-done | bytes 524320 | tf_op jit(solution)/shard_map/ppermute | solution.py:23
  60.2 1.4 %collective-permute-start.8 = (bf16[2,144,1024]{2,1,0:T(8,128)(2,1)S(1)}, bf16[2,144,1024]{2,1,0:T(8,128)(2,1)S(1)}, u32[]{:S(2)}, u32[]{:S(2)}) collective-permute-start(bf16[2,144,1024]{2,1,0:T(8,128)(2,1)S(1)} %slice.9), channel_id=1, source_target_pairs={{0,3},{1,0},{2,1},{3,2},{4,7},{5,4},{6,5},{7,6},{8,11},{9,8},{10,9... | collective-permute-start | bytes 1769480 | tf_op jit(solution)/shard_map/ppermute | solution.py:23
  61.6 0.0 collective-permute-done.11.refs_15_
  61.6 2.7 %collective-permute-start.13 = (bf16[4,144,1024]{2,1,0:T(8,128)(2,1)S(1)}, bf16[4,144,1024]{2,1,0:T(8,128)(2,1)S(1)}, u32[]{:S(2)}, u32[]{:S(2)}) collective-permute-start(bf16[4,144,1024]{2,1,0:T(8,128)(2,1)S(1)} %collective-permute-done.5.refs_1_), channel_id=1, source_target_pairs={{0,16},{1,17},{2,18},{3,19},{4,20},{5,21},{6,22},{7,23},{8,24},{9,... | collective-permute-start | bytes 3538952 | tf_op jit(solution)/shard_map/ppermute | solution.py:23
  64.3 0.0 collective-permute-done.9.refs_10_
  64.3 0.1 collective-permute-start.14
  64.4 2.8 %collective-permute-done.7.refs_3_ = bf16[2,144,1024]{2,1,0:T(8,128)(2,1)S(1)} collective-permute-done((bf16[2,144,1024]{2,1,0:T(8,128)(2,1)S(1)}, bf16[2,144,1024]{2,1,0:T(8,128)(2,1)S(1)}, u32[]{:S(2)}, u32[]{:S(2)}) %collective-permute-start.7) | collective-permute-done | bytes 589856 | tf_op jit(solution)/shard_map/ppermute | solution.py:23
  67.1 2.1 %collective-permute-done.8.refs_4_ = bf16[2,144,1024]{2,1,0:T(8,128)(2,1)S(1)} collective-permute-done((bf16[2,144,1024]{2,1,0:T(8,128)(2,1)S(1)}, bf16[2,144,1024]{2,1,0:T(8,128)(2,1)S(1)}, u32[]{:S(2)}, u32[]{:S(2)}) %collective-permute-start.8) | collective-permute-done | bytes 589856 | tf_op jit(solution)/shard_map/ppermute | solution.py:23
  69.2 4.7 %collective-permute-start.15 = (bf16[2,144,1024]{2,1,0:T(8,128)(2,1)S(1)}, bf16[2,144,1024]{2,1,0:T(8,128)(2,1)S(1)}, u32[]{:S(2)}, u32[]{:S(2)}) collective-permute-start(bf16[2,144,1024]{2,1,0:T(8,128)(2,1)S(1)} %collective-permute-done.7.refs_3_), channel_id=1, source_target_pairs={{0,16},{1,17},{2,18},{3,19},{4,20},{5,21},{6,22},{7,23},{8,24},{9,... | collective-permute-start | bytes 1769480 | tf_op jit(solution)/shard_map/ppermute | solution.py:23
  73.9 0.0 collective-permute-start.16
  73.9 0.0 collective-permute-done.12.refs_5_
  73.9 0.0 collective-permute-start.17
  73.9 1.6 %collective-permute-done.15.refs_8_ = bf16[2,144,1024]{2,1,0:T(8,128)(2,1)S(1)} collective-permute-done((bf16[2,144,1024]{2,1,0:T(8,128)(2,1)S(1)}, bf16[2,144,1024]{2,1,0:T(8,128)(2,1)S(1)}, u32[]{:S(2)}, u32[]{:S(2)}) %collective-permute-start.15) | collective-permute-done | bytes 589856 | tf_op jit(solution)/shard_map/ppermute | solution.py:23
  75.5 0.8 collective-permute-done.16.refs_9_
  76.4 0.0 collective-permute-done.13.refs_6_
  76.4 0.0 collective-permute-done.14.refs_7_
  76.4 0.0 copy-done.1
  76.4 10.9 %score_early.1 = (f32[2,8,128]{2,1,0:T(8,128)S(1)}, s32[8,128]{1,0:T(8,128)S(1)}) custom-call(s32[4]{0:T(128)S(1)} %pad_add_fusion.pos_ref, bf16[4,144,1024]{2,1,0:T(8,128)(2,1)S(1)} %pad_maximum_fusion.refs_0_, bf16[4,144,1024]{2,1,0:T(8,128)(2,1)S(1)} %collective-permute-done.5.refs_1_, bf16[4,144,1024]{2,1,0:T(8,128)(2,1)S(1)} %collective-permute-done.6.refs_2_, ...), custom_call_target="tpu_custom_call" | custom-call | flops 1048576 | bytes 1024 | tf_op jit(solution)/shard_map/score_early/pallas_call | solution.py:350
  87.3 0.0 collective-permute-done.17.refs_11_
  87.3 3.3 %score_late.1 = f32[128,1,128]{2,1,0:T(1,128)S(1)} custom-call(s32[4]{0:T(128)S(1)} %pad_add_fusion.pos_ref, s32[1]{0:T(128)} %bitcast.26.count_ref, s32[8,128]{1,0:T(8,128)S(1)} %get-tuple-element.33.todo, bf16[4,144,1024]{2,1,0:T(8,128)(2,1)S(1)} %pad_maximum_fusion.refs_0_, bf16[4,144,1024]{2,1,0:T(8,128)(2,1)S(1)} %collective-permute-done.5.refs_1_, ...), custom_call_target="tpu_custom_call" | custom-call | flops 1073741824 | bytes 1048576 | tf_op jit(solution)/shard_map/score_late/pallas_call | solution.py:350
  90.7 19.2 %all_to_all.5.got_ref = f32[128,1,128]{2,1,0:T(1,128)} all-to-all(f32[128,1,128]{2,1,0:T(1,128)S(1)} %score_late.1), channel_id=1, replica_groups=mesh['dp'=8,'prompt'=16] {'dp','prompt'}, dimensions={0} | all-to-all | bytes 131072 | tf_op jit(solution)/shard_map/all_to_all | solution.py:450
  109.9 1.6 %finish.1 = (f32[3,1,1,32]{3,2,1,0:T(1,128)}, f32[1,3]{1,0:T(1,128)}) custom-call(f32[128,1,128]{2,1,0:T(1,128)} %all_to_all.5.got_ref), custom_call_target="tpu_custom_call" | custom-call | tf_op jit(solution)/shard_map/finish/pallas_call | solution.py:451
  (2 shorter events, 0.1 us)
Async XLA Ops:
  16.8 19.9 %collective-permute-start = (bf16[272,1024]{1,0:T(8,128)(2,1)}, bf16[272,1024]{1,0:T(8,128)(2,1)S(1)}, u32[]{:S(2)}, u32[]{:S(2)}) collective-permute-start(bf16[272,1024]{1,0:T(8,128)(2,1)} %get-tuple-element.20.refs_10_), channel_id=1, source_target_pairs={{0,4},{1,5},{2,6},{3,7},{4,8},{5,9},{6,10},{7,11},{8,12},{9,13},{1... | collective-permute-start | bytes 1671176 | tf_op jit(solution)/shard_map/ppermute | solution.py:23
  20.1 16.6 %collective-permute-start.1 = (bf16[272,1024]{1,0:T(8,128)(2,1)}, bf16[272,1024]{1,0:T(8,128)(2,1)S(1)}, u32[]{:S(2)}, u32[]{:S(2)}) collective-permute-start(bf16[272,1024]{1,0:T(8,128)(2,1)} %get-tuple-element.20.refs_10_), channel_id=1, source_target_pairs={{0,12},{1,13},{2,14},{3,15},{4,0},{5,1},{6,2},{7,3},{8,4},{9,5},{1... | collective-permute-start | bytes 1671176 | tf_op jit(solution)/shard_map/ppermute | solution.py:23
  20.1 16.5 %collective-permute-start.2 = (bf16[144,1024]{1,0:T(8,128)(2,1)}, bf16[144,1024]{1,0:T(8,128)(2,1)S(1)}, u32[]{:S(2)}, u32[]{:S(2)}) collective-permute-start(bf16[144,1024]{1,0:T(8,128)(2,1)} %get-tuple-element.21), channel_id=1, source_target_pairs={{0,32},{1,33},{2,34},{3,35},{4,36},{5,37},{6,38},{7,39},{8,40},{9,... | collective-permute-start | bytes 884744 | tf_op jit(solution)/shard_map/ppermute | solution.py:23
  21.8 14.9 %collective-permute-start.3 = (bf16[144,1024]{1,0:T(8,128)(2,1)}, bf16[144,1024]{1,0:T(8,128)(2,1)S(1)}, u32[]{:S(2)}, u32[]{:S(2)}) collective-permute-start(bf16[144,1024]{1,0:T(8,128)(2,1)} %get-tuple-element.21), channel_id=1, source_target_pairs={{0,64},{1,65},{2,66},{3,67},{4,68},{5,69},{6,70},{7,71},{8,72},{9,... | collective-permute-start | bytes 884744 | tf_op jit(solution)/shard_map/ppermute | solution.py:23
  25.1 11.6 %collective-permute-start.4 = (bf16[144,1024]{1,0:T(8,128)(2,1)}, bf16[144,1024]{1,0:T(8,128)(2,1)S(1)}, u32[]{:S(2)}, u32[]{:S(2)}) collective-permute-start(bf16[144,1024]{1,0:T(8,128)(2,1)} %get-tuple-element.21), channel_id=1, source_target_pairs={{0,96},{1,97},{2,98},{3,99},{4,100},{5,101},{6,102},{7,103},{8,104... | collective-permute-start | bytes 884744 | tf_op jit(solution)/shard_map/ppermute | solution.py:23
  25.9 10.8 %copy-start.2 = (bf16[144,1024]{1,0:T(8,128)(2,1)S(1)}, bf16[144,1024]{1,0:T(8,128)(2,1)}, u32[]{:S(2)}) copy-start(bf16[144,1024]{1,0:T(8,128)(2,1)} %get-tuple-element.21) | copy-start | bytes 884740
  36.7 5.7 %copy-start = (bf16[256,1024]{1,0:T(8,128)(2,1)S(1)}, bf16[256,1024]{1,0:T(8,128)(2,1)}, u32[]{:S(2)}) copy-start(bf16[256,1024]{1,0:T(8,128)(2,1)} %encode.3.refs_11_) | copy-start | bytes 1572868
  36.9 39.5 %copy-start.1 = (bf16[272,1024]{1,0:T(8,128)(2,1)S(1)}, bf16[272,1024]{1,0:T(8,128)(2,1)}, u32[]{:S(2)}) copy-start(bf16[272,1024]{1,0:T(8,128)(2,1)} %get-tuple-element.20.refs_10_) | copy-start | bytes 1671172
  36.9 16.7 %collective-permute-start.5 = (bf16[4,144,1024]{2,1,0:T(8,128)(2,1)S(1)}, bf16[4,144,1024]{2,1,0:T(8,128)(2,1)S(1)}, u32[]{:S(2)}, u32[]{:S(2)}) collective-permute-start(bf16[4,144,1024]{2,1,0:T(8,128)(2,1)S(1)} %pad_maximum_fusion.refs_0_), channel_id=1, source_target_pairs={{0,1},{1,2},{2,3},{3,0},{4,5},{5,6},{6,7},{7,4},{8,9},{9,10},{10,1... | collective-permute-start | bytes 3538952 | tf_op jit(solution)/shard_map/ppermute | solution.py:23
  38.3 18.6 %collective-permute-start.6 = (bf16[4,144,1024]{2,1,0:T(8,128)(2,1)S(1)}, bf16[4,144,1024]{2,1,0:T(8,128)(2,1)S(1)}, u32[]{:S(2)}, u32[]{:S(2)}) collective-permute-start(bf16[4,144,1024]{2,1,0:T(8,128)(2,1)S(1)} %pad_maximum_fusion.refs_0_), channel_id=1, source_target_pairs={{0,3},{1,0},{2,1},{3,2},{4,7},{5,4},{6,5},{7,6},{8,11},{9,8},{10,9... | collective-permute-start | bytes 3538952 | tf_op jit(solution)/shard_map/ppermute | solution.py:23
  39.8 24.5 %collective-permute-start.9 = (bf16[272,1024]{1,0:T(8,128)(2,1)S(1)}, bf16[272,1024]{1,0:T(8,128)(2,1)S(1)}, u32[]{:S(2)}, u32[]{:S(2)}) collective-permute-start(bf16[272,1024]{1,0:T(8,128)(2,1)S(1)} %collective-permute-done.refs_12_), channel_id=1, source_target_pairs={{0,4},{1,5},{2,6},{3,7},{4,8},{5,9},{6,10},{7,11},{8,12},{9,13},{1... | collective-permute-start | bytes 1671176 | tf_op jit(solution)/shard_map/ppermute | solution.py:23
  42.5 17.7 %collective-permute-start.10 = (bf16[256,1024]{1,0:T(8,128)(2,1)S(1)}, bf16[256,1024]{1,0:T(8,128)(2,1)S(1)}, u32[]{:S(2)}, u32[]{:S(2)}) collective-permute-start(bf16[256,1024]{1,0:T(8,128)(2,1)S(1)} %copy-done), channel_id=1, source_target_pairs={{0,4},{1,5},{2,6},{3,7},{4,8},{5,9},{6,10},{7,11},{8,12},{9,13},{1... | collective-permute-start | bytes 1572872 | tf_op jit(solution)/shard_map/ppermute | solution.py:23
  42.5 19.1 %collective-permute-start.11 = (bf16[256,1024]{1,0:T(8,128)(2,1)S(1)}, bf16[256,1024]{1,0:T(8,128)(2,1)S(1)}, u32[]{:S(2)}, u32[]{:S(2)}) collective-permute-start(bf16[256,1024]{1,0:T(8,128)(2,1)S(1)} %copy-done), channel_id=1, source_target_pairs={{0,12},{1,13},{2,14},{3,15},{4,0},{5,1},{6,2},{7,3},{8,4},{9,5},{1... | collective-permute-start | bytes 1572872 | tf_op jit(solution)/shard_map/ppermute | solution.py:23
  53.6 20.3 %collective-permute-start.12 = (bf16[4,144,1024]{2,1,0:T(8,128)(2,1)S(1)}, bf16[4,144,1024]{2,1,0:T(8,128)(2,1)S(1)}, u32[]{:S(2)}, u32[]{:S(2)}) collective-permute-start(bf16[4,144,1024]{2,1,0:T(8,128)(2,1)S(1)} %pad_maximum_fusion.refs_0_), channel_id=1, source_target_pairs={{0,16},{1,17},{2,18},{3,19},{4,20},{5,21},{6,22},{7,23},{8,24},{9,... | collective-permute-start | bytes 3538952 | tf_op jit(solution)/shard_map/ppermute | solution.py:23
  56.8 10.3 %collective-permute-start.7 = (bf16[2,144,1024]{2,1,0:T(8,128)(2,1)S(1)}, bf16[2,144,1024]{2,1,0:T(8,128)(2,1)S(1)}, u32[]{:S(2)}, u32[]{:S(2)}) collective-permute-start(bf16[2,144,1024]{2,1,0:T(8,128)(2,1)S(1)} %slice.8), channel_id=1, source_target_pairs={{0,1},{1,2},{2,3},{3,0},{4,5},{5,6},{6,7},{7,4},{8,9},{9,10},{10,1... | collective-permute-start | bytes 1769480 | tf_op jit(solution)/shard_map/ppermute | solution.py:23
  60.2 9.0 %collective-permute-start.8 = (bf16[2,144,1024]{2,1,0:T(8,128)(2,1)S(1)}, bf16[2,144,1024]{2,1,0:T(8,128)(2,1)S(1)}, u32[]{:S(2)}, u32[]{:S(2)}) collective-permute-start(bf16[2,144,1024]{2,1,0:T(8,128)(2,1)S(1)} %slice.9), channel_id=1, source_target_pairs={{0,3},{1,0},{2,1},{3,2},{4,7},{5,4},{6,5},{7,6},{8,11},{9,8},{10,9... | collective-permute-start | bytes 1769480 | tf_op jit(solution)/shard_map/ppermute | solution.py:23
  61.6 14.8 %collective-permute-start.13 = (bf16[4,144,1024]{2,1,0:T(8,128)(2,1)S(1)}, bf16[4,144,1024]{2,1,0:T(8,128)(2,1)S(1)}, u32[]{:S(2)}, u32[]{:S(2)}) collective-permute-start(bf16[4,144,1024]{2,1,0:T(8,128)(2,1)S(1)} %collective-permute-done.5.refs_1_), channel_id=1, source_target_pairs={{0,16},{1,17},{2,18},{3,19},{4,20},{5,21},{6,22},{7,23},{8,24},{9,... | collective-permute-start | bytes 3538952 | tf_op jit(solution)/shard_map/ppermute | solution.py:23
  64.3 12.1 %collective-permute-start.14 = (bf16[4,144,1024]{2,1,0:T(8,128)(2,1)S(1)}, bf16[4,144,1024]{2,1,0:T(8,128)(2,1)S(1)}, u32[]{:S(2)}, u32[]{:S(2)}) collective-permute-start(bf16[4,144,1024]{2,1,0:T(8,128)(2,1)S(1)} %collective-permute-done.6.refs_2_), channel_id=1, source_target_pairs={{0,16},{1,17},{2,18},{3,19},{4,20},{5,21},{6,22},{7,23},{8,24},{9,... | collective-permute-start | bytes 3538952 | tf_op jit(solution)/shard_map/ppermute | solution.py:23
  69.2 6.3 %collective-permute-start.15 = (bf16[2,144,1024]{2,1,0:T(8,128)(2,1)S(1)}, bf16[2,144,1024]{2,1,0:T(8,128)(2,1)S(1)}, u32[]{:S(2)}, u32[]{:S(2)}) collective-permute-start(bf16[2,144,1024]{2,1,0:T(8,128)(2,1)S(1)} %collective-permute-done.7.refs_3_), channel_id=1, source_target_pairs={{0,16},{1,17},{2,18},{3,19},{4,20},{5,21},{6,22},{7,23},{8,24},{9,... | collective-permute-start | bytes 1769480 | tf_op jit(solution)/shard_map/ppermute | solution.py:23
  73.9 2.5 %collective-permute-start.16 = (bf16[2,144,1024]{2,1,0:T(8,128)(2,1)S(1)}, bf16[2,144,1024]{2,1,0:T(8,128)(2,1)S(1)}, u32[]{:S(2)}, u32[]{:S(2)}) collective-permute-start(bf16[2,144,1024]{2,1,0:T(8,128)(2,1)S(1)} %collective-permute-done.8.refs_4_), channel_id=1, source_target_pairs={{0,16},{1,17},{2,18},{3,19},{4,20},{5,21},{6,22},{7,23},{8,24},{9,... | collective-permute-start | bytes 1769480 | tf_op jit(solution)/shard_map/ppermute | solution.py:23
  73.9 13.4 %collective-permute-start.17 = (bf16[256,1024]{1,0:T(8,128)(2,1)S(1)}, bf16[256,1024]{1,0:T(8,128)(2,1)S(1)}, u32[]{:S(2)}, u32[]{:S(2)}) collective-permute-start(bf16[256,1024]{1,0:T(8,128)(2,1)S(1)} %collective-permute-done.10.refs_13_), channel_id=1, source_target_pairs={{0,4},{1,5},{2,6},{3,7},{4,8},{5,9},{6,10},{7,11},{8,12},{9,13},{1... | collective-permute-start | bytes 1572872 | tf_op jit(solution)/shard_map/ppermute | solution.py:23

commit v4 on v1

v4 whole, which is shorter than its diff:
```python
import functools

import jax
import jax.numpy as jnp
from jax import lax
from jax.experimental import pallas as pl
from jax.experimental.pallas import tpu as pltpu
from jax.sharding import PartitionSpec as P

D = 1024
L = 128
SLOTS = 32
TABLE_ROWS = 400
AXES = ("dp", "prompt")
GRID = [(y, c, x, z) for y in range(4) for c in range(2) for x in range(4) for z in range(4)]


def number(y, c, x, z):
    return (((y % 4) * 2 + c) * 4 + x % 4) * 4 + z % 4


def send(value, where):
    return lax.ppermute(value, AXES, [(number(*a), number(*where(*a))) for a in GRID])


def along_x(step):
    return lambda y, c, x, z: (y, c, x + (step if c == 0 else -step), z)


def along_first(step):
    return lambda y, c, x, z: (y + step, c, x, z) if c == 0 else (y, c, x, z + step)


def along_second(step):
    return lambda y, c, x, z: (y, c, x, z + step) if c == 0 else (y + step, c, x, z)


def along_z(step):
    return lambda y, c, x, z: (y, c, x, z + step)


def to_other_core(y, c, x, z):
    return (y, 1 - c, x, z)


def encode_kernel(
    sub, clen_ref, rlen_ref, count_ref, cid_ref, rid_ref, pc_ref, pr_ref, tbl_ref, ch_ref, rh_ref,
    up, upb, dn, dnb, gain, bias, co_ref, ra_ref, rb_ref, x_ref, acc_ref,
):
    step = pl.program_id(0)

    def token_weights(ids, length):
        high, low = ids >> 7, ids & 127
        hot = (lax.broadcasted_iota(jnp.int32, (TABLE_ROWS, L), 0) == high).astype(jnp.bfloat16)
        rows = lax.dot_general(
            tbl_ref[...].astype(jnp.bfloat16), hot, (((0,), (0,)), ((), ())), preferred_element_type=jnp.float32
        )
        mine = lax.broadcasted_iota(jnp.int32, (128, L), 0) == low
        value = jnp.sum(jnp.where(mine, rows, 0.0), axis=0, keepdims=True)
        live = lax.broadcasted_iota(jnp.int32, (1, L), 1) < length
        return jnp.where(live, value, 0.0)

    @pl.when(step == 0)
    def _():
        x_ref[0:L, :] = ch_ref[0]
        for q in range(4):
            x_ref[L * (q + 1) : L * (q + 2), :] = rh_ref[q]
        if True:
            row = lax.broadcasted_iota(jnp.int32, (16, L), 0)
            co_ref[L:, :] = jnp.zeros((16, D), jnp.bfloat16)
            ra_ref[L:, :] = jnp.zeros((16, D), jnp.bfloat16)
            w = token_weights(cid_ref[...], clen_ref[0])
            count = jnp.full((1, 2 * SLOTS), count_ref[0], jnp.int32)
            slots = jnp.concatenate([pc_ref[...], pr_ref[...], count], axis=1).astype(jnp.float32)
            words = jnp.where(row == 0, w, jnp.where(row == 1, slots, 0.0))
            co_ref[L:, 0:L] = words.astype(jnp.bfloat16)
            block = jnp.zeros((16, L), jnp.float32)
            for q in range(4):
                block = jnp.where(row == q, token_weights(rid_ref[q : q + 1, :], rlen_ref[q]), block)
            ra_ref[L:, 0:L] = block.astype(jnp.bfloat16)

    w = up.shape[1] // sub
    x = x_ref[...]
    pre = [
        jnp.dot(x, up[:, k * w : (k + 1) * w], preferred_element_type=jnp.float32)
        + upb[:, k * w : (k + 1) * w]
        for k in range(sub)
    ]
    part = None
    for k in range(sub):
        h = pre[k]
        act = (0.5 * h * (lax.erf(h * 0.7071067811865476) + 1.0)).astype(jnp.bfloat16)
        d = jnp.dot(act, dn[k * w : (k + 1) * w, :], preferred_element_type=jnp.float32)
        part = d if part is None else part + d

    @pl.when(step == 0)
    def _():
        acc_ref[...] = part

    @pl.when(step > 0)
    def _():
        acc_ref[...] += part

    @pl.when(step == pl.num_programs(0) - 1)
    def _():
        for c in range(0, 5 * L, 64):
            r = slice(c, c + 64)
            s = x_ref[r, :].astype(jnp.float32) + acc_ref[r, :] + dnb[...]
            center = jnp.mean(s, axis=-1, keepdims=True)
            e = s - center
            spread = jnp.mean(e * e, axis=-1, keepdims=True)
            y = e * lax.rsqrt(spread + 1e-5) * gain[...] + bias[...]
            m = jnp.sum(y * y, axis=-1, keepdims=True)
            unit = (y * lax.rsqrt(m + 1e-6)).astype(jnp.bfloat16)
            if c < L:
                co_ref[r, :] = unit
            elif c < 2 * L:
                ra_ref[c - L : c - L + 64, :] = unit
            else:
                rb_ref[c - 2 * L : c - 2 * L + 64, :] = unit


def encode(words, cand, refs, layer, f=1024, sub=4):
    def full(a):
        return pl.BlockSpec(a.shape, lambda i: (0,) * a.ndim, pipeline_mode=pl.Buffered(1))

    up, upb, dn, dnb, gain, bias = layer
    smem = pl.BlockSpec(memory_space=pltpu.SMEM)
    outs = [jax.ShapeDtypeStruct((n, D), jnp.bfloat16) for n in (L + 16, L + 16, 3 * L)]
    first = [*words, cand, refs]
    return pl.pallas_call(
        functools.partial(encode_kernel, sub),
        grid=(up.shape[1] // f,),
        in_specs=[smem if k < 3 else full(a) for k, a in enumerate(first)]
        + [
            pl.BlockSpec((D, f), lambda i: (0, i)),
            pl.BlockSpec((1, f), lambda i: (0, i)),
            pl.BlockSpec((f, D), lambda i: (i, 0)),
            full(dnb),
            full(gain),
            full(bias),
        ],
        out_specs=[pl.BlockSpec(o.shape, lambda i: (0, 0)) for o in outs],
        out_shape=outs,
        scratch_shapes=[pltpu.VMEM((5 * L, D), jnp.bfloat16), pltpu.VMEM((5 * L, D), jnp.float32)],
        compiler_params=pltpu.CompilerParams(
            dimension_semantics=("arbitrary",), vmem_limit_bytes=60 << 20
        ),
        name="encode",
    )(*first, up, upb, dn, dnb, gain, bias)


GROUP = 8


def pair_kernel(pos_ref, count_ref, *refs):
    cands, blocks, refs = refs[:10], refs[10:18], refs[18:]
    out_ref, cbuf, rbuf, wbuf, todo, lint, lists, lsem = refs
    y, core, x, z = pos_ref[0], pos_ref[1], pos_ref[2], pos_ref[3]

    for own, places in ((0, ((0, 0), (1, 0), (2, 0), (3, 0))), (1, ((0, 0), (0, 1), (0, 3), (0, 2)))):
        @pl.when(core == own)
        def _(places=places):
            for k, (buf, row) in enumerate(places):
                words = cands[buf][row, L : L + 16, 0:L].astype(jnp.float32)
                lint[k : k + 1, :] = words[1:2, :].astype(jnp.int32)

    move = pltpu.make_async_copy(lint, lists, lsem)
    move.start()
    move.wait()
    n = jnp.int32(0)
    for k, dz in enumerate((0, 3, 1, 2)):
        zj = (z + dz) & 3

        def scan(s, n, k=k, dz=dz, zj=zj):
            c = lists[k, s]
            r = lists[k, SLOTS + s]
            mine = (r & 3) == z

            @pl.when(mine)
            def _():
                dx = (((r & 15) >> 2) - x) & 3
                kc = c & 1
                dy = ((c >> 1) - y) & 3
                u1 = jnp.where(kc == 0, dy, dz)
                u2 = jnp.where(kc == 0, dz, dy)
                i1 = (4 - u1) & 3
                g2 = (u2 == 3) * 1 + (u2 == 1) * 2 + (u2 == 2) * 3
                g2 = jnp.where((g2 == 3) & (i1 >= 2), 4, g2)
                i = r >> 4
                back = jnp.where(core == 0, 3, 1)
                rs = jnp.where(dx == 0, 0, jnp.where(dx == 2, 3, jnp.where(dx == back, 1, 2)))
                todo[0, n] = g2 + jnp.where(kc == core, 0, 5)
                todo[1, n] = jnp.where(g2 == 4, i1 - 2, i1)
                todo[2, n] = rs * 2 + jnp.where(i == 0, 0, 1)
                todo[3, n] = jnp.maximum(i - 1, 0)
                todo[4, n] = i
                todo[5, n] = zj
                todo[6, n] = s

            return n + jnp.where(mine, 1, 0)

        n = lax.fori_loop(0, lists[k, 2 * SLOTS], scan, n)

    lane = lax.broadcasted_iota(jnp.int32, (8, L), 1)
    sub = lax.broadcasted_iota(jnp.int32, (8, L), 0)
    eye = lax.broadcasted_iota(jnp.int32, (L, L), 0) == lax.broadcasted_iota(jnp.int32, (L, L), 1)

    def fetch(t, b):
        for k, buf in enumerate(cands):
            @pl.when(todo[0, t] == k)
            def _(buf=buf):
                cbuf[b] = buf[todo[1, t]]
        for k, buf in enumerate(blocks):
            @pl.when(todo[2, t] == k)
            def _(k=k, buf=buf):
                if k % 2:
                    rbuf[b] = buf[pl.ds(pl.multiple_of(todo[3, t] * L, L), L), :]
                else:
                    rbuf[b] = buf[0:L, :]
                wbuf[b] = blocks[k - k % 2][L : L + 16, 0:L]

    def one(t, b):
        similar = lax.dot_general(
            cbuf[b, 0:L, :], rbuf[b], (((1,), (1,)), ((), ())), preferred_element_type=jnp.float32
        )
        cw = cbuf[b, L:, 0:L].astype(jnp.float32)[0:1, :]
        wide = wbuf[b].astype(jnp.float32)
        rsub = lax.broadcasted_iota(jnp.int32, (16, L), 0)
        rw = jnp.sum(jnp.where(rsub == todo[4, t], wide, 0.0), axis=0, keepdims=True)
        cw_col = jnp.sum(jnp.where(eye, cw, 0.0), axis=1, keepdims=True)
        row_best = jnp.max(jnp.where(rw > 0, similar, -10000.0), axis=1, keepdims=True)
        col_best = jnp.max(jnp.where(cw_col > 0, similar, -10000.0), axis=0, keepdims=True)
        precision = jnp.sum(cw_col * row_best, axis=0, keepdims=True) / jnp.sum(
            cw, axis=1, keepdims=True
        )
        recall = jnp.sum(rw * col_best, axis=1, keepdims=True) / jnp.sum(rw, axis=1, keepdims=True)
        fmeasure = 2.0 * precision * recall / jnp.maximum(precision + recall, 0.7)
        return precision, recall, fmeasure

    def group(g, carry):
        acc, total = carry
        for k in range(GROUP):
            t = g * GROUP + k

            @pl.when(t < n)
            def _(t=t, k=k):
                fetch(t, k)

        scores = []
        for k in range(GROUP):
            t = jnp.minimum(g * GROUP + k, n - 1)
            scores.append((t, g * GROUP + k < n, one(t, k)))
        for t, real, (p, r, f) in scores:
            three = jnp.where(lane < 32, p, jnp.where(lane < 64, r, f))
            here = (sub == todo[5, t]) & ((lane & 31) == todo[6, t]) & (lane < 96) & real
            acc = jnp.where(here, three, acc)
            rows = jnp.where(sub == 0, p, jnp.where(sub == 1, r, f))
            total = total + jnp.where(real, rows, 0.0)
        return acc, total

    zero = jnp.zeros((8, L), jnp.float32)
    acc, total = lax.fori_loop(0, (n + GROUP - 1) // GROUP, group, (zero, zero))
    line = lax.broadcasted_iota(jnp.int32, (1, L), 1)
    count = count_ref[0].astype(jnp.float32)
    sums = jnp.where(
        line == 96,
        total[0:1, :],
        jnp.where(line == 97, total[1:2, :], jnp.where(line == 98, total[2:3, :], count)),
    )
    sums = jnp.where((line >= 96) & (line < 100), sums, 0.0)
    out_ref[...] = jnp.broadcast_to(sums[None], out_ref.shape)
    mine = (y * 2 + core) * 4 + x
    for q in range(4):
        out_ref[mine * 4 + q] = acc[q : q + 1, :] + sums


def finish_kernel(got_ref, scores_ref, totals_ref):
    s = jnp.sum(got_ref[...], axis=0)
    for k in range(3):
        scores_ref[k, 0] = s[:, k * SLOTS : (k + 1) * SLOTS]
    totals_ref[...] = s[:, 96:99] / s[:, 99:100]


def score_pairs(pos, count, blocks):
    smem = pl.BlockSpec(memory_space=pltpu.SMEM)
    vmem = pl.BlockSpec(memory_space=pltpu.VMEM)
    return pl.pallas_call(
        pair_kernel,
        in_specs=[smem] * 2 + [vmem] * len(blocks),
        out_specs=vmem,
        out_shape=jax.ShapeDtypeStruct((128, 1, L), jnp.float32),
        scratch_shapes=[
            pltpu.VMEM((GROUP, L + 16, D), jnp.bfloat16),
            pltpu.VMEM((GROUP, L, D), jnp.bfloat16),
            pltpu.VMEM((GROUP, 16, L), jnp.bfloat16),
            pltpu.SMEM((8, 4 * SLOTS), jnp.int32),
            pltpu.VMEM((8, L), jnp.int32),
            pltpu.SMEM((8, L), jnp.int32),
            pltpu.SemaphoreType.DMA,
        ],
        compiler_params=pltpu.CompilerParams(vmem_limit_bytes=30 << 20),
        name="score_pairs",
    )(pos, count, *blocks)


def on_device(
    cand_hidden, ref_hidden, cand_ids, ref_ids, cand_len, reference_length, idf_table, up_weight,
    up_bias, down_weight, down_bias, norm_gain, norm_bias, pair_cand, pair_ref, pair_count,
):
    table = jnp.pad(idf_table, (0, TABLE_ROWS * 128 - idf_table.shape[0])).reshape(TABLE_ROWS, 128)
    count = pair_count.reshape(1)
    dp, prompt = lax.axis_index("dp"), lax.axis_index("prompt")
    pos = jnp.stack([dp >> 1, dp & 1, prompt >> 2, prompt & 3]).astype(jnp.int32)
    layer = (
        up_weight,
        up_bias.reshape(1, -1),
        down_weight,
        down_bias.reshape(1, -1),
        norm_gain.reshape(1, -1),
        norm_bias.reshape(1, -1),
    )
    hidden = ref_hidden.reshape(4, L, D)
    words = (
        cand_len.reshape(1),
        reference_length.reshape(4),
        count,
        cand_ids.reshape(1, L),
        ref_ids.reshape(4, L),
        pair_cand.reshape(1, SLOTS),
        pair_ref.reshape(1, SLOTS),
        table,
    )
    cand, refs_a, refs_b = encode(words, cand_hidden.reshape(1, L, D), hidden, layer)
    back_a = send(refs_a, along_x(1))
    ahead_a = send(refs_a, along_x(-1))
    c1 = send(cand, along_first(1))
    c3 = send(cand, along_first(-1))
    c2 = send(cand, along_first(2))
    back_a, ahead_a, c1, c2, c3, pos = lax.optimization_barrier((back_a, ahead_a, c1, c2, c3, pos))
    back_b = send(refs_b, along_x(1))
    ahead_b = send(refs_b, along_x(-1))
    far_a = send(back_a, along_x(1))
    own4 = jnp.stack([cand, c1, c2, c3])
    d1 = send(own4, along_second(1))
    d2 = send(own4, along_second(-1))
    d1, d2, back_b, ahead_b, far_a = lax.optimization_barrier((d1, d2, back_b, ahead_b, far_a))
    d3 = send(d1[:2], along_second(1))
    d4 = send(d2[2:], along_second(-1))
    far_b = send(back_b, along_x(1))
    d3, d4, far_b = lax.optimization_barrier((d3, d4, far_b))
    others = [send(v, to_other_core) for v in (own4, d1, d2, d3, d4)]
    cands = [own4, d1, d2, d3, d4, *others]
    blocks = [refs_a, refs_b, back_a, back_b, ahead_a, ahead_b, far_a, far_b]
    payload = score_pairs(pos, count, [*cands, *blocks])
    got = lax.all_to_all(payload, AXES, 0, 0)
    scores, totals = pl.pallas_call(
        finish_kernel,
        out_shape=[
            jax.ShapeDtypeStruct((3, 1, 1, SLOTS), jnp.float32),
            jax.ShapeDtypeStruct((1, 3), jnp.float32),
        ],
        name="finish",
    )(got)
    return scores, totals.reshape(3)


def solution(mesh):
    placed = (
        P("prompt", "dp", None, None),
        P("dp", "prompt", None, None),
        P("prompt", "dp", None),
        P("dp", "prompt", None),
        P("prompt", "dp"),
        P("dp", "prompt"),
        P(),
        P(),
        P(),
        P(),
        P(),
        P(),
        P(),
        P("dp", "prompt", None),
        P("dp", "prompt", None),
        P("dp", "prompt"),
    )
    return jax.shard_map(
        on_device,
        mesh=mesh,
        in_specs=placed,
        out_specs=(P(None, "dp", "prompt", None), P()),
        check_vma=False,
    )
```

time: 129 us -> 117 us (0.907); the launches traced: 128 us -> 114 us
  starting transfers between devices: 42.1 us -> 22.2 us
  blocking collectives: 0 us -> 19.1 us
  waiting for transfers between devices: 46 us -> 39.8 us
  Pallas kernels: 31.4 us -> 28.3 us
  other arithmetic: 4.09 us -> 1.26 us
    all_to_all x0 -> x1, blocking collectives: none -> 19.1 us  [on_device(): got = lax.all_to_all(payload, AXES, 0, 0)]
    all_to_all x1 -> x0, waiting for transfers between devices: 13.4 us -> none  [on_device(): got = jnp.sum(lax.all_to_all(payload, AXES, 0, 0), axis=0)]
    ppermute x18, starting transfers between devices: 34.8 us -> 22.2 us  [send(): lax.ppermute(value, AXES, [(number(*a), number(*where(*a))) for a in GRID])]
    all_to_all x1 -> x0, starting transfers between devices: 7.35 us -> none  [on_device(): got = jnp.sum(lax.all_to_all(payload, AXES, 0, 0), axis=0)]
    ppermute x18, waiting for transfers between devices: 32.6 us -> 39.8 us  [send(): lax.ppermute(value, AXES, [(number(*a), number(*where(*a))) for a in GRID])]
    pallas_call x1 -> x2, Pallas kernels: 12.9 us -> 9.82 us  [the longest x1 8.19 us: score_pairs(): pl.pallas_call(pair_kernel, in_specs=[smem] * 2 + [vmem] * len(blocks), o...]
    reshape x1, local copies, waits for them, and re-layouts: 0.07 us -> 1.62 us  [on_device(): jnp.pad(idf_table, (0, TABLE_ROWS * 128 - idf_table.shape[0]))]
    another operation x2 -> x1, other arithmetic: 1.52 us -> 0.08 us  [on_device(): jnp.stack([dp >> 1, dp & 1, prompt >> 2, prompt & 3]).astype(jnp.int32)]
  transfers between devices with their start and end apart: 19 -> 18, of which waited for: 7 -> 9; matrix products, arithmetic and copies ran while one was open for 1% -> 0% of each run, Pallas kernels for 0% -> 0%
where the time goes in v4:
time: 117 us; the launch traced here: 114 us
  waiting for transfers between devices  39.8 us (34%)
  Pallas kernels  28.3 us (24%)
  starting transfers between devices  22.2 us (19%)
  blocking collectives  19.1 us (16%)
  between operations  2 us (2%)
  local copies, waits for them, and re-layouts  1.71 us (1%)
  other arithmetic  1.26 us (1%)
    ppermute x18, waiting for transfers between devices, send(): lax.ppermute(value, AXES, [(number(*a), number(*where(*a))) for a in GRID])  39.8 us
    ppermute x18, starting transfers between devices, send(): lax.ppermute(value, AXES, [(number(*a), number(*where(*a))) for a in GRID])  22.2 us
    all_to_all x1, blocking collectives, on_device(): got = lax.all_to_all(payload, AXES, 0, 0)  19.1 us
    pallas_call x1, Pallas kernels, encode(): pl.pallas_call(functools.partial(encode_kernel, sub), grid=(up.shape[1] /...  18.5 us
    pallas_call x1, Pallas kernels, score_pairs(): pl.pallas_call(pair_kernel, in_specs=[smem] * 2 + [vmem] * len(blocks), o...  8.19 us
  transfers between devices with their start and end apart: 18, of which 9 were waited for; matrix products, arithmetic and copies ran while one was open for 0% of the time, Pallas kernels for 0%

profile of v4, /device:TPU:1, one launch (start us, length us, event | category | flops | bytes accessed | tf_op | source)
XLA Modules:
  0.0 114.4 jit_solution(11855651831411621459)
XLA Ops:
  1.9 1.6 %pad_bitcast_fusion.tbl_ref = f32[400,128]{1,0:T(8,128)} fusion(f32[50265]{0:T(1024)} %param.22), kind=kLoop, calls=%fused_computation.1 | loop fusion | bytes 405860 | tf_op jit(solution)/shard_map/reshape | solution.py:311
  3.5 18.5 %encode.1 = (bf16[144,1024]{1,0:T(8,128)(2,1)}, bf16[144,1024]{1,0:T(8,128)(2,1)}, bf16[384,1024]{1,0:T(8,128)(2,1)}) custom-call(s32[1]{0:T(128)} %bitcast.24.clen_ref, s32[4]{0:T(128)} %bitcast.38, s32[1]{0:T(128)} %bitcast.25.count_ref, s32[1,128]{1,0:T(1,128)} %bitcast.39, s32[4,128]{1,0:T(4,128)} %bitcast.37, s32[1,32]{1,0:T(1,128)} %bitcast.40, ...), custom_call_target="tpu_custom_call" | custom-call | tf_op jit(solution)/shard_map/encode/pallas_call | solution.py:131
  22.0 2.0 %collective-permute-start.1 = (bf16[144,1024]{1,0:T(8,128)(2,1)}, bf16[144,1024]{1,0:T(8,128)(2,1)S(1)}, u32[]{:S(2)}, u32[]{:S(2)}) collective-permute-start(bf16[144,1024]{1,0:T(8,128)(2,1)} %get-tuple-element.21.refs_10_), channel_id=1, source_target_pairs={{0,12},{1,13},{2,14},{3,15},{4,0},{5,1},{6,2},{7,3},{8,4},{9,5},{1... | collective-permute-start | bytes 884744 | tf_op jit(solution)/shard_map/ppermute | solution.py:23
  24.1 1.3 %collective-permute-start = (bf16[144,1024]{1,0:T(8,128)(2,1)}, bf16[144,1024]{1,0:T(8,128)(2,1)S(1)}, u32[]{:S(2)}, u32[]{:S(2)}) collective-permute-start(bf16[144,1024]{1,0:T(8,128)(2,1)} %get-tuple-element.21.refs_10_), channel_id=1, source_target_pairs={{0,4},{1,5},{2,6},{3,7},{4,8},{5,9},{6,10},{7,11},{8,12},{9,13},{1... | collective-permute-start | bytes 884744 | tf_op jit(solution)/shard_map/ppermute | solution.py:23
  25.4 3.9 %collective-permute-start.4 = (bf16[144,1024]{1,0:T(8,128)(2,1)}, bf16[144,1024]{1,0:T(8,128)(2,1)S(1)}, u32[]{:S(2)}, u32[]{:S(2)}) collective-permute-start(bf16[144,1024]{1,0:T(8,128)(2,1)} %get-tuple-element.22), channel_id=1, source_target_pairs={{0,96},{1,97},{2,98},{3,99},{4,100},{5,101},{6,102},{7,103},{8,104... | collective-permute-start | bytes 884744 | tf_op jit(solution)/shard_map/ppermute | solution.py:23
  29.3 0.0 collective-permute-start.3
  29.3 0.7 collective-permute-start.2
  30.0 0.1 pad_add_fusion.pos_ref
  30.1 0.0 collective-permute-done.1.refs_14_
  30.1 3.1 %collective-permute-done.refs_12_ = bf16[144,1024]{1,0:T(8,128)(2,1)S(1)} collective-permute-done((bf16[144,1024]{1,0:T(8,128)(2,1)}, bf16[144,1024]{1,0:T(8,128)(2,1)S(1)}, u32[]{:S(2)}, u32[]{:S(2)}) %collective-permute-start) | collective-permute-done | bytes 294944 | tf_op jit(solution)/shard_map/ppermute | solution.py:23
  33.1 3.3 %collective-permute-done.4 = bf16[144,1024]{1,0:T(8,128)(2,1)S(1)} collective-permute-done((bf16[144,1024]{1,0:T(8,128)(2,1)}, bf16[144,1024]{1,0:T(8,128)(2,1)S(1)}, u32[]{:S(2)}, u32[]{:S(2)}) %collective-permute-start.4) | collective-permute-done | bytes 294944 | tf_op jit(solution)/shard_map/ppermute | solution.py:23
  36.4 0.5 collective-permute-done.3
  36.9 2.8 %collective-permute-done.2 = bf16[144,1024]{1,0:T(8,128)(2,1)S(1)} collective-permute-done((bf16[144,1024]{1,0:T(8,128)(2,1)}, bf16[144,1024]{1,0:T(8,128)(2,1)S(1)}, u32[]{:S(2)}, u32[]{:S(2)}) %collective-permute-start.2) | collective-permute-done | bytes 294944 | tf_op jit(solution)/shard_map/ppermute | solution.py:23
  39.7 0.0 copy-start
  39.7 1.2 %pad_maximum_fusion.refs_0_ = bf16[4,144,1024]{2,1,0:T(8,128)(2,1)S(1)} fusion(bf16[1,144,1024]{2,1,0:T(8,128)(2,1)S(1)} %bitcast.29, bf16[1,144,1024]{2,1,0:T(8,128)(2,1)S(1)} %bitcast.30, bf16[1,144,1024]{2,1,0:T(8,128)(2,1)S(1)} %bitcast.31, bf16[1,144,1024]{2,1,0:T(8,128)(2,1)} %bitcast.28), kind=kLoop, calls=%fused_computation | loop fusion | flops 1769472 | bytes 2359296 | tf_op jit(solution)/shard_map/stack | solution.py:344
  40.9 2.5 %collective-permute-start.6 = (bf16[4,144,1024]{2,1,0:T(8,128)(2,1)S(1)}, bf16[4,144,1024]{2,1,0:T(8,128)(2,1)S(1)}, u32[]{:S(2)}, u32[]{:S(2)}) collective-permute-start(bf16[4,144,1024]{2,1,0:T(8,128)(2,1)S(1)} %pad_maximum_fusion.refs_0_), channel_id=1, source_target_pairs={{0,3},{1,0},{2,1},{3,2},{4,7},{5,4},{6,5},{7,6},{8,11},{9,8},{10,9... | collective-permute-start | bytes 3538952 | tf_op jit(solution)/shard_map/ppermute | solution.py:23
  43.4 0.0 collective-permute-start.5
  43.4 0.0 copy-done
  43.4 0.0 copy-start.1
  43.4 0.1 collective-permute-start.8
  43.5 2.7 %collective-permute-start.7 = (bf16[384,1024]{1,0:T(8,128)(2,1)S(1)}, bf16[384,1024]{1,0:T(8,128)(2,1)S(1)}, u32[]{:S(2)}, u32[]{:S(2)}) collective-permute-start(bf16[384,1024]{1,0:T(8,128)(2,1)S(1)} %copy-done), channel_id=1, source_target_pairs={{0,4},{1,5},{2,6},{3,7},{4,8},{5,9},{6,10},{7,11},{8,12},{9,13},{1... | collective-permute-start | bytes 2359304 | tf_op jit(solution)/shard_map/ppermute | solution.py:23
  46.2 0.1 collective-permute-start.9
  46.2 20.1 %collective-permute-done.9.refs_16_ = bf16[144,1024]{1,0:T(8,128)(2,1)S(1)} collective-permute-done((bf16[144,1024]{1,0:T(8,128)(2,1)S(1)}, bf16[144,1024]{1,0:T(8,128)(2,1)S(1)}, u32[]{:S(2)}, u32[]{:S(2)}) %collective-permute-start.9) | collective-permute-done | bytes 294944 | tf_op jit(solution)/shard_map/ppermute | solution.py:23
  66.3 0.0 collective-permute-done.8.refs_15_
  66.3 0.0 collective-permute-done.7.refs_13_
  66.3 0.0 collective-permute-done.6.refs_2_
  66.3 0.0 collective-permute-done.5.refs_1_
  66.4 3.1 %collective-permute-start.11 = (bf16[2,144,1024]{2,1,0:T(8,128)(2,1)S(1)}, bf16[2,144,1024]{2,1,0:T(8,128)(2,1)S(1)}, u32[]{:S(2)}, u32[]{:S(2)}) collective-permute-start(bf16[2,144,1024]{2,1,0:T(8,128)(2,1)S(1)} %slice.7), channel_id=1, source_target_pairs={{0,3},{1,0},{2,1},{3,2},{4,7},{5,4},{6,5},{7,6},{8,11},{9,8},{10,9... | collective-permute-start | bytes 1769480 | tf_op jit(solution)/shard_map/ppermute | solution.py:23
  69.5 3.1 %collective-permute-start.12 = (bf16[384,1024]{1,0:T(8,128)(2,1)S(1)}, bf16[384,1024]{1,0:T(8,128)(2,1)S(1)}, u32[]{:S(2)}, u32[]{:S(2)}) collective-permute-start(bf16[384,1024]{1,0:T(8,128)(2,1)S(1)} %collective-permute-done.7.refs_13_), channel_id=1, source_target_pairs={{0,4},{1,5},{2,6},{3,7},{4,8},{5,9},{6,10},{7,11},{8,12},{9,13},{1... | collective-permute-start | bytes 2359304 | tf_op jit(solution)/shard_map/ppermute | solution.py:23
  72.6 0.1 collective-permute-start.10
  72.7 0.1 collective-permute-start.13
  72.8 0.5 collective-permute-start.14
  73.3 3.0 %collective-permute-done.11.refs_4_ = bf16[2,144,1024]{2,1,0:T(8,128)(2,1)S(1)} collective-permute-done((bf16[2,144,1024]{2,1,0:T(8,128)(2,1)S(1)}, bf16[2,144,1024]{2,1,0:T(8,128)(2,1)S(1)}, u32[]{:S(2)}, u32[]{:S(2)}) %collective-permute-start.11) | collective-permute-done | bytes 589856 | tf_op jit(solution)/shard_map/ppermute | solution.py:23
  76.3 1.6 %collective-permute-start.15 = (bf16[4,144,1024]{2,1,0:T(8,128)(2,1)S(1)}, bf16[4,144,1024]{2,1,0:T(8,128)(2,1)S(1)}, u32[]{:S(2)}, u32[]{:S(2)}) collective-permute-start(bf16[4,144,1024]{2,1,0:T(8,128)(2,1)S(1)} %collective-permute-done.6.refs_2_), channel_id=1, source_target_pairs={{0,16},{1,17},{2,18},{3,19},{4,20},{5,21},{6,22},{7,23},{8,24},{9,... | collective-permute-start | bytes 3538952 | tf_op jit(solution)/shard_map/ppermute | solution.py:23
  77.9 4.8 %collective-permute-done.10.refs_3_ = bf16[2,144,1024]{2,1,0:T(8,128)(2,1)S(1)} collective-permute-done((bf16[2,144,1024]{2,1,0:T(8,128)(2,1)S(1)}, bf16[2,144,1024]{2,1,0:T(8,128)(2,1)S(1)}, u32[]{:S(2)}, u32[]{:S(2)}) %collective-permute-start.10) | collective-permute-done | bytes 589856 | tf_op jit(solution)/shard_map/ppermute | solution.py:23
  82.6 0.0 collective-permute-done.12.refs_17_
  82.6 0.0 collective-permute-start.16
  82.6 0.5 collective-permute-start.17
  83.1 0.0 collective-permute-done.13.refs_5_
  83.1 0.0 collective-permute-done.14.refs_6_
  83.1 0.0 collective-permute-done.15.refs_7_
  83.2 1.5 %collective-permute-done.16.refs_8_ = bf16[2,144,1024]{2,1,0:T(8,128)(2,1)S(1)} collective-permute-done((bf16[2,144,1024]{2,1,0:T(8,128)(2,1)S(1)}, bf16[2,144,1024]{2,1,0:T(8,128)(2,1)S(1)}, u32[]{:S(2)}, u32[]{:S(2)}) %collective-permute-start.16) | collective-permute-done | bytes 589856 | tf_op jit(solution)/shard_map/ppermute | solution.py:23
  84.6 0.8 collective-permute-done.17.refs_9_
  85.5 0.0 copy-done.1
  85.5 8.2 %score_pairs.1 = f32[128,1,128]{2,1,0:T(1,128)S(1)} custom-call(s32[4]{0:T(128)S(1)} %pad_add_fusion.pos_ref, s32[1]{0:T(128)} %bitcast.26.count_ref, bf16[4,144,1024]{2,1,0:T(8,128)(2,1)S(1)} %pad_maximum_fusion.refs_0_, bf16[4,144,1024]{2,1,0:T(8,128)(2,1)S(1)} %collective-permute-done.5.refs_1_, bf16[4,144,1024]{2,1,0:T(8,128)(2,1)S(1)} %collective-permute-done.6.refs_2_, ...), custom_call_target="tpu_custom_call" | custom-call | tf_op jit(solution)/shard_map/score_pairs/pallas_call | solution.py:288
  93.7 19.1 %all_to_all.5.got_ref = f32[128,1,128]{2,1,0:T(1,128)} all-to-all(f32[128,1,128]{2,1,0:T(1,128)S(1)} %score_pairs.1), channel_id=1, replica_groups=mesh['dp'=8,'prompt'=16] {'dp','prompt'}, dimensions={0} | all-to-all | bytes 131072 | tf_op jit(solution)/shard_map/all_to_all | solution.py:356
  112.7 1.6 %finish.1 = (f32[3,1,1,32]{3,2,1,0:T(1,128)}, f32[1,3]{1,0:T(1,128)}) custom-call(f32[128,1,128]{2,1,0:T(1,128)} %all_to_all.5.got_ref), custom_call_target="tpu_custom_call" | custom-call | tf_op jit(solution)/shard_map/finish/pallas_call | solution.py:357
  (2 shorter events, 0.1 us)
Async XLA Ops:
  22.0 8.0 %collective-permute-start.1 = (bf16[144,1024]{1,0:T(8,128)(2,1)}, bf16[144,1024]{1,0:T(8,128)(2,1)S(1)}, u32[]{:S(2)}, u32[]{:S(2)}) collective-permute-start(bf16[144,1024]{1,0:T(8,128)(2,1)} %get-tuple-element.21.refs_10_), channel_id=1, source_target_pairs={{0,12},{1,13},{2,14},{3,15},{4,0},{5,1},{6,2},{7,3},{8,4},{9,5},{1... | collective-permute-start | bytes 884744 | tf_op jit(solution)/shard_map/ppermute | solution.py:23
  24.1 9.1 %collective-permute-start = (bf16[144,1024]{1,0:T(8,128)(2,1)}, bf16[144,1024]{1,0:T(8,128)(2,1)S(1)}, u32[]{:S(2)}, u32[]{:S(2)}) collective-permute-start(bf16[144,1024]{1,0:T(8,128)(2,1)} %get-tuple-element.21.refs_10_), channel_id=1, source_target_pairs={{0,4},{1,5},{2,6},{3,7},{4,8},{5,9},{6,10},{7,11},{8,12},{9,13},{1... | collective-permute-start | bytes 884744 | tf_op jit(solution)/shard_map/ppermute | solution.py:23
  25.4 11.0 %collective-permute-start.4 = (bf16[144,1024]{1,0:T(8,128)(2,1)}, bf16[144,1024]{1,0:T(8,128)(2,1)S(1)}, u32[]{:S(2)}, u32[]{:S(2)}) collective-permute-start(bf16[144,1024]{1,0:T(8,128)(2,1)} %get-tuple-element.22), channel_id=1, source_target_pairs={{0,96},{1,97},{2,98},{3,99},{4,100},{5,101},{6,102},{7,103},{8,104... | collective-permute-start | bytes 884744 | tf_op jit(solution)/shard_map/ppermute | solution.py:23
  29.3 7.6 %collective-permute-start.3 = (bf16[144,1024]{1,0:T(8,128)(2,1)}, bf16[144,1024]{1,0:T(8,128)(2,1)S(1)}, u32[]{:S(2)}, u32[]{:S(2)}) collective-permute-start(bf16[144,1024]{1,0:T(8,128)(2,1)} %get-tuple-element.22), channel_id=1, source_target_pairs={{0,64},{1,65},{2,66},{3,67},{4,68},{5,69},{6,70},{7,71},{8,72},{9,... | collective-permute-start | bytes 884744 | tf_op jit(solution)/shard_map/ppermute | solution.py:23
  29.3 10.4 %collective-permute-start.2 = (bf16[144,1024]{1,0:T(8,128)(2,1)}, bf16[144,1024]{1,0:T(8,128)(2,1)S(1)}, u32[]{:S(2)}, u32[]{:S(2)}) collective-permute-start(bf16[144,1024]{1,0:T(8,128)(2,1)} %get-tuple-element.22), channel_id=1, source_target_pairs={{0,32},{1,33},{2,34},{3,35},{4,36},{5,37},{6,38},{7,39},{8,40},{9,... | collective-permute-start | bytes 884744 | tf_op jit(solution)/shard_map/ppermute | solution.py:23
  39.7 3.7 %copy-start = (bf16[384,1024]{1,0:T(8,128)(2,1)S(1)}, bf16[384,1024]{1,0:T(8,128)(2,1)}, u32[]{:S(2)}) copy-start(bf16[384,1024]{1,0:T(8,128)(2,1)} %get-tuple-element.27.refs_11_) | copy-start | bytes 2359300
  40.9 25.4 %collective-permute-start.6 = (bf16[4,144,1024]{2,1,0:T(8,128)(2,1)S(1)}, bf16[4,144,1024]{2,1,0:T(8,128)(2,1)S(1)}, u32[]{:S(2)}, u32[]{:S(2)}) collective-permute-start(bf16[4,144,1024]{2,1,0:T(8,128)(2,1)S(1)} %pad_maximum_fusion.refs_0_), channel_id=1, source_target_pairs={{0,3},{1,0},{2,1},{3,2},{4,7},{5,4},{6,5},{7,6},{8,11},{9,8},{10,9... | collective-permute-start | bytes 3538952 | tf_op jit(solution)/shard_map/ppermute | solution.py:23
  43.4 22.9 %collective-permute-start.5 = (bf16[4,144,1024]{2,1,0:T(8,128)(2,1)S(1)}, bf16[4,144,1024]{2,1,0:T(8,128)(2,1)S(1)}, u32[]{:S(2)}, u32[]{:S(2)}) collective-permute-start(bf16[4,144,1024]{2,1,0:T(8,128)(2,1)S(1)} %pad_maximum_fusion.refs_0_), channel_id=1, source_target_pairs={{0,1},{1,2},{2,3},{3,0},{4,5},{5,6},{6,7},{7,4},{8,9},{9,10},{10,1... | collective-permute-start | bytes 3538952 | tf_op jit(solution)/shard_map/ppermute | solution.py:23
  43.4 42.0 %copy-start.1 = (bf16[144,1024]{1,0:T(8,128)(2,1)S(1)}, bf16[144,1024]{1,0:T(8,128)(2,1)}, u32[]{:S(2)}) copy-start(bf16[144,1024]{1,0:T(8,128)(2,1)} %get-tuple-element.21.refs_10_) | copy-start | bytes 884740
  43.4 22.9 %collective-permute-start.8 = (bf16[384,1024]{1,0:T(8,128)(2,1)S(1)}, bf16[384,1024]{1,0:T(8,128)(2,1)S(1)}, u32[]{:S(2)}, u32[]{:S(2)}) collective-permute-start(bf16[384,1024]{1,0:T(8,128)(2,1)S(1)} %copy-done), channel_id=1, source_target_pairs={{0,12},{1,13},{2,14},{3,15},{4,0},{5,1},{6,2},{7,3},{8,4},{9,5},{1... | collective-permute-start | bytes 2359304 | tf_op jit(solution)/shard_map/ppermute | solution.py:23
  43.5 22.8 %collective-permute-start.7 = (bf16[384,1024]{1,0:T(8,128)(2,1)S(1)}, bf16[384,1024]{1,0:T(8,128)(2,1)S(1)}, u32[]{:S(2)}, u32[]{:S(2)}) collective-permute-start(bf16[384,1024]{1,0:T(8,128)(2,1)S(1)} %copy-done), channel_id=1, source_target_pairs={{0,4},{1,5},{2,6},{3,7},{4,8},{5,9},{6,10},{7,11},{8,12},{9,13},{1... | collective-permute-start | bytes 2359304 | tf_op jit(solution)/shard_map/ppermute | solution.py:23
  46.2 20.1 %collective-permute-start.9 = (bf16[144,1024]{1,0:T(8,128)(2,1)S(1)}, bf16[144,1024]{1,0:T(8,128)(2,1)S(1)}, u32[]{:S(2)}, u32[]{:S(2)}) collective-permute-start(bf16[144,1024]{1,0:T(8,128)(2,1)S(1)} %collective-permute-done.refs_12_), channel_id=1, source_target_pairs={{0,4},{1,5},{2,6},{3,7},{4,8},{5,9},{6,10},{7,11},{8,12},{9,13},{1... | collective-permute-start | bytes 884744 | tf_op jit(solution)/shard_map/ppermute | solution.py:23
  66.4 9.9 %collective-permute-start.11 = (bf16[2,144,1024]{2,1,0:T(8,128)(2,1)S(1)}, bf16[2,144,1024]{2,1,0:T(8,128)(2,1)S(1)}, u32[]{:S(2)}, u32[]{:S(2)}) collective-permute-start(bf16[2,144,1024]{2,1,0:T(8,128)(2,1)S(1)} %slice.7), channel_id=1, source_target_pairs={{0,3},{1,0},{2,1},{3,2},{4,7},{5,4},{6,5},{7,6},{8,11},{9,8},{10,9... | collective-permute-start | bytes 1769480 | tf_op jit(solution)/shard_map/ppermute | solution.py:23
  69.5 13.2 %collective-permute-start.12 = (bf16[384,1024]{1,0:T(8,128)(2,1)S(1)}, bf16[384,1024]{1,0:T(8,128)(2,1)S(1)}, u32[]{:S(2)}, u32[]{:S(2)}) collective-permute-start(bf16[384,1024]{1,0:T(8,128)(2,1)S(1)} %collective-permute-done.7.refs_13_), channel_id=1, source_target_pairs={{0,4},{1,5},{2,6},{3,7},{4,8},{5,9},{6,10},{7,11},{8,12},{9,13},{1... | collective-permute-start | bytes 2359304 | tf_op jit(solution)/shard_map/ppermute | solution.py:23
  72.6 10.0 %collective-permute-start.10 = (bf16[2,144,1024]{2,1,0:T(8,128)(2,1)S(1)}, bf16[2,144,1024]{2,1,0:T(8,128)(2,1)S(1)}, u32[]{:S(2)}, u32[]{:S(2)}) collective-permute-start(bf16[2,144,1024]{2,1,0:T(8,128)(2,1)S(1)} %slice.6), channel_id=1, source_target_pairs={{0,1},{1,2},{2,3},{3,0},{4,5},{5,6},{6,7},{7,4},{8,9},{9,10},{10,1... | collective-permute-start | bytes 1769480 | tf_op jit(solution)/shard_map/ppermute | solution.py:23
  72.7 10.4 %collective-permute-start.13 = (bf16[4,144,1024]{2,1,0:T(8,128)(2,1)S(1)}, bf16[4,144,1024]{2,1,0:T(8,128)(2,1)S(1)}, u32[]{:S(2)}, u32[]{:S(2)}) collective-permute-start(bf16[4,144,1024]{2,1,0:T(8,128)(2,1)S(1)} %pad_maximum_fusion.refs_0_), channel_id=1, source_target_pairs={{0,16},{1,17},{2,18},{3,19},{4,20},{5,21},{6,22},{7,23},{8,24},{9,... | collective-permute-start | bytes 3538952 | tf_op jit(solution)/shard_map/ppermute | solution.py:23
  72.8 10.4 %collective-permute-start.14 = (bf16[4,144,1024]{2,1,0:T(8,128)(2,1)S(1)}, bf16[4,144,1024]{2,1,0:T(8,128)(2,1)S(1)}, u32[]{:S(2)}, u32[]{:S(2)}) collective-permute-start(bf16[4,144,1024]{2,1,0:T(8,128)(2,1)S(1)} %collective-permute-done.5.refs_1_), channel_id=1, source_target_pairs={{0,16},{1,17},{2,18},{3,19},{4,20},{5,21},{6,22},{7,23},{8,24},{9,... | collective-permute-start | bytes 3538952 | tf_op jit(solution)/shard_map/ppermute | solution.py:23
  76.3 6.9 %collective-permute-start.15 = (bf16[4,144,1024]{2,1,0:T(8,128)(2,1)S(1)}, bf16[4,144,1024]{2,1,0:T(8,128)(2,1)S(1)}, u32[]{:S(2)}, u32[]{:S(2)}) collective-permute-start(bf16[4,144,1024]{2,1,0:T(8,128)(2,1)S(1)} %collective-permute-done.6.refs_2_), channel_id=1, source_target_pairs={{0,16},{1,17},{2,18},{3,19},{4,20},{5,21},{6,22},{7,23},{8,24},{9,... | collective-permute-start | bytes 3538952 | tf_op jit(solution)/shard_map/ppermute | solution.py:23
  82.6 2.0 %collective-permute-start.16 = (bf16[2,144,1024]{2,1,0:T(8,128)(2,1)S(1)}, bf16[2,144,1024]{2,1,0:T(8,128)(2,1)S(1)}, u32[]{:S(2)}, u32[]{:S(2)}) collective-permute-start(bf16[2,144,1024]{2,1,0:T(8,128)(2,1)S(1)} %collective-permute-done.10.refs_3_), channel_id=1, source_target_pairs={{0,16},{1,17},{2,18},{3,19},{4,20},{5,21},{6,22},{7,23},{8,24},{9,... | collective-permute-start | bytes 1769480 | tf_op jit(solution)/shard_map/ppermute | solution.py:23
  82.6 2.8 %collective-permute-start.17 = (bf16[2,144,1024]{2,1,0:T(8,128)(2,1)S(1)}, bf16[2,144,1024]{2,1,0:T(8,128)(2,1)S(1)}, u32[]{:S(2)}, u32[]{:S(2)}) collective-permute-start(bf16[2,144,1024]{2,1,0:T(8,128)(2,1)S(1)} %collective-permute-done.11.refs_4_), channel_id=1, source_target_pairs={{0,16},{1,17},{2,18},{3,19},{4,20},{5,21},{6,22},{7,23},{8,24},{9,... | collective-permute-start | bytes 1769480 | tf_op jit(solution)/shard_map/ppermute | solution.py:23

commit v5 on v4

--- a/solution.py
+++ b/solution.py
@@ -43,11 +43,18 @@
     return (y, 1 - c, x, z)
 
 
-def encode_kernel(
-    sub, clen_ref, rlen_ref, count_ref, cid_ref, rid_ref, pc_ref, pr_ref, tbl_ref, ch_ref, rh_ref,
-    up, upb, dn, dnb, gain, bias, co_ref, ra_ref, rb_ref, x_ref, acc_ref,
-):
+def encode_kernel(n_cand, picks, weights, sub, *refs):
+    refs = list(refs)
+    if weights:
+        clen_ref, rlen_ref, count_ref, cid_ref, rid_ref, pc_ref, pr_ref, tbl_ref = refs[:8]
+        refs = refs[8:]
+    ch_ref = refs.pop(0) if n_cand else None
+    rh_ref, up, upb, dn, dnb, gain, bias = refs[:7]
+    refs = refs[7:]
+    co_ref = refs.pop(0) if n_cand else None
+    ro_ref, x_ref, acc_ref = refs
     step = pl.program_id(0)
+    seqs = n_cand + len(picks)
 
     def token_weights(ids, length):
         high, low = ids >> 7, ids & 127
@@ -62,13 +69,14 @@
 
     @pl.when(step == 0)
     def _():
-        x_ref[0:L, :] = ch_ref[0]
-        for q in range(4):
-            x_ref[L * (q + 1) : L * (q + 2), :] = rh_ref[q]
-        if True:
+        if n_cand:
+            x_ref[0:L, :] = ch_ref[0]
+        for k, q in enumerate(picks):
+            x_ref[L * (n_cand + k) : L * (n_cand + k + 1), :] = rh_ref[q]
+        if weights:
             row = lax.broadcasted_iota(jnp.int32, (16, L), 0)
             co_ref[L:, :] = jnp.zeros((16, D), jnp.bfloat16)
-            ra_ref[L:, :] = jnp.zeros((16, D), jnp.bfloat16)
+            ro_ref[len(picks) * L :, :] = jnp.zeros((16, D), jnp.bfloat16)
             w = token_weights(cid_ref[...], clen_ref[0])
             count = jnp.full((1, 2 * SLOTS), count_ref[0], jnp.int32)
             slots = jnp.concatenate([pc_ref[...], pr_ref[...], count], axis=1).astype(jnp.float32)
@@ -77,7 +85,7 @@
             block = jnp.zeros((16, L), jnp.float32)
             for q in range(4):
                 block = jnp.where(row == q, token_weights(rid_ref[q : q + 1, :], rlen_ref[q]), block)
-            ra_ref[L:, 0:L] = block.astype(jnp.bfloat16)
+            ro_ref[len(picks) * L :, 0:L] = block.astype(jnp.bfloat16)
 
     w = up.shape[1] // sub
     x = x_ref[...]
@@ -103,7 +111,7 @@
 
     @pl.when(step == pl.num_programs(0) - 1)
     def _():
-        for c in range(0, 5 * L, 64):
+        for c in range(0, seqs * L, 64):
             r = slice(c, c + 64)
             s = x_ref[r, :].astype(jnp.float32) + acc_ref[r, :] + dnb[...]
             center = jnp.mean(s, axis=-1, keepdims=True)
@@ -112,26 +120,29 @@
             y = e * lax.rsqrt(spread + 1e-5) * gain[...] + bias[...]
             m = jnp.sum(y * y, axis=-1, keepdims=True)
             unit = (y * lax.rsqrt(m + 1e-6)).astype(jnp.bfloat16)
-            if c < L:
+            if c < L * n_cand:
                 co_ref[r, :] = unit
-            elif c < 2 * L:
-                ra_ref[c - L : c - L + 64, :] = unit
             else:
-                rb_ref[c - 2 * L : c - 2 * L + 64, :] = unit
-
-
-def encode(words, cand, refs, layer, f=1024, sub=4):
+                ro_ref[c - L * n_cand : c - L * n_cand + 64, :] = unit
+
+
+def encode(picks, cand, rh, words, layer, f=1024, sub=4):
     def full(a):
         return pl.BlockSpec(a.shape, lambda i: (0,) * a.ndim, pipeline_mode=pl.Buffered(1))
 
     up, upb, dn, dnb, gain, bias = layer
+    n_cand = 0 if cand is None else 1
+    extra = 16 if words else 0
+    seqs = n_cand + len(picks)
     smem = pl.BlockSpec(memory_space=pltpu.SMEM)
-    outs = [jax.ShapeDtypeStruct((n, D), jnp.bfloat16) for n in (L + 16, L + 16, 3 * L)]
-    first = [*words, cand, refs]
+    outs = [jax.ShapeDtypeStruct((L + extra, D), jnp.bfloat16)] * n_cand + [
+        jax.ShapeDtypeStruct((len(picks) * L + extra, D), jnp.bfloat16)
+    ]
+    first = list(words) + ([cand] if n_cand else []) + [rh]
     return pl.pallas_call(
-        functools.partial(encode_kernel, sub),
+        functools.partial(encode_kernel, n_cand, picks, bool(words), sub),
         grid=(up.shape[1] // f,),
-        in_specs=[smem if k < 3 else full(a) for k, a in enumerate(first)]
+        in_specs=[smem if k < 3 and words else full(a) for k, a in enumerate(first)]
         + [
             pl.BlockSpec((D, f), lambda i: (0, i)),
             pl.BlockSpec((1, f), lambda i: (0, i)),
@@ -142,15 +153,22 @@
         ],
         out_specs=[pl.BlockSpec(o.shape, lambda i: (0, 0)) for o in outs],
         out_shape=outs,
-        scratch_shapes=[pltpu.VMEM((5 * L, D), jnp.bfloat16), pltpu.VMEM((5 * L, D), jnp.float32)],
+        scratch_shapes=[
+            pltpu.VMEM((seqs * L, D), jnp.bfloat16),
+            pltpu.VMEM((seqs * L, D), jnp.float32),
+        ],
         compiler_params=pltpu.CompilerParams(
             dimension_semantics=("arbitrary",), vmem_limit_bytes=60 << 20
         ),
+        cost_estimate=pl.CostEstimate(
+            flops=4 * seqs * L * D * up.shape[1], bytes_accessed=17 << 20, transcendentals=0
+        ),
         name="encode",
     )(*first, up, upb, dn, dnb, gain, bias)
 
 
 GROUP = 8
+AHEAD = 3
 
 
 def pair_kernel(pos_ref, count_ref, *refs):
@@ -158,6 +176,7 @@
     out_ref, cbuf, rbuf, wbuf, todo, lint, lists, lsem = refs
     y, core, x, z = pos_ref[0], pos_ref[1], pos_ref[2], pos_ref[3]
 
+    lint[...] = jnp.zeros((8, L), jnp.int32)
     for own, places in ((0, ((0, 0), (1, 0), (2, 0), (3, 0))), (1, ((0, 0), (0, 1), (0, 3), (0, 2)))):
         @pl.when(core == own)
         def _(places=places):
@@ -165,60 +184,69 @@
                 words = cands[buf][row, L : L + 16, 0:L].astype(jnp.float32)
                 lint[k : k + 1, :] = words[1:2, :].astype(jnp.int32)
 
+    lane = lax.broadcasted_iota(jnp.int32, (8, L), 1)
+    sub = lax.broadcasted_iota(jnp.int32, (8, L), 0)
+    c = lint[...]
+    r = pltpu.roll(c, L - SLOTS, 1)
+    live = (lane < SLOTS) & (lane < pltpu.roll(c, 2 * SLOTS, 1)) & ((r & 3) == z)
+    dz = jnp.where(sub == 1, 3, jnp.where(sub == 2, 1, jnp.where(sub == 3, 2, 0)))
+    dx = (((r & 15) >> 2) - x) & 3
+    dy = ((c >> 1) - y) & 3
+    even = (c & 1) == 0
+    u1 = jnp.where(even, dy, dz)
+    u2 = jnp.where(even, dz, dy)
+    i1 = (4 - u1) & 3
+    g2 = jnp.where(u2 == 3, 1, jnp.where(u2 == 1, 2, jnp.where(u2 == 2, jnp.where(i1 >= 2, 4, 3), 0)))
+    source = g2 + jnp.where((c & 1) == core, 0, 5)
+    row = jnp.where(g2 == 4, i1 - 2, i1)
+    back = jnp.where(core == 0, 3, 1)
+    rs = jnp.where(dx == 0, 0, jnp.where(dx == 2, 3, jnp.where(dx == back, 1, 2)))
+    i = (r >> 4) & 3
+    code = source | (row << 4) | (rs << 6) | (i << 8) | (((z + dz) & 3) << 10) | (lane << 12)
+    lint[...] = jnp.where(live, code, -1)
     move = pltpu.make_async_copy(lint, lists, lsem)
     move.start()
     move.wait()
-    n = jnp.int32(0)
-    for k, dz in enumerate((0, 3, 1, 2)):
-        zj = (z + dz) & 3
-
-        def scan(s, n, k=k, dz=dz, zj=zj):
-            c = lists[k, s]
-            r = lists[k, SLOTS + s]
-            mine = (r & 3) == z
-
-            @pl.when(mine)
-            def _():
-                dx = (((r & 15) >> 2) - x) & 3
-                kc = c & 1
-                dy = ((c >> 1) - y) & 3
-                u1 = jnp.where(kc == 0, dy, dz)
-                u2 = jnp.where(kc == 0, dz, dy)
-                i1 = (4 - u1) & 3
-                g2 = (u2 == 3) * 1 + (u2 == 1) * 2 + (u2 == 2) * 3
-                g2 = jnp.where((g2 == 3) & (i1 >= 2), 4, g2)
-                i = r >> 4
-                back = jnp.where(core == 0, 3, 1)
-                rs = jnp.where(dx == 0, 0, jnp.where(dx == 2, 3, jnp.where(dx == back, 1, 2)))
-                todo[0, n] = g2 + jnp.where(kc == core, 0, 5)
-                todo[1, n] = jnp.where(g2 == 4, i1 - 2, i1)
-                todo[2, n] = rs * 2 + jnp.where(i == 0, 0, 1)
-                todo[3, n] = jnp.maximum(i - 1, 0)
-                todo[4, n] = i
-                todo[5, n] = zj
-                todo[6, n] = s
-
-            return n + jnp.where(mine, 1, 0)
-
-        n = lax.fori_loop(0, lists[k, 2 * SLOTS], scan, n)
-
-    lane = lax.broadcasted_iota(jnp.int32, (8, L), 1)
-    sub = lax.broadcasted_iota(jnp.int32, (8, L), 0)
+
+    def scan(s, n):
+        for k in range(4):
+            v = lists[k, s]
+            todo[n] = v
+            n = n + jnp.where(v >= 0, 1, 0)
+        return n
+
+    n = lax.fori_loop(0, SLOTS, scan, jnp.int32(0))
     eye = lax.broadcasted_iota(jnp.int32, (L, L), 0) == lax.broadcasted_iota(jnp.int32, (L, L), 1)
 
+    def choose(v, low, high, act):
+        if high - low == 1:
+            act(low)
+            return
+        middle = (low + high) // 2
+
+        @pl.when(v < middle)
+        def _():
+            choose(v, low, middle, act)
+
+        @pl.when(v >= middle)
+        def _():
+            choose(v, middle, high, act)
+
     def fetch(t, b):
-        for k, buf in enumerate(cands):
-            @pl.when(todo[0, t] == k)
-            def _(buf=buf):
-                cbuf[b] = buf[todo[1, t]]
-        for k, buf in enumerate(blocks):
-            @pl.when(todo[2, t] == k)
-            def _(k=k, buf=buf):
-                if k % 2:
-                    rbuf[b] = buf[pl.ds(pl.multiple_of(todo[3, t] * L, L), L), :]
-                else:
-                    rbuf[b] = buf[0:L, :]
-                wbuf[b] = blocks[k - k % 2][L : L + 16, 0:L]
+        code = todo[t]
+        row = (code >> 4) & 3
+        i = (code >> 8) & 3
+        at = pl.multiple_of(jnp.where(i < AHEAD, i, i - AHEAD) * L, L)
+
+        def take_cand(k):
+            cbuf[b] = cands[k][row]
+
+        def take_ref(k):
+            rbuf[b] = blocks[k][pl.ds(at, L), :]
+            wbuf[b] = blocks[k - k % 2][AHEAD * L : AHEAD * L + 16, 0:L]
+
+        choose(code & 15, 0, 10, take_cand)
+        choose(((code >> 6) & 3) * 2 + jnp.where(i < AHEAD, 0, 1), 0, 8, take_ref)
 
     def one(t, b):
         similar = lax.dot_general(
@@ -227,7 +255,7 @@
         cw = cbuf[b, L:, 0:L].astype(jnp.float32)[0:1, :]
         wide = wbuf[b].astype(jnp.float32)
         rsub = lax.broadcasted_iota(jnp.int32, (16, L), 0)
-        rw = jnp.sum(jnp.where(rsub == todo[4, t], wide, 0.0), axis=0, keepdims=True)
+        rw = jnp.sum(jnp.where(rsub == ((todo[t] >> 8) & 3), wide, 0.0), axis=0, keepdims=True)
         cw_col = jnp.sum(jnp.where(eye, cw, 0.0), axis=1, keepdims=True)
         row_best = jnp.max(jnp.where(rw > 0, similar, -10000.0), axis=1, keepdims=True)
         col_best = jnp.max(jnp.where(cw_col > 0, similar, -10000.0), axis=0, keepdims=True)
@@ -249,11 +277,11 @@
 
         scores = []
         for k in range(GROUP):
-            t = jnp.minimum(g * GROUP + k, n - 1)
+            t = g * GROUP + k
             scores.append((t, g * GROUP + k < n, one(t, k)))
         for t, real, (p, r, f) in scores:
             three = jnp.where(lane < 32, p, jnp.where(lane < 64, r, f))
-            here = (sub == todo[5, t]) & ((lane & 31) == todo[6, t]) & (lane < 96) & real
+            here = (sub == ((todo[t] >> 10) & 3)) & ((lane & 31) == ((todo[t] >> 12) & 31)) & (lane < 96) & real
             acc = jnp.where(here, three, acc)
             rows = jnp.where(sub == 0, p, jnp.where(sub == 1, r, f))
             total = total + jnp.where(real, rows, 0.0)
@@ -294,7 +322,7 @@
             pltpu.VMEM((GROUP, L + 16, D), jnp.bfloat16),
             pltpu.VMEM((GROUP, L, D), jnp.bfloat16),
             pltpu.VMEM((GROUP, 16, L), jnp.bfloat16),
-            pltpu.SMEM((8, 4 * SLOTS), jnp.int32),
+            pltpu.SMEM((4 * SLOTS + GROUP,), jnp.int32),
             pltpu.VMEM((8, L), jnp.int32),
             pltpu.SMEM((8, L), jnp.int32),
             pltpu.SemaphoreType.DMA,
@@ -331,25 +359,28 @@
         pair_ref.reshape(1, SLOTS),
         table,
     )
-    cand, refs_a, refs_b = encode(words, cand_hidden.reshape(1, L, D), hidden, layer)
-    back_a = send(refs_a, along_x(1))
-    ahead_a = send(refs_a, along_x(-1))
+    cand, refs_a = encode((0, 1, 2), cand_hidden.reshape(1, L, D), hidden, words, layer)
     c1 = send(cand, along_first(1))
     c3 = send(cand, along_first(-1))
     c2 = send(cand, along_first(2))
-    back_a, ahead_a, c1, c2, c3, pos = lax.optimization_barrier((back_a, ahead_a, c1, c2, c3, pos))
+    back_a = send(refs_a, along_x(1))
+    ahead_a = send(refs_a, along_x(-1))
+    c1, c2, c3, hidden, pos = lax.optimization_barrier((c1, c2, c3, hidden, pos))
+    own4 = jnp.stack([cand, c1, c2, c3])
+    d1 = send(own4, along_second(1))
+    d2 = send(own4, along_second(-1))
+    (refs_b,) = encode((3,), None, hidden, (), layer)
+    back_a, ahead_a, refs_b = lax.optimization_barrier((back_a, ahead_a, refs_b))
     back_b = send(refs_b, along_x(1))
     ahead_b = send(refs_b, along_x(-1))
     far_a = send(back_a, along_x(1))
-    own4 = jnp.stack([cand, c1, c2, c3])
-    d1 = send(own4, along_second(1))
-    d2 = send(own4, along_second(-1))
-    d1, d2, back_b, ahead_b, far_a = lax.optimization_barrier((d1, d2, back_b, ahead_b, far_a))
     d3 = send(d1[:2], along_second(1))
     d4 = send(d2[2:], along_second(-1))
+    own4, d1, d2, back_b, ahead_b = lax.optimization_barrier((own4, d1, d2, back_b, ahead_b))
     far_b = send(back_b, along_x(1))
-    d3, d4, far_b = lax.optimization_barrier((d3, d4, far_b))
-    others = [send(v, to_other_core) for v in (own4, d1, d2, d3, d4)]
+    others = [send(v, to_other_core) for v in (own4, d1, d2)]
+    d3, d4, far_a, far_b = lax.optimization_barrier((d3, d4, far_a, far_b))
+    others += [send(v, to_other_core) for v in (d3, d4)]
     cands = [own4, d1, d2, d3, d4, *others]
     blocks = [refs_a, refs_b, back_a, back_b, ahead_a, ahead_b, far_a, far_b]
     payload = score_pairs(pos, count, [*cands, *blocks])

time: 117 us -> 110 us (0.940); the launches traced: 114 us -> 110 us
  waiting for transfers between devices: 39.8 us -> 26.6 us
  starting transfers between devices: 22.2 us -> 27.7 us
  Pallas kernels: 28.3 us -> 33.2 us
  blocking collectives: 19.1 us -> 17.3 us
    ppermute x18, waiting for transfers between devices: 39.8 us -> 26.6 us  [send(): lax.ppermute(value, AXES, [(number(*a), number(*where(*a))) for a in GRID])]
    pallas_call x1 -> x2, Pallas kernels: 18.5 us -> 24.7 us  [encode(): pl.pallas_call(functools.partial(encode_kernel, n_cand, picks, bool(words...]
    ppermute x18, starting transfers between devices: 22.2 us -> 27.7 us  [send(): lax.ppermute(value, AXES, [(number(*a), number(*where(*a))) for a in GRID])]
    all_to_all x1, blocking collectives: 19.1 us -> 17.3 us  [on_device(): got = lax.all_to_all(payload, AXES, 0, 0)]
    pallas_call x1, Pallas kernels: 8.19 us -> 6.88 us  [score_pairs(): pl.pallas_call(pair_kernel, in_specs=[smem] * 2 + [vmem] * len(blocks), o...]
  transfers between devices with their start and end apart: 18 -> 18, of which waited for: 9 -> 9; matrix products, arithmetic and copies ran while one was open for 0% -> 1% of each run, Pallas kernels for 0% -> 8%
where the time goes in v5:
time: 110 us
  Pallas kernels  33.2 us (30%)
  starting transfers between devices  27.7 us (25%)
  waiting for transfers between devices  26.6 us (24%)
  blocking collectives  17.3 us (16%)
  between operations  2 us (2%)
  local copies, waits for them, and re-layouts  1.7 us (2%)
  other arithmetic  1.19 us (1%)
    ppermute x18, starting transfers between devices, send(): lax.ppermute(value, AXES, [(number(*a), number(*where(*a))) for a in GRID])  27.7 us
    ppermute x18, waiting for transfers between devices, send(): lax.ppermute(value, AXES, [(number(*a), number(*where(*a))) for a in GRID])  26.6 us
    pallas_call x2, Pallas kernels, encode(): pl.pallas_call(functools.partial(encode_kernel, n_cand, picks, bool(words...  24.7 us
    all_to_all x1, blocking collectives, on_device(): got = lax.all_to_all(payload, AXES, 0, 0)  17.3 us
    pallas_call x1, Pallas kernels, score_pairs(): pl.pallas_call(pair_kernel, in_specs=[smem] * 2 + [vmem] * len(blocks), o...  6.88 us
  transfers between devices with their start and end apart: 18, of which 9 were waited for; matrix products, arithmetic and copies ran while one was open for 1% of the time, Pallas kernels for 8%

profile of v5, /device:TPU:1, one launch (start us, length us, event | category | flops | bytes accessed | tf_op | source)
XLA Modules:
  0.0 109.6 jit_solution(9379913334322692109)
XLA Ops:
  1.9 1.6 %pad_bitcast_fusion.refs_7_ = f32[400,128]{1,0:T(8,128)} fusion(f32[50265]{0:T(1024)} %param.22), kind=kLoop, calls=%fused_computation.1 | loop fusion | bytes 405860 | tf_op jit(solution)/shard_map/reshape | solution.py:339
  3.5 15.6 %encode.2 = (bf16[144,1024]{1,0:T(8,128)(2,1)}, bf16[400,1024]{1,0:T(8,128)(2,1)}) custom-call(s32[1]{0:T(128)} %bitcast.24.refs_0_, s32[4]{0:T(128)} %bitcast.43, s32[1]{0:T(128)} %bitcast.25.refs_2_, s32[1,128]{1,0:T(1,128)} %bitcast.44, s32[4,128]{1,0:T(4,128)} %bitcast.42, s32[1,32]{1,0:T(1,128)} %bitcast.45, s32[1,32]{1,0:T(1,128)} %bitcast.46, ...), custom_call_target="tpu_custom_call" | custom-call | flops 8589934592 | bytes 17825792 | tf_op jit(solution)/shard_map/encode/pallas_call | solution.py:142
  19.2 4.6 %collective-permute-start.2 = (bf16[144,1024]{1,0:T(8,128)(2,1)}, bf16[144,1024]{1,0:T(8,128)(2,1)S(1)}, u32[]{:S(2)}, u32[]{:S(2)}) collective-permute-start(bf16[144,1024]{1,0:T(8,128)(2,1)} %get-tuple-element.23), channel_id=1, source_target_pairs={{0,96},{1,97},{2,98},{3,99},{4,100},{5,101},{6,102},{7,103},{8,104... | collective-permute-start | bytes 884744 | tf_op jit(solution)/shard_map/ppermute | solution.py:23
  23.8 0.0 collective-permute-start.1
  23.8 0.7 collective-permute-start
  24.5 1.2 %collective-permute-start.6 = (bf16[400,1024]{1,0:T(8,128)(2,1)}, bf16[400,1024]{1,0:T(8,128)(2,1)}, u32[]{:S(2)}, u32[]{:S(2)}) collective-permute-start(bf16[400,1024]{1,0:T(8,128)(2,1)} %get-tuple-element.28.refs_10_), channel_id=1, source_target_pairs={{0,12},{1,13},{2,14},{3,15},{4,0},{5,1},{6,2},{7,3},{8,4},{9,5},{1... | collective-permute-start | bytes 2457608 | tf_op jit(solution)/shard_map/ppermute | solution.py:23
  25.7 1.5 %collective-permute-start.5 = (bf16[400,1024]{1,0:T(8,128)(2,1)}, bf16[400,1024]{1,0:T(8,128)(2,1)}, u32[]{:S(2)}, u32[]{:S(2)}) collective-permute-start(bf16[400,1024]{1,0:T(8,128)(2,1)} %get-tuple-element.28.refs_10_), channel_id=1, source_target_pairs={{0,4},{1,5},{2,6},{3,7},{4,8},{5,9},{6,10},{7,11},{8,12},{9,13},{1... | collective-permute-start | bytes 2457608 | tf_op jit(solution)/shard_map/ppermute | solution.py:23
  27.2 0.1 pad_add_fusion.pos_ref
  27.2 3.7 %collective-permute-done.2 = bf16[144,1024]{1,0:T(8,128)(2,1)S(1)} collective-permute-done((bf16[144,1024]{1,0:T(8,128)(2,1)}, bf16[144,1024]{1,0:T(8,128)(2,1)S(1)}, u32[]{:S(2)}, u32[]{:S(2)}) %collective-permute-start.2) | collective-permute-done | bytes 294944 | tf_op jit(solution)/shard_map/ppermute | solution.py:23
  30.9 0.5 collective-permute-done.1
  31.4 2.9 %collective-permute-done = bf16[144,1024]{1,0:T(8,128)(2,1)S(1)} collective-permute-done((bf16[144,1024]{1,0:T(8,128)(2,1)}, bf16[144,1024]{1,0:T(8,128)(2,1)S(1)}, u32[]{:S(2)}, u32[]{:S(2)}) %collective-permute-start) | collective-permute-done | bytes 294944 | tf_op jit(solution)/shard_map/ppermute | solution.py:23
  34.3 1.1 %pad_maximum_fusion.refs_0_ = bf16[4,144,1024]{2,1,0:T(8,128)(2,1)S(1)} fusion(bf16[1,144,1024]{2,1,0:T(8,128)(2,1)S(1)} %bitcast.30, bf16[1,144,1024]{2,1,0:T(8,128)(2,1)S(1)} %bitcast.31, bf16[1,144,1024]{2,1,0:T(8,128)(2,1)S(1)} %bitcast.32, bf16[1,144,1024]{2,1,0:T(8,128)(2,1)} %bitcast.29), kind=kLoop, calls=%fused_computation | loop fusion | flops 1769472 | bytes 2359296 | tf_op jit(solution)/shard_map/stack | solution.py:369
  35.4 2.8 %collective-permute-start.4 = (bf16[4,144,1024]{2,1,0:T(8,128)(2,1)S(1)}, bf16[4,144,1024]{2,1,0:T(8,128)(2,1)S(1)}, u32[]{:S(2)}, u32[]{:S(2)}) collective-permute-start(bf16[4,144,1024]{2,1,0:T(8,128)(2,1)S(1)} %pad_maximum_fusion.refs_0_), channel_id=1, source_target_pairs={{0,3},{1,0},{2,1},{3,2},{4,7},{5,4},{6,5},{7,6},{8,11},{9,8},{10,9... | collective-permute-start | bytes 3538952 | tf_op jit(solution)/shard_map/ppermute | solution.py:23
  38.3 0.0 collective-permute-start.3
  38.3 9.0 %encode.3.refs_11_ = bf16[128,1024]{1,0:T(8,128)(2,1)} custom-call(bf16[4,128,1024]{2,1,0:T(8,128)(2,1)} %bitcast.28, bf16[1024,4096]{1,0:T(8,128)(2,1)} %refs_1_.1, f32[1,4096]{1,0:T(1,128)} %bitcast.34, bf16[4096,1024]{1,0:T(8,128)(2,1)} %refs_3_.1, f32[1,1024]{1,0:T(1,128)} %bitcast.36, f32[1,1024]{1,0:T(1,128)} %bitcast.38, f32[1,1024]{1,0:T(1,128)} %bitcast.40), custom_call_target="tpu_custom_call" | custom-call | flops 2147483648 | bytes 17825792 | tf_op jit(solution)/shard_map/encode/pallas_call | solution.py:142
  47.3 0.0 copy-start
  47.3 0.0 copy-start.1
  47.3 0.0 collective-permute-done.6.refs_14_
  47.3 0.0 collective-permute-done.5.refs_12_
  47.3 2.6 %collective-permute-start.11 = (bf16[400,1024]{1,0:T(8,128)(2,1)}, bf16[400,1024]{1,0:T(8,128)(2,1)S(1)}, u32[]{:S(2)}, u32[]{:S(2)}) collective-permute-start(bf16[400,1024]{1,0:T(8,128)(2,1)} %collective-permute-done.5.refs_12_), channel_id=1, source_target_pairs={{0,4},{1,5},{2,6},{3,7},{4,8},{5,9},{6,10},{7,11},{8,12},{9,13},{1... | collective-permute-start | bytes 2457608 | tf_op jit(solution)/shard_map/ppermute | solution.py:23
  49.9 0.0 collective-permute-start.8
  49.9 2.7 %collective-permute-start.7 = (bf16[128,1024]{1,0:T(8,128)(2,1)}, bf16[128,1024]{1,0:T(8,128)(2,1)S(1)}, u32[]{:S(2)}, u32[]{:S(2)}) collective-permute-start(bf16[128,1024]{1,0:T(8,128)(2,1)} %encode.3.refs_11_), channel_id=1, source_target_pairs={{0,4},{1,5},{2,6},{3,7},{4,8},{5,9},{6,10},{7,11},{8,12},{9,13},{1... | collective-permute-start | bytes 786440 | tf_op jit(solution)/shard_map/ppermute | solution.py:23
  52.5 6.8 %collective-permute-done.8.refs_15_ = bf16[128,1024]{1,0:T(8,128)(2,1)S(1)} collective-permute-done((bf16[128,1024]{1,0:T(8,128)(2,1)}, bf16[128,1024]{1,0:T(8,128)(2,1)S(1)}, u32[]{:S(2)}, u32[]{:S(2)}) %collective-permute-start.8) | collective-permute-done | bytes 262176 | tf_op jit(solution)/shard_map/ppermute | solution.py:23
  59.4 5.7 %collective-permute-done.7.refs_13_ = bf16[128,1024]{1,0:T(8,128)(2,1)S(1)} collective-permute-done((bf16[128,1024]{1,0:T(8,128)(2,1)}, bf16[128,1024]{1,0:T(8,128)(2,1)S(1)}, u32[]{:S(2)}, u32[]{:S(2)}) %collective-permute-start.7) | collective-permute-done | bytes 262176 | tf_op jit(solution)/shard_map/ppermute | solution.py:23
  65.1 0.0 collective-permute-done.4.refs_2_
  65.1 0.0 collective-permute-done.3.refs_1_
  65.1 3.0 %collective-permute-start.12 = (bf16[128,1024]{1,0:T(8,128)(2,1)S(1)}, bf16[128,1024]{1,0:T(8,128)(2,1)S(1)}, u32[]{:S(2)}, u32[]{:S(2)}) collective-permute-start(bf16[128,1024]{1,0:T(8,128)(2,1)S(1)} %collective-permute-done.7.refs_13_), channel_id=1, source_target_pairs={{0,4},{1,5},{2,6},{3,7},{4,8},{5,9},{6,10},{7,11},{8,12},{9,13},{1... | collective-permute-start | bytes 786440 | tf_op jit(solution)/shard_map/ppermute | solution.py:23
  68.1 2.7 %collective-permute-start.10 = (bf16[2,144,1024]{2,1,0:T(8,128)(2,1)S(1)}, bf16[2,144,1024]{2,1,0:T(8,128)(2,1)S(1)}, u32[]{:S(2)}, u32[]{:S(2)}) collective-permute-start(bf16[2,144,1024]{2,1,0:T(8,128)(2,1)S(1)} %slice.9), channel_id=1, source_target_pairs={{0,3},{1,0},{2,1},{3,2},{4,7},{5,4},{6,5},{7,6},{8,11},{9,8},{10,9... | collective-permute-start | bytes 1769480 | tf_op jit(solution)/shard_map/ppermute | solution.py:23
  70.9 0.1 collective-permute-start.9
  71.0 0.1 collective-permute-start.13
  71.1 0.0 collective-permute-done.11.refs_16_
  71.1 0.5 collective-permute-start.14
  71.6 0.0 collective-permute-done.12.refs_17_
  71.6 4.8 %collective-permute-start.15 = (bf16[4,144,1024]{2,1,0:T(8,128)(2,1)S(1)}, bf16[4,144,1024]{2,1,0:T(8,128)(2,1)S(1)}, u32[]{:S(2)}, u32[]{:S(2)}) collective-permute-start(bf16[4,144,1024]{2,1,0:T(8,128)(2,1)S(1)} %collective-permute-done.4.refs_2_), channel_id=1, source_target_pairs={{0,16},{1,17},{2,18},{3,19},{4,20},{5,21},{6,22},{7,23},{8,24},{9,... | collective-permute-start | bytes 3538952 | tf_op jit(solution)/shard_map/ppermute | solution.py:23
  76.4 1.3 %collective-permute-done.10.refs_4_ = bf16[2,144,1024]{2,1,0:T(8,128)(2,1)S(1)} collective-permute-done((bf16[2,144,1024]{2,1,0:T(8,128)(2,1)S(1)}, bf16[2,144,1024]{2,1,0:T(8,128)(2,1)S(1)}, u32[]{:S(2)}, u32[]{:S(2)}) %collective-permute-start.10) | collective-permute-done | bytes 589856 | tf_op jit(solution)/shard_map/ppermute | solution.py:23
  77.7 3.2 %collective-permute-done.9.refs_3_ = bf16[2,144,1024]{2,1,0:T(8,128)(2,1)S(1)} collective-permute-done((bf16[2,144,1024]{2,1,0:T(8,128)(2,1)S(1)}, bf16[2,144,1024]{2,1,0:T(8,128)(2,1)S(1)}, u32[]{:S(2)}, u32[]{:S(2)}) %collective-permute-start.9) | collective-permute-done | bytes 589856 | tf_op jit(solution)/shard_map/ppermute | solution.py:23
  80.9 0.1 collective-permute-start.16
  81.1 0.4 collective-permute-start.17
  81.4 0.0 collective-permute-done.13.refs_5_
  81.4 0.0 collective-permute-done.14.refs_6_
  81.4 0.0 collective-permute-done.15.refs_7_
  81.5 1.5 %collective-permute-done.16.refs_8_ = bf16[2,144,1024]{2,1,0:T(8,128)(2,1)S(1)} collective-permute-done((bf16[2,144,1024]{2,1,0:T(8,128)(2,1)S(1)}, bf16[2,144,1024]{2,1,0:T(8,128)(2,1)S(1)}, u32[]{:S(2)}, u32[]{:S(2)}) %collective-permute-start.16) | collective-permute-done | bytes 589856 | tf_op jit(solution)/shard_map/ppermute | solution.py:23
  82.9 0.8 collective-permute-done.17.refs_9_
  83.8 0.0 copy-done
  83.8 0.0 copy-done.1
  83.8 6.9 %score_pairs.1 = f32[128,1,128]{2,1,0:T(1,128)S(1)} custom-call(s32[4]{0:T(128)S(1)} %pad_add_fusion.pos_ref, s32[1]{0:T(128)} %bitcast.26.count_ref, bf16[4,144,1024]{2,1,0:T(8,128)(2,1)S(1)} %pad_maximum_fusion.refs_0_, bf16[4,144,1024]{2,1,0:T(8,128)(2,1)S(1)} %collective-permute-done.3.refs_1_, bf16[4,144,1024]{2,1,0:T(8,128)(2,1)S(1)} %collective-permute-done.4.refs_2_, ...), custom_call_target="tpu_custom_call" | custom-call | tf_op jit(solution)/shard_map/score_pairs/pallas_call | solution.py:316
  90.7 17.3 %all_to_all.5.got_ref = f32[128,1,128]{2,1,0:T(1,128)} all-to-all(f32[128,1,128]{2,1,0:T(1,128)S(1)} %score_pairs.1), channel_id=1, replica_groups=mesh['dp'=8,'prompt'=16] {'dp','prompt'}, dimensions={0} | all-to-all | bytes 131072 | tf_op jit(solution)/shard_map/all_to_all | solution.py:387
  107.9 1.6 %finish.1 = (f32[3,1,1,32]{3,2,1,0:T(1,128)}, f32[1,3]{1,0:T(1,128)}) custom-call(f32[128,1,128]{2,1,0:T(1,128)} %all_to_all.5.got_ref), custom_call_target="tpu_custom_call" | custom-call | tf_op jit(solution)/shard_map/finish/pallas_call | solution.py:388
  (2 shorter events, 0.1 us)
Async XLA Ops:
  19.2 11.7 %collective-permute-start.2 = (bf16[144,1024]{1,0:T(8,128)(2,1)}, bf16[144,1024]{1,0:T(8,128)(2,1)S(1)}, u32[]{:S(2)}, u32[]{:S(2)}) collective-permute-start(bf16[144,1024]{1,0:T(8,128)(2,1)} %get-tuple-element.23), channel_id=1, source_target_pairs={{0,96},{1,97},{2,98},{3,99},{4,100},{5,101},{6,102},{7,103},{8,104... | collective-permute-start | bytes 884744 | tf_op jit(solution)/shard_map/ppermute | solution.py:23
  23.8 7.6 %collective-permute-start.1 = (bf16[144,1024]{1,0:T(8,128)(2,1)}, bf16[144,1024]{1,0:T(8,128)(2,1)S(1)}, u32[]{:S(2)}, u32[]{:S(2)}) collective-permute-start(bf16[144,1024]{1,0:T(8,128)(2,1)} %get-tuple-element.23), channel_id=1, source_target_pairs={{0,64},{1,65},{2,66},{3,67},{4,68},{5,69},{6,70},{7,71},{8,72},{9,... | collective-permute-start | bytes 884744 | tf_op jit(solution)/shard_map/ppermute | solution.py:23
  23.8 10.6 %collective-permute-start = (bf16[144,1024]{1,0:T(8,128)(2,1)}, bf16[144,1024]{1,0:T(8,128)(2,1)S(1)}, u32[]{:S(2)}, u32[]{:S(2)}) collective-permute-start(bf16[144,1024]{1,0:T(8,128)(2,1)} %get-tuple-element.23), channel_id=1, source_target_pairs={{0,32},{1,33},{2,34},{3,35},{4,36},{5,37},{6,38},{7,39},{8,40},{9,... | collective-permute-start | bytes 884744 | tf_op jit(solution)/shard_map/ppermute | solution.py:23
  24.5 22.8 %collective-permute-start.6 = (bf16[400,1024]{1,0:T(8,128)(2,1)}, bf16[400,1024]{1,0:T(8,128)(2,1)}, u32[]{:S(2)}, u32[]{:S(2)}) collective-permute-start(bf16[400,1024]{1,0:T(8,128)(2,1)} %get-tuple-element.28.refs_10_), channel_id=1, source_target_pairs={{0,12},{1,13},{2,14},{3,15},{4,0},{5,1},{6,2},{7,3},{8,4},{9,5},{1... | collective-permute-start | bytes 2457608 | tf_op jit(solution)/shard_map/ppermute | solution.py:23
  25.7 21.6 %collective-permute-start.5 = (bf16[400,1024]{1,0:T(8,128)(2,1)}, bf16[400,1024]{1,0:T(8,128)(2,1)}, u32[]{:S(2)}, u32[]{:S(2)}) collective-permute-start(bf16[400,1024]{1,0:T(8,128)(2,1)} %get-tuple-element.28.refs_10_), channel_id=1, source_target_pairs={{0,4},{1,5},{2,6},{3,7},{4,8},{5,9},{6,10},{7,11},{8,12},{9,13},{1... | collective-permute-start | bytes 2457608 | tf_op jit(solution)/shard_map/ppermute | solution.py:23
  35.4 29.6 %collective-permute-start.4 = (bf16[4,144,1024]{2,1,0:T(8,128)(2,1)S(1)}, bf16[4,144,1024]{2,1,0:T(8,128)(2,1)S(1)}, u32[]{:S(2)}, u32[]{:S(2)}) collective-permute-start(bf16[4,144,1024]{2,1,0:T(8,128)(2,1)S(1)} %pad_maximum_fusion.refs_0_), channel_id=1, source_target_pairs={{0,3},{1,0},{2,1},{3,2},{4,7},{5,4},{6,5},{7,6},{8,11},{9,8},{10,9... | collective-permute-start | bytes 3538952 | tf_op jit(solution)/shard_map/ppermute | solution.py:23
  38.3 26.8 %collective-permute-start.3 = (bf16[4,144,1024]{2,1,0:T(8,128)(2,1)S(1)}, bf16[4,144,1024]{2,1,0:T(8,128)(2,1)S(1)}, u32[]{:S(2)}, u32[]{:S(2)}) collective-permute-start(bf16[4,144,1024]{2,1,0:T(8,128)(2,1)S(1)} %pad_maximum_fusion.refs_0_), channel_id=1, source_target_pairs={{0,1},{1,2},{2,3},{3,0},{4,5},{5,6},{6,7},{7,4},{8,9},{9,10},{10,1... | collective-permute-start | bytes 3538952 | tf_op jit(solution)/shard_map/ppermute | solution.py:23
  47.3 36.5 %copy-start = (bf16[128,1024]{1,0:T(8,128)(2,1)S(1)}, bf16[128,1024]{1,0:T(8,128)(2,1)}, u32[]{:S(2)}) copy-start(bf16[128,1024]{1,0:T(8,128)(2,1)} %encode.3.refs_11_) | copy-start | bytes 786436
  47.3 36.5 %copy-start.1 = (bf16[400,1024]{1,0:T(8,128)(2,1)S(1)}, bf16[400,1024]{1,0:T(8,128)(2,1)}, u32[]{:S(2)}) copy-start(bf16[400,1024]{1,0:T(8,128)(2,1)} %get-tuple-element.28.refs_10_) | copy-start | bytes 2457604
  47.3 23.8 %collective-permute-start.11 = (bf16[400,1024]{1,0:T(8,128)(2,1)}, bf16[400,1024]{1,0:T(8,128)(2,1)S(1)}, u32[]{:S(2)}, u32[]{:S(2)}) collective-permute-start(bf16[400,1024]{1,0:T(8,128)(2,1)} %collective-permute-done.5.refs_12_), channel_id=1, source_target_pairs={{0,4},{1,5},{2,6},{3,7},{4,8},{5,9},{6,10},{7,11},{8,12},{9,13},{1... | collective-permute-start | bytes 2457608 | tf_op jit(solution)/shard_map/ppermute | solution.py:23
  49.9 9.5 %collective-permute-start.8 = (bf16[128,1024]{1,0:T(8,128)(2,1)}, bf16[128,1024]{1,0:T(8,128)(2,1)S(1)}, u32[]{:S(2)}, u32[]{:S(2)}) collective-permute-start(bf16[128,1024]{1,0:T(8,128)(2,1)} %encode.3.refs_11_), channel_id=1, source_target_pairs={{0,12},{1,13},{2,14},{3,15},{4,0},{5,1},{6,2},{7,3},{8,4},{9,5},{1... | collective-permute-start | bytes 786440 | tf_op jit(solution)/shard_map/ppermute | solution.py:23
  49.9 15.2 %collective-permute-start.7 = (bf16[128,1024]{1,0:T(8,128)(2,1)}, bf16[128,1024]{1,0:T(8,128)(2,1)S(1)}, u32[]{:S(2)}, u32[]{:S(2)}) collective-permute-start(bf16[128,1024]{1,0:T(8,128)(2,1)} %encode.3.refs_11_), channel_id=1, source_target_pairs={{0,4},{1,5},{2,6},{3,7},{4,8},{5,9},{6,10},{7,11},{8,12},{9,13},{1... | collective-permute-start | bytes 786440 | tf_op jit(solution)/shard_map/ppermute | solution.py:23
  65.1 6.5 %collective-permute-start.12 = (bf16[128,1024]{1,0:T(8,128)(2,1)S(1)}, bf16[128,1024]{1,0:T(8,128)(2,1)S(1)}, u32[]{:S(2)}, u32[]{:S(2)}) collective-permute-start(bf16[128,1024]{1,0:T(8,128)(2,1)S(1)} %collective-permute-done.7.refs_13_), channel_id=1, source_target_pairs={{0,4},{1,5},{2,6},{3,7},{4,8},{5,9},{6,10},{7,11},{8,12},{9,13},{1... | collective-permute-start | bytes 786440 | tf_op jit(solution)/shard_map/ppermute | solution.py:23
  68.1 9.6 %collective-permute-start.10 = (bf16[2,144,1024]{2,1,0:T(8,128)(2,1)S(1)}, bf16[2,144,1024]{2,1,0:T(8,128)(2,1)S(1)}, u32[]{:S(2)}, u32[]{:S(2)}) collective-permute-start(bf16[2,144,1024]{2,1,0:T(8,128)(2,1)S(1)} %slice.9), channel_id=1, source_target_pairs={{0,3},{1,0},{2,1},{3,2},{4,7},{5,4},{6,5},{7,6},{8,11},{9,8},{10,9... | collective-permute-start | bytes 1769480 | tf_op jit(solution)/shard_map/ppermute | solution.py:23
  70.9 10.0 %collective-permute-start.9 = (bf16[2,144,1024]{2,1,0:T(8,128)(2,1)S(1)}, bf16[2,144,1024]{2,1,0:T(8,128)(2,1)S(1)}, u32[]{:S(2)}, u32[]{:S(2)}) collective-permute-start(bf16[2,144,1024]{2,1,0:T(8,128)(2,1)S(1)} %slice.8), channel_id=1, source_target_pairs={{0,1},{1,2},{2,3},{3,0},{4,5},{5,6},{6,7},{7,4},{8,9},{9,10},{10,1... | collective-permute-start | bytes 1769480 | tf_op jit(solution)/shard_map/ppermute | solution.py:23
  71.0 10.4 %collective-permute-start.13 = (bf16[4,144,1024]{2,1,0:T(8,128)(2,1)S(1)}, bf16[4,144,1024]{2,1,0:T(8,128)(2,1)S(1)}, u32[]{:S(2)}, u32[]{:S(2)}) collective-permute-start(bf16[4,144,1024]{2,1,0:T(8,128)(2,1)S(1)} %pad_maximum_fusion.refs_0_), channel_id=1, source_target_pairs={{0,16},{1,17},{2,18},{3,19},{4,20},{5,21},{6,22},{7,23},{8,24},{9,... | collective-permute-start | bytes 3538952 | tf_op jit(solution)/shard_map/ppermute | solution.py:23
  71.1 10.3 %collective-permute-start.14 = (bf16[4,144,1024]{2,1,0:T(8,128)(2,1)S(1)}, bf16[4,144,1024]{2,1,0:T(8,128)(2,1)S(1)}, u32[]{:S(2)}, u32[]{:S(2)}) collective-permute-start(bf16[4,144,1024]{2,1,0:T(8,128)(2,1)S(1)} %collective-permute-done.3.refs_1_), channel_id=1, source_target_pairs={{0,16},{1,17},{2,18},{3,19},{4,20},{5,21},{6,22},{7,23},{8,24},{9,... | collective-permute-start | bytes 3538952 | tf_op jit(solution)/shard_map/ppermute | solution.py:23
  71.6 9.9 %collective-permute-start.15 = (bf16[4,144,1024]{2,1,0:T(8,128)(2,1)S(1)}, bf16[4,144,1024]{2,1,0:T(8,128)(2,1)S(1)}, u32[]{:S(2)}, u32[]{:S(2)}) collective-permute-start(bf16[4,144,1024]{2,1,0:T(8,128)(2,1)S(1)} %collective-permute-done.4.refs_2_), channel_id=1, source_target_pairs={{0,16},{1,17},{2,18},{3,19},{4,20},{5,21},{6,22},{7,23},{8,24},{9,... | collective-permute-start | bytes 3538952 | tf_op jit(solution)/shard_map/ppermute | solution.py:23
  80.9 2.0 %collective-permute-start.16 = (bf16[2,144,1024]{2,1,0:T(8,128)(2,1)S(1)}, bf16[2,144,1024]{2,1,0:T(8,128)(2,1)S(1)}, u32[]{:S(2)}, u32[]{:S(2)}) collective-permute-start(bf16[2,144,1024]{2,1,0:T(8,128)(2,1)S(1)} %collective-permute-done.9.refs_3_), channel_id=1, source_target_pairs={{0,16},{1,17},{2,18},{3,19},{4,20},{5,21},{6,22},{7,23},{8,24},{9,... | collective-permute-start | bytes 1769480 | tf_op jit(solution)/shard_map/ppermute | solution.py:23
  81.1 2.7 %collective-permute-start.17 = (bf16[2,144,1024]{2,1,0:T(8,128)(2,1)S(1)}, bf16[2,144,1024]{2,1,0:T(8,128)(2,1)S(1)}, u32[]{:S(2)}, u32[]{:S(2)}) collective-permute-start(bf16[2,144,1024]{2,1,0:T(8,128)(2,1)S(1)} %collective-permute-done.10.refs_4_), channel_id=1, source_target_pairs={{0,16},{1,17},{2,18},{3,19},{4,20},{5,21},{6,22},{7,23},{8,24},{9,... | collective-permute-start | bytes 1769480 | tf_op jit(solution)/shard_map/ppermute | solution.py:23

commit v6 on v5

--- a/solution.py
+++ b/solution.py
@@ -376,10 +376,10 @@
     far_a = send(back_a, along_x(1))
     d3 = send(d1[:2], along_second(1))
     d4 = send(d2[2:], along_second(-1))
-    own4, d1, d2, back_b, ahead_b = lax.optimization_barrier((own4, d1, d2, back_b, ahead_b))
+    own4, d1, d2 = lax.optimization_barrier((own4, d1, d2))
+    others = [send(v, to_other_core) for v in (own4, d1, d2)]
+    d3, d4, far_a, back_b, ahead_b = lax.optimization_barrier((d3, d4, far_a, back_b, ahead_b))
     far_b = send(back_b, along_x(1))
-    others = [send(v, to_other_core) for v in (own4, d1, d2)]
-    d3, d4, far_a, far_b = lax.optimization_barrier((d3, d4, far_a, far_b))
     others += [send(v, to_other_core) for v in (d3, d4)]
     cands = [own4, d1, d2, d3, d4, *others]
     blocks = [refs_a, refs_b, back_a, back_b, ahead_a, ahead_b, far_a, far_b]

time: 110 us -> 104 us (0.945)
  waiting for transfers between devices: 26.6 us -> 20.8 us
  Pallas kernels: 33.2 us -> 34.7 us
  blocking collectives: 17.3 us -> 15.8 us
    ppermute x18, waiting for transfers between devices: 26.6 us -> 20.8 us  [send(): lax.ppermute(value, AXES, [(number(*a), number(*where(*a))) for a in GRID])]
    pallas_call x1, Pallas kernels: 6.88 us -> 8.41 us  [score_pairs(): pl.pallas_call(pair_kernel, in_specs=[smem] * 2 + [vmem] * len(blocks), o...]
    all_to_all x1, blocking collectives: 17.3 us -> 15.8 us  [on_device(): got = lax.all_to_all(payload, AXES, 0, 0)]
  transfers between devices with their start and end apart: 18 -> 18, of which waited for: 9 -> 7; matrix products, arithmetic and copies ran while one was open for 1% -> 1% of each run, Pallas kernels for 8% -> 9%
where the time goes in v6:
time: 104 us
  Pallas kernels  34.7 us (33%)
  starting transfers between devices  28.2 us (27%)
  waiting for transfers between devices  20.8 us (20%)
  blocking collectives  15.8 us (15%)
  between operations  2 us (2%)
  local copies, waits for them, and re-layouts  1.7 us (2%)
  other arithmetic  1.19 us (1%)
    ppermute x18, starting transfers between devices, send(): lax.ppermute(value, AXES, [(number(*a), number(*where(*a))) for a in GRID])  28.2 us
    pallas_call x2, Pallas kernels, encode(): pl.pallas_call(functools.partial(encode_kernel, n_cand, picks, bool(words...  24.7 us
    ppermute x18, waiting for transfers between devices, send(): lax.ppermute(value, AXES, [(number(*a), number(*where(*a))) for a in GRID])  20.8 us
    all_to_all x1, blocking collectives, on_device(): got = lax.all_to_all(payload, AXES, 0, 0)  15.8 us
    pallas_call x1, Pallas kernels, score_pairs(): pl.pallas_call(pair_kernel, in_specs=[smem] * 2 + [vmem] * len(blocks), o...  8.41 us
  transfers between devices with their start and end apart: 18, of which 7 were waited for; matrix products, arithmetic and copies ran while one was open for 1% of the time, Pallas kernels for 9%

profile of v6, /device:TPU:1, one launch (start us, length us, event | category | flops | bytes accessed | tf_op | source)
XLA Modules:
  0.0 104.4 jit_solution(12415902507784687862)
XLA Ops:
  1.9 1.6 %pad_bitcast_fusion.refs_7_ = f32[400,128]{1,0:T(8,128)} fusion(f32[50265]{0:T(1024)} %param.22), kind=kLoop, calls=%fused_computation.1 | loop fusion | bytes 405860 | tf_op jit(solution)/shard_map/reshape | solution.py:339
  3.5 15.6 %encode.2 = (bf16[144,1024]{1,0:T(8,128)(2,1)}, bf16[400,1024]{1,0:T(8,128)(2,1)}) custom-call(s32[1]{0:T(128)} %bitcast.24.refs_0_, s32[4]{0:T(128)} %bitcast.43, s32[1]{0:T(128)} %bitcast.25.refs_2_, s32[1,128]{1,0:T(1,128)} %bitcast.44, s32[4,128]{1,0:T(4,128)} %bitcast.42, s32[1,32]{1,0:T(1,128)} %bitcast.45, s32[1,32]{1,0:T(1,128)} %bitcast.46, ...), custom_call_target="tpu_custom_call" | custom-call | flops 8589934592 | bytes 17825792 | tf_op jit(solution)/shard_map/encode/pallas_call | solution.py:142
  19.2 4.6 %collective-permute-start.2 = (bf16[144,1024]{1,0:T(8,128)(2,1)}, bf16[144,1024]{1,0:T(8,128)(2,1)S(1)}, u32[]{:S(2)}, u32[]{:S(2)}) collective-permute-start(bf16[144,1024]{1,0:T(8,128)(2,1)} %get-tuple-element.22), channel_id=1, source_target_pairs={{0,96},{1,97},{2,98},{3,99},{4,100},{5,101},{6,102},{7,103},{8,104... | collective-permute-start | bytes 884744 | tf_op jit(solution)/shard_map/ppermute | solution.py:23
  23.8 0.0 collective-permute-start.1
  23.8 0.7 collective-permute-start
  24.5 1.2 %collective-permute-start.8 = (bf16[400,1024]{1,0:T(8,128)(2,1)}, bf16[400,1024]{1,0:T(8,128)(2,1)}, u32[]{:S(2)}, u32[]{:S(2)}) collective-permute-start(bf16[400,1024]{1,0:T(8,128)(2,1)} %get-tuple-element.30.refs_10_), channel_id=1, source_target_pairs={{0,12},{1,13},{2,14},{3,15},{4,0},{5,1},{6,2},{7,3},{8,4},{9,5},{1... | collective-permute-start | bytes 2457608 | tf_op jit(solution)/shard_map/ppermute | solution.py:23
  25.7 1.5 %collective-permute-start.7 = (bf16[400,1024]{1,0:T(8,128)(2,1)}, bf16[400,1024]{1,0:T(8,128)(2,1)}, u32[]{:S(2)}, u32[]{:S(2)}) collective-permute-start(bf16[400,1024]{1,0:T(8,128)(2,1)} %get-tuple-element.30.refs_10_), channel_id=1, source_target_pairs={{0,4},{1,5},{2,6},{3,7},{4,8},{5,9},{6,10},{7,11},{8,12},{9,13},{1... | collective-permute-start | bytes 2457608 | tf_op jit(solution)/shard_map/ppermute | solution.py:23
  27.2 0.1 pad_add_fusion.pos_ref
  27.2 3.7 %collective-permute-done.2 = bf16[144,1024]{1,0:T(8,128)(2,1)S(1)} collective-permute-done((bf16[144,1024]{1,0:T(8,128)(2,1)}, bf16[144,1024]{1,0:T(8,128)(2,1)S(1)}, u32[]{:S(2)}, u32[]{:S(2)}) %collective-permute-start.2) | collective-permute-done | bytes 294944 | tf_op jit(solution)/shard_map/ppermute | solution.py:23
  30.9 0.5 collective-permute-done.1
  31.4 2.9 %collective-permute-done = bf16[144,1024]{1,0:T(8,128)(2,1)S(1)} collective-permute-done((bf16[144,1024]{1,0:T(8,128)(2,1)}, bf16[144,1024]{1,0:T(8,128)(2,1)S(1)}, u32[]{:S(2)}, u32[]{:S(2)}) %collective-permute-start) | collective-permute-done | bytes 294944 | tf_op jit(solution)/shard_map/ppermute | solution.py:23
  34.3 1.1 %pad_maximum_fusion.refs_0_ = bf16[4,144,1024]{2,1,0:T(8,128)(2,1)S(1)} fusion(bf16[1,144,1024]{2,1,0:T(8,128)(2,1)S(1)} %bitcast.30, bf16[1,144,1024]{2,1,0:T(8,128)(2,1)S(1)} %bitcast.31, bf16[1,144,1024]{2,1,0:T(8,128)(2,1)S(1)} %bitcast.32, bf16[1,144,1024]{2,1,0:T(8,128)(2,1)} %bitcast.29), kind=kLoop, calls=%fused_computation | loop fusion | flops 1769472 | bytes 2359296 | tf_op jit(solution)/shard_map/stack | solution.py:369
  35.4 2.8 %collective-permute-start.4 = (bf16[4,144,1024]{2,1,0:T(8,128)(2,1)S(1)}, bf16[4,144,1024]{2,1,0:T(8,128)(2,1)S(1)}, u32[]{:S(2)}, u32[]{:S(2)}) collective-permute-start(bf16[4,144,1024]{2,1,0:T(8,128)(2,1)S(1)} %pad_maximum_fusion.refs_0_), channel_id=1, source_target_pairs={{0,3},{1,0},{2,1},{3,2},{4,7},{5,4},{6,5},{7,6},{8,11},{9,8},{10,9... | collective-permute-start | bytes 3538952 | tf_op jit(solution)/shard_map/ppermute | solution.py:23
  38.3 0.0 collective-permute-start.3
  38.3 9.0 %encode.3.refs_11_ = bf16[128,1024]{1,0:T(8,128)(2,1)} custom-call(bf16[4,128,1024]{2,1,0:T(8,128)(2,1)} %bitcast.28, bf16[1024,4096]{1,0:T(8,128)(2,1)} %refs_1_.1, f32[1,4096]{1,0:T(1,128)} %bitcast.34, bf16[4096,1024]{1,0:T(8,128)(2,1)} %refs_3_.1, f32[1,1024]{1,0:T(1,128)} %bitcast.36, f32[1,1024]{1,0:T(1,128)} %bitcast.38, f32[1,1024]{1,0:T(1,128)} %bitcast.40), custom_call_target="tpu_custom_call" | custom-call | flops 2147483648 | bytes 17825792 | tf_op jit(solution)/shard_map/encode/pallas_call | solution.py:142
  47.3 0.0 copy-start
  47.3 0.0 copy-start.1
  47.3 0.0 collective-permute-done.8.refs_14_
  47.3 0.0 collective-permute-done.7.refs_12_
  47.3 2.6 %collective-permute-start.9 = (bf16[400,1024]{1,0:T(8,128)(2,1)}, bf16[400,1024]{1,0:T(8,128)(2,1)S(1)}, u32[]{:S(2)}, u32[]{:S(2)}) collective-permute-start(bf16[400,1024]{1,0:T(8,128)(2,1)} %collective-permute-done.7.refs_12_), channel_id=1, source_target_pairs={{0,4},{1,5},{2,6},{3,7},{4,8},{5,9},{6,10},{7,11},{8,12},{9,13},{1... | collective-permute-start | bytes 2457608 | tf_op jit(solution)/shard_map/ppermute | solution.py:23
  49.9 0.0 collective-permute-start.11
  49.9 2.7 %collective-permute-start.10 = (bf16[128,1024]{1,0:T(8,128)(2,1)}, bf16[128,1024]{1,0:T(8,128)(2,1)S(1)}, u32[]{:S(2)}, u32[]{:S(2)}) collective-permute-start(bf16[128,1024]{1,0:T(8,128)(2,1)} %encode.3.refs_11_), channel_id=1, source_target_pairs={{0,4},{1,5},{2,6},{3,7},{4,8},{5,9},{6,10},{7,11},{8,12},{9,13},{1... | collective-permute-start | bytes 786440 | tf_op jit(solution)/shard_map/ppermute | solution.py:23
  52.5 0.0 collective-permute-done.4.refs_2_
  52.6 2.7 %collective-permute-start.6 = (bf16[2,144,1024]{2,1,0:T(8,128)(2,1)S(1)}, bf16[2,144,1024]{2,1,0:T(8,128)(2,1)S(1)}, u32[]{:S(2)}, u32[]{:S(2)}) collective-permute-start(bf16[2,144,1024]{2,1,0:T(8,128)(2,1)S(1)} %slice.9), channel_id=1, source_target_pairs={{0,3},{1,0},{2,1},{3,2},{4,7},{5,4},{6,5},{7,6},{8,11},{9,8},{10,9... | collective-permute-start | bytes 1769480 | tf_op jit(solution)/shard_map/ppermute | solution.py:23
  55.3 0.0 collective-permute-done.3.refs_1_
  55.4 0.1 collective-permute-start.5
  55.4 3.9 %collective-permute-done.11.refs_15_ = bf16[128,1024]{1,0:T(8,128)(2,1)S(1)} collective-permute-done((bf16[128,1024]{1,0:T(8,128)(2,1)}, bf16[128,1024]{1,0:T(8,128)(2,1)S(1)}, u32[]{:S(2)}, u32[]{:S(2)}) %collective-permute-start.11) | collective-permute-done | bytes 262176 | tf_op jit(solution)/shard_map/ppermute | solution.py:23
  59.4 1.2 %collective-permute-start.12 = (bf16[4,144,1024]{2,1,0:T(8,128)(2,1)S(1)}, bf16[4,144,1024]{2,1,0:T(8,128)(2,1)S(1)}, u32[]{:S(2)}, u32[]{:S(2)}) collective-permute-start(bf16[4,144,1024]{2,1,0:T(8,128)(2,1)S(1)} %pad_maximum_fusion.refs_0_), channel_id=1, source_target_pairs={{0,16},{1,17},{2,18},{3,19},{4,20},{5,21},{6,22},{7,23},{8,24},{9,... | collective-permute-start | bytes 3538952 | tf_op jit(solution)/shard_map/ppermute | solution.py:23
  60.6 4.5 %collective-permute-done.10.refs_13_ = bf16[128,1024]{1,0:T(8,128)(2,1)S(1)} collective-permute-done((bf16[128,1024]{1,0:T(8,128)(2,1)}, bf16[128,1024]{1,0:T(8,128)(2,1)S(1)}, u32[]{:S(2)}, u32[]{:S(2)}) %collective-permute-start.10) | collective-permute-done | bytes 262176 | tf_op jit(solution)/shard_map/ppermute | solution.py:23
  65.1 3.7 %collective-permute-start.13 = (bf16[4,144,1024]{2,1,0:T(8,128)(2,1)S(1)}, bf16[4,144,1024]{2,1,0:T(8,128)(2,1)S(1)}, u32[]{:S(2)}, u32[]{:S(2)}) collective-permute-start(bf16[4,144,1024]{2,1,0:T(8,128)(2,1)S(1)} %collective-permute-done.3.refs_1_), channel_id=1, source_target_pairs={{0,16},{1,17},{2,18},{3,19},{4,20},{5,21},{6,22},{7,23},{8,24},{9,... | collective-permute-start | bytes 3538952 | tf_op jit(solution)/shard_map/ppermute | solution.py:23
  68.8 0.0 collective-permute-done.9.refs_16_
  68.8 0.0 collective-permute-start.14
  68.8 0.0 collective-permute-done.6.refs_4_
  68.8 0.0 collective-permute-done.5.refs_3_
  68.8 0.1 collective-permute-start.17
  68.9 1.8 %collective-permute-start.15 = (bf16[2,144,1024]{2,1,0:T(8,128)(2,1)S(1)}, bf16[2,144,1024]{2,1,0:T(8,128)(2,1)S(1)}, u32[]{:S(2)}, u32[]{:S(2)}) collective-permute-start(bf16[2,144,1024]{2,1,0:T(8,128)(2,1)S(1)} %collective-permute-done.5.refs_3_), channel_id=1, source_target_pairs={{0,16},{1,17},{2,18},{3,19},{4,20},{5,21},{6,22},{7,23},{8,24},{9,... | collective-permute-start | bytes 1769480 | tf_op jit(solution)/shard_map/ppermute | solution.py:23
  70.8 3.6 %collective-permute-done.17.refs_17_ = bf16[128,1024]{1,0:T(8,128)(2,1)S(1)} collective-permute-done((bf16[128,1024]{1,0:T(8,128)(2,1)S(1)}, bf16[128,1024]{1,0:T(8,128)(2,1)S(1)}, u32[]{:S(2)}, u32[]{:S(2)}) %collective-permute-start.17) | collective-permute-done | bytes 262176 | tf_op jit(solution)/shard_map/ppermute | solution.py:23
  74.4 2.5 %collective-permute-start.16 = (bf16[2,144,1024]{2,1,0:T(8,128)(2,1)S(1)}, bf16[2,144,1024]{2,1,0:T(8,128)(2,1)S(1)}, u32[]{:S(2)}, u32[]{:S(2)}) collective-permute-start(bf16[2,144,1024]{2,1,0:T(8,128)(2,1)S(1)} %collective-permute-done.6.refs_4_), channel_id=1, source_target_pairs={{0,16},{1,17},{2,18},{3,19},{4,20},{5,21},{6,22},{7,23},{8,24},{9,... | collective-permute-start | bytes 1769480 | tf_op jit(solution)/shard_map/ppermute | solution.py:23
  76.9 0.0 collective-permute-done.12.refs_5_
  76.9 0.0 collective-permute-done.13.refs_6_
  76.9 0.0 collective-permute-done.14.refs_7_
  76.9 0.0 collective-permute-done.15.refs_8_
  76.9 1.6 %collective-permute-done.16.refs_9_ = bf16[2,144,1024]{2,1,0:T(8,128)(2,1)S(1)} collective-permute-done((bf16[2,144,1024]{2,1,0:T(8,128)(2,1)S(1)}, bf16[2,144,1024]{2,1,0:T(8,128)(2,1)S(1)}, u32[]{:S(2)}, u32[]{:S(2)}) %collective-permute-start.16) | collective-permute-done | bytes 589856 | tf_op jit(solution)/shard_map/ppermute | solution.py:23
  78.5 0.0 copy-done
  78.5 0.0 copy-done.1
  78.5 8.4 %score_pairs.1 = f32[128,1,128]{2,1,0:T(1,128)S(1)} custom-call(s32[4]{0:T(128)S(1)} %pad_add_fusion.pos_ref, s32[1]{0:T(128)} %bitcast.26.count_ref, bf16[4,144,1024]{2,1,0:T(8,128)(2,1)S(1)} %pad_maximum_fusion.refs_0_, bf16[4,144,1024]{2,1,0:T(8,128)(2,1)S(1)} %collective-permute-done.3.refs_1_, bf16[4,144,1024]{2,1,0:T(8,128)(2,1)S(1)} %collective-permute-done.4.refs_2_, ...), custom_call_target="tpu_custom_call" | custom-call | tf_op jit(solution)/shard_map/score_pairs/pallas_call | solution.py:316
  86.9 15.8 %all_to_all.5.got_ref = f32[128,1,128]{2,1,0:T(1,128)} all-to-all(f32[128,1,128]{2,1,0:T(1,128)S(1)} %score_pairs.1), channel_id=1, replica_groups=mesh['dp'=8,'prompt'=16] {'dp','prompt'}, dimensions={0} | all-to-all | bytes 131072 | tf_op jit(solution)/shard_map/all_to_all | solution.py:387
  102.8 1.6 %finish.1 = (f32[3,1,1,32]{3,2,1,0:T(1,128)}, f32[1,3]{1,0:T(1,128)}) custom-call(f32[128,1,128]{2,1,0:T(1,128)} %all_to_all.5.got_ref), custom_call_target="tpu_custom_call" | custom-call | tf_op jit(solution)/shard_map/finish/pallas_call | solution.py:388
  (2 shorter events, 0.1 us)
Async XLA Ops:
  19.2 11.7 %collective-permute-start.2 = (bf16[144,1024]{1,0:T(8,128)(2,1)}, bf16[144,1024]{1,0:T(8,128)(2,1)S(1)}, u32[]{:S(2)}, u32[]{:S(2)}) collective-permute-start(bf16[144,1024]{1,0:T(8,128)(2,1)} %get-tuple-element.22), channel_id=1, source_target_pairs={{0,96},{1,97},{2,98},{3,99},{4,100},{5,101},{6,102},{7,103},{8,104... | collective-permute-start | bytes 884744 | tf_op jit(solution)/shard_map/ppermute | solution.py:23
  23.8 7.6 %collective-permute-start.1 = (bf16[144,1024]{1,0:T(8,128)(2,1)}, bf16[144,1024]{1,0:T(8,128)(2,1)S(1)}, u32[]{:S(2)}, u32[]{:S(2)}) collective-permute-start(bf16[144,1024]{1,0:T(8,128)(2,1)} %get-tuple-element.22), channel_id=1, source_target_pairs={{0,64},{1,65},{2,66},{3,67},{4,68},{5,69},{6,70},{7,71},{8,72},{9,... | collective-permute-start | bytes 884744 | tf_op jit(solution)/shard_map/ppermute | solution.py:23
  23.8 10.6 %collective-permute-start = (bf16[144,1024]{1,0:T(8,128)(2,1)}, bf16[144,1024]{1,0:T(8,128)(2,1)S(1)}, u32[]{:S(2)}, u32[]{:S(2)}) collective-permute-start(bf16[144,1024]{1,0:T(8,128)(2,1)} %get-tuple-element.22), channel_id=1, source_target_pairs={{0,32},{1,33},{2,34},{3,35},{4,36},{5,37},{6,38},{7,39},{8,40},{9,... | collective-permute-start | bytes 884744 | tf_op jit(solution)/shard_map/ppermute | solution.py:23
  24.5 22.8 %collective-permute-start.8 = (bf16[400,1024]{1,0:T(8,128)(2,1)}, bf16[400,1024]{1,0:T(8,128)(2,1)}, u32[]{:S(2)}, u32[]{:S(2)}) collective-permute-start(bf16[400,1024]{1,0:T(8,128)(2,1)} %get-tuple-element.30.refs_10_), channel_id=1, source_target_pairs={{0,12},{1,13},{2,14},{3,15},{4,0},{5,1},{6,2},{7,3},{8,4},{9,5},{1... | collective-permute-start | bytes 2457608 | tf_op jit(solution)/shard_map/ppermute | solution.py:23
  25.7 21.6 %collective-permute-start.7 = (bf16[400,1024]{1,0:T(8,128)(2,1)}, bf16[400,1024]{1,0:T(8,128)(2,1)}, u32[]{:S(2)}, u32[]{:S(2)}) collective-permute-start(bf16[400,1024]{1,0:T(8,128)(2,1)} %get-tuple-element.30.refs_10_), channel_id=1, source_target_pairs={{0,4},{1,5},{2,6},{3,7},{4,8},{5,9},{6,10},{7,11},{8,12},{9,13},{1... | collective-permute-start | bytes 2457608 | tf_op jit(solution)/shard_map/ppermute | solution.py:23
  35.4 17.1 %collective-permute-start.4 = (bf16[4,144,1024]{2,1,0:T(8,128)(2,1)S(1)}, bf16[4,144,1024]{2,1,0:T(8,128)(2,1)S(1)}, u32[]{:S(2)}, u32[]{:S(2)}) collective-permute-start(bf16[4,144,1024]{2,1,0:T(8,128)(2,1)S(1)} %pad_maximum_fusion.refs_0_), channel_id=1, source_target_pairs={{0,3},{1,0},{2,1},{3,2},{4,7},{5,4},{6,5},{7,6},{8,11},{9,8},{10,9... | collective-permute-start | bytes 3538952 | tf_op jit(solution)/shard_map/ppermute | solution.py:23
  38.3 17.1 %collective-permute-start.3 = (bf16[4,144,1024]{2,1,0:T(8,128)(2,1)S(1)}, bf16[4,144,1024]{2,1,0:T(8,128)(2,1)S(1)}, u32[]{:S(2)}, u32[]{:S(2)}) collective-permute-start(bf16[4,144,1024]{2,1,0:T(8,128)(2,1)S(1)} %pad_maximum_fusion.refs_0_), channel_id=1, source_target_pairs={{0,1},{1,2},{2,3},{3,0},{4,5},{5,6},{6,7},{7,4},{8,9},{9,10},{10,1... | collective-permute-start | bytes 3538952 | tf_op jit(solution)/shard_map/ppermute | solution.py:23
  47.3 31.2 %copy-start = (bf16[128,1024]{1,0:T(8,128)(2,1)S(1)}, bf16[128,1024]{1,0:T(8,128)(2,1)}, u32[]{:S(2)}) copy-start(bf16[128,1024]{1,0:T(8,128)(2,1)} %encode.3.refs_11_) | copy-start | bytes 786436
  47.3 31.2 %copy-start.1 = (bf16[400,1024]{1,0:T(8,128)(2,1)S(1)}, bf16[400,1024]{1,0:T(8,128)(2,1)}, u32[]{:S(2)}) copy-start(bf16[400,1024]{1,0:T(8,128)(2,1)} %get-tuple-element.30.refs_10_) | copy-start | bytes 2457604
  47.3 21.5 %collective-permute-start.9 = (bf16[400,1024]{1,0:T(8,128)(2,1)}, bf16[400,1024]{1,0:T(8,128)(2,1)S(1)}, u32[]{:S(2)}, u32[]{:S(2)}) collective-permute-start(bf16[400,1024]{1,0:T(8,128)(2,1)} %collective-permute-done.7.refs_12_), channel_id=1, source_target_pairs={{0,4},{1,5},{2,6},{3,7},{4,8},{5,9},{6,10},{7,11},{8,12},{9,13},{1... | collective-permute-start | bytes 2457608 | tf_op jit(solution)/shard_map/ppermute | solution.py:23
  49.9 9.5 %collective-permute-start.11 = (bf16[128,1024]{1,0:T(8,128)(2,1)}, bf16[128,1024]{1,0:T(8,128)(2,1)S(1)}, u32[]{:S(2)}, u32[]{:S(2)}) collective-permute-start(bf16[128,1024]{1,0:T(8,128)(2,1)} %encode.3.refs_11_), channel_id=1, source_target_pairs={{0,12},{1,13},{2,14},{3,15},{4,0},{5,1},{6,2},{7,3},{8,4},{9,5},{1... | collective-permute-start | bytes 786440 | tf_op jit(solution)/shard_map/ppermute | solution.py:23
  49.9 15.2 %collective-permute-start.10 = (bf16[128,1024]{1,0:T(8,128)(2,1)}, bf16[128,1024]{1,0:T(8,128)(2,1)S(1)}, u32[]{:S(2)}, u32[]{:S(2)}) collective-permute-start(bf16[128,1024]{1,0:T(8,128)(2,1)} %encode.3.refs_11_), channel_id=1, source_target_pairs={{0,4},{1,5},{2,6},{3,7},{4,8},{5,9},{6,10},{7,11},{8,12},{9,13},{1... | collective-permute-start | bytes 786440 | tf_op jit(solution)/shard_map/ppermute | solution.py:23
  52.6 16.2 %collective-permute-start.6 = (bf16[2,144,1024]{2,1,0:T(8,128)(2,1)S(1)}, bf16[2,144,1024]{2,1,0:T(8,128)(2,1)S(1)}, u32[]{:S(2)}, u32[]{:S(2)}) collective-permute-start(bf16[2,144,1024]{2,1,0:T(8,128)(2,1)S(1)} %slice.9), channel_id=1, source_target_pairs={{0,3},{1,0},{2,1},{3,2},{4,7},{5,4},{6,5},{7,6},{8,11},{9,8},{10,9... | collective-permute-start | bytes 1769480 | tf_op jit(solution)/shard_map/ppermute | solution.py:23
  55.4 13.4 %collective-permute-start.5 = (bf16[2,144,1024]{2,1,0:T(8,128)(2,1)S(1)}, bf16[2,144,1024]{2,1,0:T(8,128)(2,1)S(1)}, u32[]{:S(2)}, u32[]{:S(2)}) collective-permute-start(bf16[2,144,1024]{2,1,0:T(8,128)(2,1)S(1)} %slice.8), channel_id=1, source_target_pairs={{0,1},{1,2},{2,3},{3,0},{4,5},{5,6},{6,7},{7,4},{8,9},{9,10},{10,1... | collective-permute-start | bytes 1769480 | tf_op jit(solution)/shard_map/ppermute | solution.py:23
  59.4 17.5 %collective-permute-start.12 = (bf16[4,144,1024]{2,1,0:T(8,128)(2,1)S(1)}, bf16[4,144,1024]{2,1,0:T(8,128)(2,1)S(1)}, u32[]{:S(2)}, u32[]{:S(2)}) collective-permute-start(bf16[4,144,1024]{2,1,0:T(8,128)(2,1)S(1)} %pad_maximum_fusion.refs_0_), channel_id=1, source_target_pairs={{0,16},{1,17},{2,18},{3,19},{4,20},{5,21},{6,22},{7,23},{8,24},{9,... | collective-permute-start | bytes 3538952 | tf_op jit(solution)/shard_map/ppermute | solution.py:23
  65.1 11.8 %collective-permute-start.13 = (bf16[4,144,1024]{2,1,0:T(8,128)(2,1)S(1)}, bf16[4,144,1024]{2,1,0:T(8,128)(2,1)S(1)}, u32[]{:S(2)}, u32[]{:S(2)}) collective-permute-start(bf16[4,144,1024]{2,1,0:T(8,128)(2,1)S(1)} %collective-permute-done.3.refs_1_), channel_id=1, source_target_pairs={{0,16},{1,17},{2,18},{3,19},{4,20},{5,21},{6,22},{7,23},{8,24},{9,... | collective-permute-start | bytes 3538952 | tf_op jit(solution)/shard_map/ppermute | solution.py:23
  68.8 8.1 %collective-permute-start.14 = (bf16[4,144,1024]{2,1,0:T(8,128)(2,1)S(1)}, bf16[4,144,1024]{2,1,0:T(8,128)(2,1)S(1)}, u32[]{:S(2)}, u32[]{:S(2)}) collective-permute-start(bf16[4,144,1024]{2,1,0:T(8,128)(2,1)S(1)} %collective-permute-done.4.refs_2_), channel_id=1, source_target_pairs={{0,16},{1,17},{2,18},{3,19},{4,20},{5,21},{6,22},{7,23},{8,24},{9,... | collective-permute-start | bytes 3538952 | tf_op jit(solution)/shard_map/ppermute | solution.py:23
  68.8 5.6 %collective-permute-start.17 = (bf16[128,1024]{1,0:T(8,128)(2,1)S(1)}, bf16[128,1024]{1,0:T(8,128)(2,1)S(1)}, u32[]{:S(2)}, u32[]{:S(2)}) collective-permute-start(bf16[128,1024]{1,0:T(8,128)(2,1)S(1)} %collective-permute-done.10.refs_13_), channel_id=1, source_target_pairs={{0,4},{1,5},{2,6},{3,7},{4,8},{5,9},{6,10},{7,11},{8,12},{9,13},{1... | collective-permute-start | bytes 786440 | tf_op jit(solution)/shard_map/ppermute | solution.py:23
  68.9 8.0 %collective-permute-start.15 = (bf16[2,144,1024]{2,1,0:T(8,128)(2,1)S(1)}, bf16[2,144,1024]{2,1,0:T(8,128)(2,1)S(1)}, u32[]{:S(2)}, u32[]{:S(2)}) collective-permute-start(bf16[2,144,1024]{2,1,0:T(8,128)(2,1)S(1)} %collective-permute-done.5.refs_3_), channel_id=1, source_target_pairs={{0,16},{1,17},{2,18},{3,19},{4,20},{5,21},{6,22},{7,23},{8,24},{9,... | collective-permute-start | bytes 1769480 | tf_op jit(solution)/shard_map/ppermute | solution.py:23
  74.4 4.1 %collective-permute-start.16 = (bf16[2,144,1024]{2,1,0:T(8,128)(2,1)S(1)}, bf16[2,144,1024]{2,1,0:T(8,128)(2,1)S(1)}, u32[]{:S(2)}, u32[]{:S(2)}) collective-permute-start(bf16[2,144,1024]{2,1,0:T(8,128)(2,1)S(1)} %collective-permute-done.6.refs_4_), channel_id=1, source_target_pairs={{0,16},{1,17},{2,18},{3,19},{4,20},{5,21},{6,22},{7,23},{8,24},{9,... | collective-permute-start | bytes 1769480 | tf_op jit(solution)/shard_map/ppermute | solution.py:23

commit v7 on v6

--- a/solution.py
+++ b/solution.py
@@ -56,17 +56,6 @@
     step = pl.program_id(0)
     seqs = n_cand + len(picks)
 
-    def token_weights(ids, length):
-        high, low = ids >> 7, ids & 127
-        hot = (lax.broadcasted_iota(jnp.int32, (TABLE_ROWS, L), 0) == high).astype(jnp.bfloat16)
-        rows = lax.dot_general(
-            tbl_ref[...].astype(jnp.bfloat16), hot, (((0,), (0,)), ((), ())), preferred_element_type=jnp.float32
-        )
-        mine = lax.broadcasted_iota(jnp.int32, (128, L), 0) == low
-        value = jnp.sum(jnp.where(mine, rows, 0.0), axis=0, keepdims=True)
-        live = lax.broadcasted_iota(jnp.int32, (1, L), 1) < length
-        return jnp.where(live, value, 0.0)
-
     @pl.when(step == 0)
     def _():
         if n_cand:
@@ -74,17 +63,31 @@
         for k, q in enumerate(picks):
             x_ref[L * (n_cand + k) : L * (n_cand + k + 1), :] = rh_ref[q]
         if weights:
+            ids = jnp.concatenate([cid_ref[...]] + [rid_ref[q : q + 1, :] for q in range(4)], axis=1)
+            high, low = ids >> 7, ids & 127
+            hot = lax.broadcasted_iota(jnp.int32, (TABLE_ROWS, 5 * L), 0) == high
+            rows = lax.dot_general(
+                tbl_ref[...].astype(jnp.bfloat16), hot.astype(jnp.bfloat16), (((0,), (0,)), ((), ())),
+                preferred_element_type=jnp.float32,
+            )
+            mine = lax.broadcasted_iota(jnp.int32, (128, 5 * L), 0) == low
+            value = jnp.sum(jnp.where(mine, rows, 0.0), axis=0, keepdims=True)
+            place = lax.broadcasted_iota(jnp.int32, (1, L), 1)
+
+            def token_weights(k, length):
+                return jnp.where(place < length, value[:, k * L : (k + 1) * L], 0.0)
+
             row = lax.broadcasted_iota(jnp.int32, (16, L), 0)
             co_ref[L:, :] = jnp.zeros((16, D), jnp.bfloat16)
             ro_ref[len(picks) * L :, :] = jnp.zeros((16, D), jnp.bfloat16)
-            w = token_weights(cid_ref[...], clen_ref[0])
+            w = token_weights(0, clen_ref[0])
             count = jnp.full((1, 2 * SLOTS), count_ref[0], jnp.int32)
             slots = jnp.concatenate([pc_ref[...], pr_ref[...], count], axis=1).astype(jnp.float32)
             words = jnp.where(row == 0, w, jnp.where(row == 1, slots, 0.0))
             co_ref[L:, 0:L] = words.astype(jnp.bfloat16)
             block = jnp.zeros((16, L), jnp.float32)
             for q in range(4):
-                block = jnp.where(row == q, token_weights(rid_ref[q : q + 1, :], rlen_ref[q]), block)
+                block = jnp.where(row == q, token_weights(q + 1, rlen_ref[q]), block)
             ro_ref[len(picks) * L :, 0:L] = block.astype(jnp.bfloat16)
 
     w = up.shape[1] // sub
@@ -168,11 +171,10 @@
 
 
 GROUP = 8
-AHEAD = 3
 
 
 def pair_kernel(pos_ref, count_ref, *refs):
-    cands, blocks, refs = refs[:10], refs[10:18], refs[18:]
+    cands, blocks, refs = refs[:9], refs[9:13], refs[13:]
     out_ref, cbuf, rbuf, wbuf, todo, lint, lists, lsem = refs
     y, core, x, z = pos_ref[0], pos_ref[1], pos_ref[2], pos_ref[3]
 
@@ -197,8 +199,9 @@
     u2 = jnp.where(even, dz, dy)
     i1 = (4 - u1) & 3
     g2 = jnp.where(u2 == 3, 1, jnp.where(u2 == 1, 2, jnp.where(u2 == 2, jnp.where(i1 >= 2, 4, 3), 0)))
-    source = g2 + jnp.where((c & 1) == core, 0, 5)
-    row = jnp.where(g2 == 4, i1 - 2, i1)
+    mine = (c & 1) == core
+    source = jnp.where(mine, g2, 5 + jnp.minimum(g2, 3))
+    row = jnp.where(mine & (g2 == 4), i1 - 2, i1)
     back = jnp.where(core == 0, 3, 1)
     rs = jnp.where(dx == 0, 0, jnp.where(dx == 2, 3, jnp.where(dx == back, 1, 2)))
     i = (r >> 4) & 3
@@ -236,17 +239,17 @@
         code = todo[t]
         row = (code >> 4) & 3
         i = (code >> 8) & 3
-        at = pl.multiple_of(jnp.where(i < AHEAD, i, i - AHEAD) * L, L)
+        at = pl.multiple_of(i * L, L)
 
         def take_cand(k):
             cbuf[b] = cands[k][row]
 
         def take_ref(k):
             rbuf[b] = blocks[k][pl.ds(at, L), :]
-            wbuf[b] = blocks[k - k % 2][AHEAD * L : AHEAD * L + 16, 0:L]
-
-        choose(code & 15, 0, 10, take_cand)
-        choose(((code >> 6) & 3) * 2 + jnp.where(i < AHEAD, 0, 1), 0, 8, take_ref)
+            wbuf[b] = blocks[k][4 * L : 4 * L + 16, 0:L]
+
+        choose(code & 15, 0, 9, take_cand)
+        choose((code >> 6) & 3, 0, 4, take_ref)
 
     def one(t, b):
         similar = lax.dot_general(
@@ -308,6 +311,23 @@
     for k in range(3):
         scores_ref[k, 0] = s[:, k * SLOTS : (k + 1) * SLOTS]
     totals_ref[...] = s[:, 96:99] / s[:, 99:100]
+
+
+def pass_on_kernel(pos_ref, out_ref):
+    for k in range(4):
+        out_ref[k] = pos_ref[k]
+
+
+def pass_on(pos):
+    smem = pl.BlockSpec(memory_space=pltpu.SMEM)
+    return pl.pallas_call(
+        pass_on_kernel,
+        in_specs=[smem],
+        out_specs=smem,
+        out_shape=jax.ShapeDtypeStruct((4,), jnp.int32),
+        cost_estimate=pl.CostEstimate(flops=17250000000, bytes_accessed=1024, transcendentals=0),
+        name="pass_on",
+    )(pos)
 
 
 def score_pairs(pos, count, blocks):
@@ -359,30 +379,26 @@
         pair_ref.reshape(1, SLOTS),
         table,
     )
-    cand, refs_a = encode((0, 1, 2), cand_hidden.reshape(1, L, D), hidden, words, layer)
+    cand, refs = encode((0, 1, 2, 3), cand_hidden.reshape(1, L, D), hidden, words, layer)
+    back = send(refs, along_x(1))
+    ahead = send(refs, along_x(-1))
+    back, ahead = lax.optimization_barrier((back, ahead))
+    far = send(back, along_x(1))
     c1 = send(cand, along_first(1))
     c3 = send(cand, along_first(-1))
     c2 = send(cand, along_first(2))
-    back_a = send(refs_a, along_x(1))
-    ahead_a = send(refs_a, along_x(-1))
-    c1, c2, c3, hidden, pos = lax.optimization_barrier((c1, c2, c3, hidden, pos))
     own4 = jnp.stack([cand, c1, c2, c3])
     d1 = send(own4, along_second(1))
     d2 = send(own4, along_second(-1))
-    (refs_b,) = encode((3,), None, hidden, (), layer)
-    back_a, ahead_a, refs_b = lax.optimization_barrier((back_a, ahead_a, refs_b))
-    back_b = send(refs_b, along_x(1))
-    ahead_b = send(refs_b, along_x(-1))
-    far_a = send(back_a, along_x(1))
     d3 = send(d1[:2], along_second(1))
     d4 = send(d2[2:], along_second(-1))
     own4, d1, d2 = lax.optimization_barrier((own4, d1, d2))
     others = [send(v, to_other_core) for v in (own4, d1, d2)]
-    d3, d4, far_a, back_b, ahead_b = lax.optimization_barrier((d3, d4, far_a, back_b, ahead_b))
-    far_b = send(back_b, along_x(1))
-    others += [send(v, to_other_core) for v in (d3, d4)]
+    others.append(send(jnp.concatenate([d3, d4]), to_other_core))
+    far, pos = lax.optimization_barrier((far, pos))
+    pos = pass_on(pos)
     cands = [own4, d1, d2, d3, d4, *others]
-    blocks = [refs_a, refs_b, back_a, back_b, ahead_a, ahead_b, far_a, far_b]
+    blocks = [refs, back, ahead, far]
     payload = score_pairs(pos, count, [*cands, *blocks])
     got = lax.all_to_all(payload, AXES, 0, 0)
     scores, totals = pl.pallas_call(

time: 104 us -> 109 us (1.048)
  waiting for transfers between devices: 20.8 us -> 29.7 us
  starting transfers between devices: 28.2 us -> 20.3 us
  local copies, waits for them, and re-layouts: 1.7 us -> 6.46 us
  Pallas kernels: 34.7 us -> 30.1 us
  other arithmetic: 1.19 us -> 4.14 us
    ppermute x18 -> x14, waiting for transfers between devices: 20.8 us -> 29.7 us  [send(): lax.ppermute(value, AXES, [(number(*a), number(*where(*a))) for a in GRID])]
    ppermute x18 -> x14, starting transfers between devices: 28.2 us -> 20.3 us  [send(): lax.ppermute(value, AXES, [(number(*a), number(*where(*a))) for a in GRID])]
    pallas_call x2 -> x1, Pallas kernels: 24.7 us -> 18.4 us  [encode(): pl.pallas_call(functools.partial(encode_kernel, n_cand, picks, bool(words...]
    unnamed x4 -> x8, local copies, waits for them, and re-layouts: 0.01 us -> 3.13 us
    concatenate x0 -> x1, other arithmetic: none -> 2.38 us  [on_device(): others.append(send(jnp.concatenate([d3, d4]), to_other_core))]
    pallas_call x0 -> x1, Pallas kernels: none -> 1.18 us  [pass_on(): pl.pallas_call(pass_on_kernel, in_specs=[smem], out_specs=smem, out_shape...]
  transfers between devices with their start and end apart: 18 -> 14, of which waited for: 7 -> 8; matrix products, arithmetic and copies ran while one was open for 1% -> 5% of each run, Pallas kernels for 9% -> 1%
where the time goes in v7:
time: 109 us
  Pallas kernels  30.1 us (28%)
  waiting for transfers between devices  29.7 us (27%)
  starting transfers between devices  20.3 us (19%)
  blocking collectives  15.9 us (15%)
  local copies, waits for them, and re-layouts  6.46 us (6%)
  other arithmetic  4.14 us (4%)
  between operations  1.99 us (2%)
    ppermute x14, waiting for transfers between devices, send(): lax.ppermute(value, AXES, [(number(*a), number(*where(*a))) for a in GRID])  29.7 us
    ppermute x14, starting transfers between devices, send(): lax.ppermute(value, AXES, [(number(*a), number(*where(*a))) for a in GRID])  20.3 us
    pallas_call x1, Pallas kernels, encode(): pl.pallas_call(functools.partial(encode_kernel, n_cand, picks, bool(words...  18.4 us
    all_to_all x1, blocking collectives, on_device(): got = lax.all_to_all(payload, AXES, 0, 0)  15.9 us
    pallas_call x1, Pallas kernels, score_pairs(): pl.pallas_call(pair_kernel, in_specs=[smem] * 2 + [vmem] * len(blocks), o...  8.91 us
    unnamed x8, local copies, waits for them, and re-layouts  3.13 us
    concatenate x1, other arithmetic, on_device(): others.append(send(jnp.concatenate([d3, d4]), to_other_core))  2.38 us
  transfers between devices with their start and end apart: 14, of which 8 were waited for; matrix products, arithmetic and copies ran while one was open for 5% of the time, Pallas kernels for 1%

profile of v7, /device:TPU:1, one launch (start us, length us, event | category | flops | bytes accessed | tf_op | source)
XLA Modules:
  0.0 108.6 jit_solution(2739997913573188183)
XLA Ops:
  1.9 1.6 %pad_bitcast_fusion.refs_7_ = f32[400,128]{1,0:T(8,128)} fusion(f32[50265]{0:T(1024)} %param.22), kind=kLoop, calls=%fused_computation.2 | loop fusion | bytes 405860 | tf_op jit(solution)/shard_map/reshape | solution.py:359
  3.5 18.4 %encode.1 = (bf16[144,1024]{1,0:T(8,128)(2,1)}, bf16[528,1024]{1,0:T(8,128)(2,1)}) custom-call(s32[1]{0:T(128)} %bitcast.24.refs_0_, s32[4]{0:T(128)} %bitcast.38, s32[1]{0:T(128)} %bitcast.25.refs_2_, s32[1,128]{1,0:T(1,128)} %bitcast.39, s32[4,128]{1,0:T(4,128)} %bitcast.37, s32[1,32]{1,0:T(1,128)} %bitcast.40, s32[1,32]{1,0:T(1,128)} %bitcast.41, ...), custom_call_target="tpu_custom_call" | custom-call | flops 10737418240 | bytes 17825792 | tf_op jit(solution)/shard_map/encode/pallas_call | solution.py:145
  22.0 4.6 %collective-permute-start.5 = (bf16[144,1024]{1,0:T(8,128)(2,1)}, bf16[144,1024]{1,0:T(8,128)(2,1)S(1)}, u32[]{:S(2)}, u32[]{:S(2)}) collective-permute-start(bf16[144,1024]{1,0:T(8,128)(2,1)} %get-tuple-element.16), channel_id=1, source_target_pairs={{0,96},{1,97},{2,98},{3,99},{4,100},{5,101},{6,102},{7,103},{8,104... | collective-permute-start | bytes 884744 | tf_op jit(solution)/shard_map/ppermute | solution.py:23
  26.5 0.0 collective-permute-start.4
  26.5 0.7 collective-permute-start.3
  27.2 1.2 %collective-permute-start.1 = (bf16[528,1024]{1,0:T(8,128)(2,1)}, bf16[528,1024]{1,0:T(8,128)(2,1)S(1)}, u32[]{:S(2)}, u32[]{:S(2)}) collective-permute-start(bf16[528,1024]{1,0:T(8,128)(2,1)} %get-tuple-element.13.refs_9_), channel_id=1, source_target_pairs={{0,12},{1,13},{2,14},{3,15},{4,0},{5,1},{6,2},{7,3},{8,4},{9,5},{1... | collective-permute-start | bytes 3244040 | tf_op jit(solution)/shard_map/ppermute | solution.py:23
  28.5 1.5 %collective-permute-start = (bf16[528,1024]{1,0:T(8,128)(2,1)}, bf16[528,1024]{1,0:T(8,128)(2,1)}, u32[]{:S(2)}, u32[]{:S(2)}) collective-permute-start(bf16[528,1024]{1,0:T(8,128)(2,1)} %get-tuple-element.13.refs_9_), channel_id=1, source_target_pairs={{0,4},{1,5},{2,6},{3,7},{4,8},{5,9},{6,10},{7,11},{8,12},{9,13},{1... | collective-permute-start | bytes 3244040 | tf_op jit(solution)/shard_map/ppermute | solution.py:23
  29.9 3.8 %collective-permute-done.5 = bf16[144,1024]{1,0:T(8,128)(2,1)S(1)} collective-permute-done((bf16[144,1024]{1,0:T(8,128)(2,1)}, bf16[144,1024]{1,0:T(8,128)(2,1)S(1)}, u32[]{:S(2)}, u32[]{:S(2)}) %collective-permute-start.5) | collective-permute-done | bytes 294944 | tf_op jit(solution)/shard_map/ppermute | solution.py:23
  33.7 0.5 collective-permute-done.4
  34.2 2.9 %collective-permute-done.3 = bf16[144,1024]{1,0:T(8,128)(2,1)S(1)} collective-permute-done((bf16[144,1024]{1,0:T(8,128)(2,1)}, bf16[144,1024]{1,0:T(8,128)(2,1)S(1)}, u32[]{:S(2)}, u32[]{:S(2)}) %collective-permute-start.3) | collective-permute-done | bytes 294944 | tf_op jit(solution)/shard_map/ppermute | solution.py:23
  37.1 1.1 %pad_maximum_fusion.refs_0_ = bf16[4,144,1024]{2,1,0:T(8,128)(2,1)S(1)} fusion(bf16[1,144,1024]{2,1,0:T(8,128)(2,1)S(1)} %bitcast.28, bf16[1,144,1024]{2,1,0:T(8,128)(2,1)S(1)} %bitcast.29, bf16[1,144,1024]{2,1,0:T(8,128)(2,1)S(1)} %bitcast.30, bf16[1,144,1024]{2,1,0:T(8,128)(2,1)} %bitcast.27), kind=kLoop, calls=%fused_computation | loop fusion | flops 1769472 | bytes 2359296 | tf_op jit(solution)/shard_map/stack | solution.py:390
  38.2 2.8 %collective-permute-start.7 = (bf16[4,144,1024]{2,1,0:T(8,128)(2,1)S(1)}, bf16[4,144,1024]{2,1,0:T(8,128)(2,1)S(1)}, u32[]{:S(2)}, u32[]{:S(2)}) collective-permute-start(bf16[4,144,1024]{2,1,0:T(8,128)(2,1)S(1)} %pad_maximum_fusion.refs_0_), channel_id=1, source_target_pairs={{0,3},{1,0},{2,1},{3,2},{4,7},{5,4},{6,5},{7,6},{8,11},{9,8},{10,9... | collective-permute-start | bytes 3538952 | tf_op jit(solution)/shard_map/ppermute | solution.py:23
  41.0 0.0 collective-permute-start.6
  41.0 9.5 %collective-permute-done.1.refs_11_ = bf16[528,1024]{1,0:T(8,128)(2,1)S(1)} collective-permute-done((bf16[528,1024]{1,0:T(8,128)(2,1)}, bf16[528,1024]{1,0:T(8,128)(2,1)S(1)}, u32[]{:S(2)}, u32[]{:S(2)}) %collective-permute-start.1) | collective-permute-done | bytes 1081376 | tf_op jit(solution)/shard_map/ppermute | solution.py:23
  50.5 0.0 copy-start.1
  50.5 4.0 %collective-permute-done.refs_10_ = bf16[528,1024]{1,0:T(8,128)(2,1)} collective-permute-done((bf16[528,1024]{1,0:T(8,128)(2,1)}, bf16[528,1024]{1,0:T(8,128)(2,1)}, u32[]{:S(2)}, u32[]{:S(2)}) %collective-permute-start) | collective-permute-done | bytes 1081376 | tf_op jit(solution)/shard_map/ppermute | solution.py:23
  54.6 1.5 %collective-permute-start.2 = (bf16[528,1024]{1,0:T(8,128)(2,1)}, bf16[528,1024]{1,0:T(8,128)(2,1)}, u32[]{:S(2)}, u32[]{:S(2)}) collective-permute-start(bf16[528,1024]{1,0:T(8,128)(2,1)} %collective-permute-done.refs_10_), channel_id=1, source_target_pairs={{0,4},{1,5},{2,6},{3,7},{4,8},{5,9},{6,10},{7,11},{8,12},{9,13},{1... | collective-permute-start | bytes 3244040 | tf_op jit(solution)/shard_map/ppermute | solution.py:23
  56.1 0.0 collective-permute-done.7.refs_2_
  56.1 0.9 slice.9
  57.0 3.6 %collective-permute-start.9 = (bf16[2,144,1024]{2,1,0:T(8,128)(2,1)}, bf16[2,144,1024]{2,1,0:T(8,128)(2,1)}, u32[]{:S(2)}, u32[]{:S(2)}) collective-permute-start(bf16[2,144,1024]{2,1,0:T(8,128)(2,1)} %slice.9), channel_id=1, source_target_pairs={{0,3},{1,0},{2,1},{3,2},{4,7},{5,4},{6,5},{7,6},{8,11},{9,8},{10,9... | collective-permute-start | bytes 1769480 | tf_op jit(solution)/shard_map/ppermute | solution.py:23
  60.6 0.0 collective-permute-done.6.refs_1_
  60.6 0.9 slice.8
  61.4 0.0 copy-done.1
  61.4 0.0 collective-permute-start.8
  61.4 0.6 pad_add_fusion.pos_ref
  62.1 1.0 collective-permute-start.10
  63.1 0.0 collective-permute-start.11
  63.1 4.6 %collective-permute-done.9.refs_4_ = bf16[2,144,1024]{2,1,0:T(8,128)(2,1)} collective-permute-done((bf16[2,144,1024]{2,1,0:T(8,128)(2,1)}, bf16[2,144,1024]{2,1,0:T(8,128)(2,1)}, u32[]{:S(2)}, u32[]{:S(2)}) %collective-permute-start.9) | collective-permute-done | bytes 589856 | tf_op jit(solution)/shard_map/ppermute | solution.py:23
  67.7 1.6 %collective-permute-start.12 = (bf16[4,144,1024]{2,1,0:T(8,128)(2,1)S(1)}, bf16[4,144,1024]{2,1,0:T(8,128)(2,1)}, u32[]{:S(2)}, u32[]{:S(2)}) collective-permute-start(bf16[4,144,1024]{2,1,0:T(8,128)(2,1)S(1)} %collective-permute-done.7.refs_2_), channel_id=1, source_target_pairs={{0,16},{1,17},{2,18},{3,19},{4,20},{5,21},{6,22},{7,23},{8,24},{9,... | collective-permute-start | bytes 3538952 | tf_op jit(solution)/shard_map/ppermute | solution.py:23
  69.3 2.7 %collective-permute-done.8.refs_3_ = bf16[2,144,1024]{2,1,0:T(8,128)(2,1)} collective-permute-done((bf16[2,144,1024]{2,1,0:T(8,128)(2,1)}, bf16[2,144,1024]{2,1,0:T(8,128)(2,1)}, u32[]{:S(2)}, u32[]{:S(2)}) %collective-permute-start.8) | collective-permute-done | bytes 589856 | tf_op jit(solution)/shard_map/ppermute | solution.py:23
  72.0 2.4 %pad_maximum_fusion.1 = bf16[4,144,1024]{2,1,0:T(8,128)(2,1)} fusion(bf16[2,144,1024]{2,1,0:T(8,128)(2,1)} %collective-permute-done.9.refs_4_, bf16[2,144,1024]{2,1,0:T(8,128)(2,1)} %collective-permute-done.8.refs_3_), kind=kLoop, calls=%fused_computation.1 | loop fusion | flops 589824 | bytes 2359296 | tf_op jit(solution)/shard_map/concatenate | solution.py:397
  74.4 1.9 %collective-permute-start.13 = (bf16[4,144,1024]{2,1,0:T(8,128)(2,1)}, bf16[4,144,1024]{2,1,0:T(8,128)(2,1)}, u32[]{:S(2)}, u32[]{:S(2)}) collective-permute-start(bf16[4,144,1024]{2,1,0:T(8,128)(2,1)} %pad_maximum_fusion.1), channel_id=1, source_target_pairs={{0,16},{1,17},{2,18},{3,19},{4,20},{5,21},{6,22},{7,23},{8,24},{9,... | collective-permute-start | bytes 3538952 | tf_op jit(solution)/shard_map/ppermute | solution.py:23
  76.2 0.0 collective-permute-done.2.refs_12_
  76.2 1.2 %pass_on.1.pos_ref = s32[4]{0:T(128)} custom-call(s32[4]{0:T(128)} %pad_add_fusion.pos_ref), custom_call_target="tpu_custom_call" | custom-call | flops 17250000896 | bytes 1024 | tf_op jit(solution)/shard_map/pass_on/pallas_call | solution.py:323
  77.4 0.0 collective-permute-done.10.refs_5_
  77.4 0.0 collective-permute-done.11.refs_6_
  77.4 0.0 collective-permute-done.12.refs_7_
  77.5 1.6 %collective-permute-done.13.refs_8_ = bf16[4,144,1024]{2,1,0:T(8,128)(2,1)} collective-permute-done((bf16[4,144,1024]{2,1,0:T(8,128)(2,1)}, bf16[4,144,1024]{2,1,0:T(8,128)(2,1)}, u32[]{:S(2)}, u32[]{:S(2)}) %collective-permute-start.13) | collective-permute-done | bytes 1179680 | tf_op jit(solution)/shard_map/ppermute | solution.py:23
  79.0 0.0 copy-start
  79.0 1.2 %copy-done = bf16[528,1024]{1,0:T(8,128)(2,1)S(1)} copy-done((bf16[528,1024]{1,0:T(8,128)(2,1)S(1)}, bf16[528,1024]{1,0:T(8,128)(2,1)}, u32[]{:S(2)}) %copy-start) | copy-done | bytes 1081368
  80.3 0.0 copy-start.2
  80.3 1.2 %copy-done.2 = bf16[528,1024]{1,0:T(8,128)(2,1)S(1)} copy-done((bf16[528,1024]{1,0:T(8,128)(2,1)S(1)}, bf16[528,1024]{1,0:T(8,128)(2,1)}, u32[]{:S(2)}) %copy-start.2) | copy-done | bytes 1081368
  81.5 0.0 copy-start.3
  81.5 0.7 copy-done.3
  82.2 8.9 %score_pairs.1 = f32[128,1,128]{2,1,0:T(1,128)S(1)} custom-call(s32[4]{0:T(128)S(1)} %copy-done.3, s32[1]{0:T(128)} %bitcast.26.count_ref, bf16[4,144,1024]{2,1,0:T(8,128)(2,1)S(1)} %pad_maximum_fusion.refs_0_, bf16[4,144,1024]{2,1,0:T(8,128)(2,1)S(1)} %collective-permute-done.6.refs_1_, bf16[4,144,1024]{2,1,0:T(8,128)(2,1)S(1)} %collective-permute-done.7.refs_2_, ...), custom_call_target="tpu_custom_call" | custom-call | tf_op jit(solution)/shard_map/score_pairs/pallas_call | solution.py:336
  91.1 15.9 %all_to_all.5.got_ref = f32[128,1,128]{2,1,0:T(1,128)} all-to-all(f32[128,1,128]{2,1,0:T(1,128)S(1)} %score_pairs.1), channel_id=1, replica_groups=mesh['dp'=8,'prompt'=16] {'dp','prompt'}, dimensions={0} | all-to-all | bytes 131072 | tf_op jit(solution)/shard_map/all_to_all | solution.py:403
  107.0 1.6 %finish.1 = (f32[3,1,1,32]{3,2,1,0:T(1,128)}, f32[1,3]{1,0:T(1,128)}) custom-call(f32[128,1,128]{2,1,0:T(1,128)} %all_to_all.5.got_ref), custom_call_target="tpu_custom_call" | custom-call | tf_op jit(solution)/shard_map/finish/pallas_call | solution.py:404
Async XLA Ops:
  22.0 11.7 %collective-permute-start.5 = (bf16[144,1024]{1,0:T(8,128)(2,1)}, bf16[144,1024]{1,0:T(8,128)(2,1)S(1)}, u32[]{:S(2)}, u32[]{:S(2)}) collective-permute-start(bf16[144,1024]{1,0:T(8,128)(2,1)} %get-tuple-element.16), channel_id=1, source_target_pairs={{0,96},{1,97},{2,98},{3,99},{4,100},{5,101},{6,102},{7,103},{8,104... | collective-permute-start | bytes 884744 | tf_op jit(solution)/shard_map/ppermute | solution.py:23
  26.5 7.6 %collective-permute-start.4 = (bf16[144,1024]{1,0:T(8,128)(2,1)}, bf16[144,1024]{1,0:T(8,128)(2,1)S(1)}, u32[]{:S(2)}, u32[]{:S(2)}) collective-permute-start(bf16[144,1024]{1,0:T(8,128)(2,1)} %get-tuple-element.16), channel_id=1, source_target_pairs={{0,64},{1,65},{2,66},{3,67},{4,68},{5,69},{6,70},{7,71},{8,72},{9,... | collective-permute-start | bytes 884744 | tf_op jit(solution)/shard_map/ppermute | solution.py:23
  26.5 10.6 %collective-permute-start.3 = (bf16[144,1024]{1,0:T(8,128)(2,1)}, bf16[144,1024]{1,0:T(8,128)(2,1)S(1)}, u32[]{:S(2)}, u32[]{:S(2)}) collective-permute-start(bf16[144,1024]{1,0:T(8,128)(2,1)} %get-tuple-element.16), channel_id=1, source_target_pairs={{0,32},{1,33},{2,34},{3,35},{4,36},{5,37},{6,38},{7,39},{8,40},{9,... | collective-permute-start | bytes 884744 | tf_op jit(solution)/shard_map/ppermute | solution.py:23
  27.2 23.3 %collective-permute-start.1 = (bf16[528,1024]{1,0:T(8,128)(2,1)}, bf16[528,1024]{1,0:T(8,128)(2,1)S(1)}, u32[]{:S(2)}, u32[]{:S(2)}) collective-permute-start(bf16[528,1024]{1,0:T(8,128)(2,1)} %get-tuple-element.13.refs_9_), channel_id=1, source_target_pairs={{0,12},{1,13},{2,14},{3,15},{4,0},{5,1},{6,2},{7,3},{8,4},{9,5},{1... | collective-permute-start | bytes 3244040 | tf_op jit(solution)/shard_map/ppermute | solution.py:23
  28.5 26.1 %collective-permute-start = (bf16[528,1024]{1,0:T(8,128)(2,1)}, bf16[528,1024]{1,0:T(8,128)(2,1)}, u32[]{:S(2)}, u32[]{:S(2)}) collective-permute-start(bf16[528,1024]{1,0:T(8,128)(2,1)} %get-tuple-element.13.refs_9_), channel_id=1, source_target_pairs={{0,4},{1,5},{2,6},{3,7},{4,8},{5,9},{6,10},{7,11},{8,12},{9,13},{1... | collective-permute-start | bytes 3244040 | tf_op jit(solution)/shard_map/ppermute | solution.py:23
  38.2 17.9 %collective-permute-start.7 = (bf16[4,144,1024]{2,1,0:T(8,128)(2,1)S(1)}, bf16[4,144,1024]{2,1,0:T(8,128)(2,1)S(1)}, u32[]{:S(2)}, u32[]{:S(2)}) collective-permute-start(bf16[4,144,1024]{2,1,0:T(8,128)(2,1)S(1)} %pad_maximum_fusion.refs_0_), channel_id=1, source_target_pairs={{0,3},{1,0},{2,1},{3,2},{4,7},{5,4},{6,5},{7,6},{8,11},{9,8},{10,9... | collective-permute-start | bytes 3538952 | tf_op jit(solution)/shard_map/ppermute | solution.py:23
  41.0 19.6 %collective-permute-start.6 = (bf16[4,144,1024]{2,1,0:T(8,128)(2,1)S(1)}, bf16[4,144,1024]{2,1,0:T(8,128)(2,1)S(1)}, u32[]{:S(2)}, u32[]{:S(2)}) collective-permute-start(bf16[4,144,1024]{2,1,0:T(8,128)(2,1)S(1)} %pad_maximum_fusion.refs_0_), channel_id=1, source_target_pairs={{0,1},{1,2},{2,3},{3,0},{4,5},{5,6},{6,7},{7,4},{8,9},{9,10},{10,1... | collective-permute-start | bytes 3538952 | tf_op jit(solution)/shard_map/ppermute | solution.py:23
  50.5 10.9 %copy-start.1 = (bf16[528,1024]{1,0:T(8,128)(2,1)}, bf16[528,1024]{1,0:T(8,128)(2,1)S(1)}, u32[]{:S(2)}) copy-start(bf16[528,1024]{1,0:T(8,128)(2,1)S(1)} %collective-permute-done.1.refs_11_) | copy-start | bytes 3244036
  54.6 21.7 %collective-permute-start.2 = (bf16[528,1024]{1,0:T(8,128)(2,1)}, bf16[528,1024]{1,0:T(8,128)(2,1)}, u32[]{:S(2)}, u32[]{:S(2)}) collective-permute-start(bf16[528,1024]{1,0:T(8,128)(2,1)} %collective-permute-done.refs_10_), channel_id=1, source_target_pairs={{0,4},{1,5},{2,6},{3,7},{4,8},{5,9},{6,10},{7,11},{8,12},{9,13},{1... | collective-permute-start | bytes 3244040 | tf_op jit(solution)/shard_map/ppermute | solution.py:23
  57.0 10.7 %collective-permute-start.9 = (bf16[2,144,1024]{2,1,0:T(8,128)(2,1)}, bf16[2,144,1024]{2,1,0:T(8,128)(2,1)}, u32[]{:S(2)}, u32[]{:S(2)}) collective-permute-start(bf16[2,144,1024]{2,1,0:T(8,128)(2,1)} %slice.9), channel_id=1, source_target_pairs={{0,3},{1,0},{2,1},{3,2},{4,7},{5,4},{6,5},{7,6},{8,11},{9,8},{10,9... | collective-permute-start | bytes 1769480 | tf_op jit(solution)/shard_map/ppermute | solution.py:23
  61.4 10.6 %collective-permute-start.8 = (bf16[2,144,1024]{2,1,0:T(8,128)(2,1)}, bf16[2,144,1024]{2,1,0:T(8,128)(2,1)}, u32[]{:S(2)}, u32[]{:S(2)}) collective-permute-start(bf16[2,144,1024]{2,1,0:T(8,128)(2,1)} %slice.8), channel_id=1, source_target_pairs={{0,1},{1,2},{2,3},{3,0},{4,5},{5,6},{6,7},{7,4},{8,9},{9,10},{10,1... | collective-permute-start | bytes 1769480 | tf_op jit(solution)/shard_map/ppermute | solution.py:23
  62.1 15.3 %collective-permute-start.10 = (bf16[4,144,1024]{2,1,0:T(8,128)(2,1)S(1)}, bf16[4,144,1024]{2,1,0:T(8,128)(2,1)}, u32[]{:S(2)}, u32[]{:S(2)}) collective-permute-start(bf16[4,144,1024]{2,1,0:T(8,128)(2,1)S(1)} %pad_maximum_fusion.refs_0_), channel_id=1, source_target_pairs={{0,16},{1,17},{2,18},{3,19},{4,20},{5,21},{6,22},{7,23},{8,24},{9,... | collective-permute-start | bytes 3538952 | tf_op jit(solution)/shard_map/ppermute | solution.py:23
  63.1 14.4 %collective-permute-start.11 = (bf16[4,144,1024]{2,1,0:T(8,128)(2,1)S(1)}, bf16[4,144,1024]{2,1,0:T(8,128)(2,1)}, u32[]{:S(2)}, u32[]{:S(2)}) collective-permute-start(bf16[4,144,1024]{2,1,0:T(8,128)(2,1)S(1)} %collective-permute-done.6.refs_1_), channel_id=1, source_target_pairs={{0,16},{1,17},{2,18},{3,19},{4,20},{5,21},{6,22},{7,23},{8,24},{9,... | collective-permute-start | bytes 3538952 | tf_op jit(solution)/shard_map/ppermute | solution.py:23
  67.7 9.7 %collective-permute-start.12 = (bf16[4,144,1024]{2,1,0:T(8,128)(2,1)S(1)}, bf16[4,144,1024]{2,1,0:T(8,128)(2,1)}, u32[]{:S(2)}, u32[]{:S(2)}) collective-permute-start(bf16[4,144,1024]{2,1,0:T(8,128)(2,1)S(1)} %collective-permute-done.7.refs_2_), channel_id=1, source_target_pairs={{0,16},{1,17},{2,18},{3,19},{4,20},{5,21},{6,22},{7,23},{8,24},{9,... | collective-permute-start | bytes 3538952 | tf_op jit(solution)/shard_map/ppermute | solution.py:23
  74.4 4.7 %collective-permute-start.13 = (bf16[4,144,1024]{2,1,0:T(8,128)(2,1)}, bf16[4,144,1024]{2,1,0:T(8,128)(2,1)}, u32[]{:S(2)}, u32[]{:S(2)}) collective-permute-start(bf16[4,144,1024]{2,1,0:T(8,128)(2,1)} %pad_maximum_fusion.1), channel_id=1, source_target_pairs={{0,16},{1,17},{2,18},{3,19},{4,20},{5,21},{6,22},{7,23},{8,24},{9,... | collective-permute-start | bytes 3538952 | tf_op jit(solution)/shard_map/ppermute | solution.py:23
  79.0 1.2 %copy-start = (bf16[528,1024]{1,0:T(8,128)(2,1)S(1)}, bf16[528,1024]{1,0:T(8,128)(2,1)}, u32[]{:S(2)}) copy-start(bf16[528,1024]{1,0:T(8,128)(2,1)} %get-tuple-element.13.refs_9_) | copy-start | bytes 3244036
  80.3 1.2 %copy-start.2 = (bf16[528,1024]{1,0:T(8,128)(2,1)S(1)}, bf16[528,1024]{1,0:T(8,128)(2,1)}, u32[]{:S(2)}) copy-start(bf16[528,1024]{1,0:T(8,128)(2,1)} %copy-done.1) | copy-start | bytes 3244036
  81.5 0.7 copy-start.3

commit v8 on v6

--- a/solution.py
+++ b/solution.py
@@ -365,21 +365,21 @@
     c2 = send(cand, along_first(2))
     back_a = send(refs_a, along_x(1))
     ahead_a = send(refs_a, along_x(-1))
-    c1, c2, c3, hidden, pos = lax.optimization_barrier((c1, c2, c3, hidden, pos))
+    (refs_b,) = encode((3,), None, hidden, (), layer)
+    c1, c2, c3, refs_b, pos = lax.optimization_barrier((c1, c2, c3, refs_b, pos))
     own4 = jnp.stack([cand, c1, c2, c3])
     d1 = send(own4, along_second(1))
     d2 = send(own4, along_second(-1))
-    (refs_b,) = encode((3,), None, hidden, (), layer)
-    back_a, ahead_a, refs_b = lax.optimization_barrier((back_a, ahead_a, refs_b))
     back_b = send(refs_b, along_x(1))
     ahead_b = send(refs_b, along_x(-1))
+    back_a, ahead_a, back_b, ahead_b = lax.optimization_barrier((back_a, ahead_a, back_b, ahead_b))
     far_a = send(back_a, along_x(1))
+    far_b = send(back_b, along_x(1))
     d3 = send(d1[:2], along_second(1))
     d4 = send(d2[2:], along_second(-1))
     own4, d1, d2 = lax.optimization_barrier((own4, d1, d2))
     others = [send(v, to_other_core) for v in (own4, d1, d2)]
-    d3, d4, far_a, back_b, ahead_b = lax.optimization_barrier((d3, d4, far_a, back_b, ahead_b))
-    far_b = send(back_b, along_x(1))
+    d3, d4, far_a, far_b = lax.optimization_barrier((d3, d4, far_a, far_b))
     others += [send(v, to_other_core) for v in (d3, d4)]
     cands = [own4, d1, d2, d3, d4, *others]
     blocks = [refs_a, refs_b, back_a, back_b, ahead_a, ahead_b, far_a, far_b]

time: 104 us -> 106 us (1.019)
  blocking collectives: 15.8 us -> 18.9 us
  waiting for transfers between devices: 20.8 us -> 23.4 us
  Pallas kernels: 34.7 us -> 32.5 us
  starting transfers between devices: 28.2 us -> 27.1 us
    all_to_all x1, blocking collectives: 15.8 us -> 18.9 us  [on_device(): got = lax.all_to_all(payload, AXES, 0, 0)]
    ppermute x18, waiting for transfers between devices: 20.8 us -> 23.4 us  [send(): lax.ppermute(value, AXES, [(number(*a), number(*where(*a))) for a in GRID])]
    pallas_call x1, Pallas kernels: 8.41 us -> 6.13 us  [score_pairs(): pl.pallas_call(pair_kernel, in_specs=[smem] * 2 + [vmem] * len(blocks), o...]
  transfers between devices with their start and end apart: 18 -> 18, of which waited for: 7 -> 7; matrix products, arithmetic and copies ran while one was open for 1% -> 0% of each run, Pallas kernels for 9% -> 9%
where the time goes in v8:
time: 106 us
  Pallas kernels  32.5 us (31%)
  starting transfers between devices  27.1 us (26%)
  waiting for transfers between devices  23.4 us (22%)
  blocking collectives  18.9 us (18%)
  between operations  2.03 us (2%)
  local copies, waits for them, and re-layouts  1.7 us (2%)
    ppermute x18, starting transfers between devices, send(): lax.ppermute(value, AXES, [(number(*a), number(*where(*a))) for a in GRID])  27.1 us
    pallas_call x2, Pallas kernels, encode(): pl.pallas_call(functools.partial(encode_kernel, n_cand, picks, bool(words...  24.7 us
    ppermute x18, waiting for transfers between devices, send(): lax.ppermute(value, AXES, [(number(*a), number(*where(*a))) for a in GRID])  23.4 us
    all_to_all x1, blocking collectives, on_device(): got = lax.all_to_all(payload, AXES, 0, 0)  18.9 us
    pallas_call x1, Pallas kernels, score_pairs(): pl.pallas_call(pair_kernel, in_specs=[smem] * 2 + [vmem] * len(blocks), o...  6.13 us
  transfers between devices with their start and end apart: 18, of which 7 were waited for; matrix products, arithmetic and copies ran while one was open for 0% of the time, Pallas kernels for 9%

profile of v8, /device:TPU:1, one launch (start us, length us, event | category | flops | bytes accessed | tf_op | source)
XLA Modules:
  0.0 105.9 jit_solution(16609141234056546460)
XLA Ops:
  1.9 1.6 %pad_bitcast_fusion.refs_7_ = f32[400,128]{1,0:T(8,128)} fusion(f32[50265]{0:T(1024)} %param.22), kind=kLoop, calls=%fused_computation.1 | loop fusion | bytes 405860 | tf_op jit(solution)/shard_map/reshape | solution.py:339
  3.5 15.7 %encode.2 = (bf16[144,1024]{1,0:T(8,128)(2,1)}, bf16[400,1024]{1,0:T(8,128)(2,1)}) custom-call(s32[1]{0:T(128)} %bitcast.24.refs_0_, s32[4]{0:T(128)} %bitcast.43, s32[1]{0:T(128)} %bitcast.25.refs_2_, s32[1,128]{1,0:T(1,128)} %bitcast.44, s32[4,128]{1,0:T(4,128)} %bitcast.42, s32[1,32]{1,0:T(1,128)} %bitcast.45, s32[1,32]{1,0:T(1,128)} %bitcast.46, ...), custom_call_target="tpu_custom_call" | custom-call | flops 8589934592 | bytes 17825792 | tf_op jit(solution)/shard_map/encode/pallas_call | solution.py:142
  19.2 4.6 %collective-permute-start.2 = (bf16[144,1024]{1,0:T(8,128)(2,1)}, bf16[144,1024]{1,0:T(8,128)(2,1)S(1)}, u32[]{:S(2)}, u32[]{:S(2)}) collective-permute-start(bf16[144,1024]{1,0:T(8,128)(2,1)} %get-tuple-element.22), channel_id=1, source_target_pairs={{0,96},{1,97},{2,98},{3,99},{4,100},{5,101},{6,102},{7,103},{8,104... | collective-permute-start | bytes 884744 | tf_op jit(solution)/shard_map/ppermute | solution.py:23
  23.8 0.0 collective-permute-start.1
  23.8 0.7 collective-permute-start
  24.5 1.2 %collective-permute-start.8 = (bf16[400,1024]{1,0:T(8,128)(2,1)}, bf16[400,1024]{1,0:T(8,128)(2,1)S(1)}, u32[]{:S(2)}, u32[]{:S(2)}) collective-permute-start(bf16[400,1024]{1,0:T(8,128)(2,1)} %get-tuple-element.30.refs_10_), channel_id=1, source_target_pairs={{0,12},{1,13},{2,14},{3,15},{4,0},{5,1},{6,2},{7,3},{8,4},{9,5},{1... | collective-permute-start | bytes 2457608 | tf_op jit(solution)/shard_map/ppermute | solution.py:23
  25.7 1.5 %collective-permute-start.7 = (bf16[400,1024]{1,0:T(8,128)(2,1)}, bf16[400,1024]{1,0:T(8,128)(2,1)S(1)}, u32[]{:S(2)}, u32[]{:S(2)}) collective-permute-start(bf16[400,1024]{1,0:T(8,128)(2,1)} %get-tuple-element.30.refs_10_), channel_id=1, source_target_pairs={{0,4},{1,5},{2,6},{3,7},{4,8},{5,9},{6,10},{7,11},{8,12},{9,13},{1... | collective-permute-start | bytes 2457608 | tf_op jit(solution)/shard_map/ppermute | solution.py:23
  27.2 0.1 pad_add_fusion.pos_ref
  27.3 0.0 copy-start.2
  27.3 9.1 %encode.3.refs_11_ = bf16[128,1024]{1,0:T(8,128)(2,1)} custom-call(bf16[4,128,1024]{2,1,0:T(8,128)(2,1)} %bitcast.28, bf16[1024,4096]{1,0:T(8,128)(2,1)} %refs_1_.1, f32[1,4096]{1,0:T(1,128)} %bitcast.34, bf16[4096,1024]{1,0:T(8,128)(2,1)} %refs_3_.1, f32[1,1024]{1,0:T(1,128)} %bitcast.36, f32[1,1024]{1,0:T(1,128)} %bitcast.38, f32[1,1024]{1,0:T(1,128)} %bitcast.40), custom_call_target="tpu_custom_call" | custom-call | flops 2147483648 | bytes 17825792 | tf_op jit(solution)/shard_map/encode/pallas_call | solution.py:142
  36.3 0.0 collective-permute-done.2
  36.3 0.0 collective-permute-done.1
  36.3 0.0 collective-permute-done
  36.3 0.1 collective-permute-start.10
  36.4 0.0 copy-done.2
  36.4 0.0 copy-start
  36.4 0.2 pad_maximum_fusion.refs_0_
  36.6 0.0 copy-start.1
  36.6 2.8 %collective-permute-start.4 = (bf16[4,144,1024]{2,1,0:T(8,128)(2,1)S(1)}, bf16[4,144,1024]{2,1,0:T(8,128)(2,1)S(1)}, u32[]{:S(2)}, u32[]{:S(2)}) collective-permute-start(bf16[4,144,1024]{2,1,0:T(8,128)(2,1)S(1)} %pad_maximum_fusion.refs_0_), channel_id=1, source_target_pairs={{0,3},{1,0},{2,1},{3,2},{4,7},{5,4},{6,5},{7,6},{8,11},{9,8},{10,9... | collective-permute-start | bytes 3538952 | tf_op jit(solution)/shard_map/ppermute | solution.py:23
  39.4 0.0 collective-permute-start.3
  39.4 8.3 %collective-permute-done.10.refs_15_ = bf16[128,1024]{1,0:T(8,128)(2,1)S(1)} collective-permute-done((bf16[128,1024]{1,0:T(8,128)(2,1)}, bf16[128,1024]{1,0:T(8,128)(2,1)S(1)}, u32[]{:S(2)}, u32[]{:S(2)}) %collective-permute-start.10) | collective-permute-done | bytes 262176 | tf_op jit(solution)/shard_map/ppermute | solution.py:23
  47.7 0.0 copy-done
  47.7 2.6 %collective-permute-start.9 = (bf16[128,1024]{1,0:T(8,128)(2,1)S(1)}, bf16[128,1024]{1,0:T(8,128)(2,1)S(1)}, u32[]{:S(2)}, u32[]{:S(2)}) collective-permute-start(bf16[128,1024]{1,0:T(8,128)(2,1)S(1)} %copy-done), channel_id=1, source_target_pairs={{0,4},{1,5},{2,6},{3,7},{4,8},{5,9},{6,10},{7,11},{8,12},{9,13},{1... | collective-permute-start | bytes 786440 | tf_op jit(solution)/shard_map/ppermute | solution.py:23
  50.3 3.3 %collective-permute-done.9.refs_13_ = bf16[128,1024]{1,0:T(8,128)(2,1)S(1)} collective-permute-done((bf16[128,1024]{1,0:T(8,128)(2,1)S(1)}, bf16[128,1024]{1,0:T(8,128)(2,1)S(1)}, u32[]{:S(2)}, u32[]{:S(2)}) %collective-permute-start.9) | collective-permute-done | bytes 262176 | tf_op jit(solution)/shard_map/ppermute | solution.py:23
  53.6 0.0 collective-permute-done.8.refs_14_
  53.6 0.0 collective-permute-done.7.refs_12_
  53.6 3.4 %collective-permute-start.11 = (bf16[400,1024]{1,0:T(8,128)(2,1)S(1)}, bf16[400,1024]{1,0:T(8,128)(2,1)S(1)}, u32[]{:S(2)}, u32[]{:S(2)}) collective-permute-start(bf16[400,1024]{1,0:T(8,128)(2,1)S(1)} %collective-permute-done.7.refs_12_), channel_id=1, source_target_pairs={{0,4},{1,5},{2,6},{3,7},{4,8},{5,9},{6,10},{7,11},{8,12},{9,13},{1... | collective-permute-start | bytes 2457608 | tf_op jit(solution)/shard_map/ppermute | solution.py:23
  57.0 0.1 collective-permute-start.12
  57.1 0.0 collective-permute-done.4.refs_2_
  57.1 2.8 %collective-permute-start.6 = (bf16[2,144,1024]{2,1,0:T(8,128)(2,1)S(1)}, bf16[2,144,1024]{2,1,0:T(8,128)(2,1)S(1)}, u32[]{:S(2)}, u32[]{:S(2)}) collective-permute-start(bf16[2,144,1024]{2,1,0:T(8,128)(2,1)S(1)} %slice.9), channel_id=1, source_target_pairs={{0,3},{1,0},{2,1},{3,2},{4,7},{5,4},{6,5},{7,6},{8,11},{9,8},{10,9... | collective-permute-start | bytes 1769480 | tf_op jit(solution)/shard_map/ppermute | solution.py:23
  59.9 0.0 collective-permute-done.3.refs_1_
  60.0 0.1 collective-permute-start.5
  60.1 2.5 %collective-permute-start.13 = (bf16[4,144,1024]{2,1,0:T(8,128)(2,1)S(1)}, bf16[4,144,1024]{2,1,0:T(8,128)(2,1)S(1)}, u32[]{:S(2)}, u32[]{:S(2)}) collective-permute-start(bf16[4,144,1024]{2,1,0:T(8,128)(2,1)S(1)} %pad_maximum_fusion.refs_0_), channel_id=1, source_target_pairs={{0,16},{1,17},{2,18},{3,19},{4,20},{5,21},{6,22},{7,23},{8,24},{9,... | collective-permute-start | bytes 3538952 | tf_op jit(solution)/shard_map/ppermute | solution.py:23
  62.6 6.5 %collective-permute-done.12.refs_17_ = bf16[128,1024]{1,0:T(8,128)(2,1)S(1)} collective-permute-done((bf16[128,1024]{1,0:T(8,128)(2,1)S(1)}, bf16[128,1024]{1,0:T(8,128)(2,1)S(1)}, u32[]{:S(2)}, u32[]{:S(2)}) %collective-permute-start.12) | collective-permute-done | bytes 262176 | tf_op jit(solution)/shard_map/ppermute | solution.py:23
  69.1 4.2 %collective-permute-start.14 = (bf16[4,144,1024]{2,1,0:T(8,128)(2,1)S(1)}, bf16[4,144,1024]{2,1,0:T(8,128)(2,1)S(1)}, u32[]{:S(2)}, u32[]{:S(2)}) collective-permute-start(bf16[4,144,1024]{2,1,0:T(8,128)(2,1)S(1)} %collective-permute-done.3.refs_1_), channel_id=1, source_target_pairs={{0,16},{1,17},{2,18},{3,19},{4,20},{5,21},{6,22},{7,23},{8,24},{9,... | collective-permute-start | bytes 3538952 | tf_op jit(solution)/shard_map/ppermute | solution.py:23
  73.4 0.0 collective-permute-done.11.refs_16_
  73.4 0.0 collective-permute-start.15
  73.4 0.0 collective-permute-done.6.refs_4_
  73.4 0.0 collective-permute-done.5.refs_3_
  73.4 0.5 collective-permute-start.16
  73.9 0.1 collective-permute-start.17
  74.0 0.0 collective-permute-done.13.refs_5_
  74.0 1.9 %collective-permute-done.14.refs_6_ = bf16[4,144,1024]{2,1,0:T(8,128)(2,1)S(1)} collective-permute-done((bf16[4,144,1024]{2,1,0:T(8,128)(2,1)S(1)}, bf16[4,144,1024]{2,1,0:T(8,128)(2,1)S(1)}, u32[]{:S(2)}, u32[]{:S(2)}) %collective-permute-start.14) | collective-permute-done | bytes 1179680 | tf_op jit(solution)/shard_map/ppermute | solution.py:23
  75.8 1.7 %collective-permute-done.15.refs_7_ = bf16[4,144,1024]{2,1,0:T(8,128)(2,1)S(1)} collective-permute-done((bf16[4,144,1024]{2,1,0:T(8,128)(2,1)S(1)}, bf16[4,144,1024]{2,1,0:T(8,128)(2,1)S(1)}, u32[]{:S(2)}, u32[]{:S(2)}) %collective-permute-start.15) | collective-permute-done | bytes 1179680 | tf_op jit(solution)/shard_map/ppermute | solution.py:23
  77.5 0.8 collective-permute-done.16.refs_8_
  78.4 0.8 collective-permute-done.17.refs_9_
  79.2 0.0 copy-done.1
  79.2 6.1 %score_pairs.1 = f32[128,1,128]{2,1,0:T(1,128)S(1)} custom-call(s32[4]{0:T(128)S(1)} %pad_add_fusion.pos_ref, s32[1]{0:T(128)} %bitcast.26.count_ref, bf16[4,144,1024]{2,1,0:T(8,128)(2,1)S(1)} %pad_maximum_fusion.refs_0_, bf16[4,144,1024]{2,1,0:T(8,128)(2,1)S(1)} %collective-permute-done.3.refs_1_, bf16[4,144,1024]{2,1,0:T(8,128)(2,1)S(1)} %collective-permute-done.4.refs_2_, ...), custom_call_target="tpu_custom_call" | custom-call | tf_op jit(solution)/shard_map/score_pairs/pallas_call | solution.py:316
  85.4 18.9 %all_to_all.5.got_ref = f32[128,1,128]{2,1,0:T(1,128)} all-to-all(f32[128,1,128]{2,1,0:T(1,128)S(1)} %score_pairs.1), channel_id=1, replica_groups=mesh['dp'=8,'prompt'=16] {'dp','prompt'}, dimensions={0} | all-to-all | bytes 131072 | tf_op jit(solution)/shard_map/all_to_all | solution.py:387
  104.3 1.6 %finish.1 = (f32[3,1,1,32]{3,2,1,0:T(1,128)}, f32[1,3]{1,0:T(1,128)}) custom-call(f32[128,1,128]{2,1,0:T(1,128)} %all_to_all.5.got_ref), custom_call_target="tpu_custom_call" | custom-call | tf_op jit(solution)/shard_map/finish/pallas_call | solution.py:388
  (2 shorter events, 0.1 us)
Async XLA Ops:
  19.2 17.1 %collective-permute-start.2 = (bf16[144,1024]{1,0:T(8,128)(2,1)}, bf16[144,1024]{1,0:T(8,128)(2,1)S(1)}, u32[]{:S(2)}, u32[]{:S(2)}) collective-permute-start(bf16[144,1024]{1,0:T(8,128)(2,1)} %get-tuple-element.22), channel_id=1, source_target_pairs={{0,96},{1,97},{2,98},{3,99},{4,100},{5,101},{6,102},{7,103},{8,104... | collective-permute-start | bytes 884744 | tf_op jit(solution)/shard_map/ppermute | solution.py:23
  23.8 12.5 %collective-permute-start.1 = (bf16[144,1024]{1,0:T(8,128)(2,1)}, bf16[144,1024]{1,0:T(8,128)(2,1)S(1)}, u32[]{:S(2)}, u32[]{:S(2)}) collective-permute-start(bf16[144,1024]{1,0:T(8,128)(2,1)} %get-tuple-element.22), channel_id=1, source_target_pairs={{0,64},{1,65},{2,66},{3,67},{4,68},{5,69},{6,70},{7,71},{8,72},{9,... | collective-permute-start | bytes 884744 | tf_op jit(solution)/shard_map/ppermute | solution.py:23
  23.8 12.5 %collective-permute-start = (bf16[144,1024]{1,0:T(8,128)(2,1)}, bf16[144,1024]{1,0:T(8,128)(2,1)S(1)}, u32[]{:S(2)}, u32[]{:S(2)}) collective-permute-start(bf16[144,1024]{1,0:T(8,128)(2,1)} %get-tuple-element.22), channel_id=1, source_target_pairs={{0,32},{1,33},{2,34},{3,35},{4,36},{5,37},{6,38},{7,39},{8,40},{9,... | collective-permute-start | bytes 884744 | tf_op jit(solution)/shard_map/ppermute | solution.py:23
  24.5 29.1 %collective-permute-start.8 = (bf16[400,1024]{1,0:T(8,128)(2,1)}, bf16[400,1024]{1,0:T(8,128)(2,1)S(1)}, u32[]{:S(2)}, u32[]{:S(2)}) collective-permute-start(bf16[400,1024]{1,0:T(8,128)(2,1)} %get-tuple-element.30.refs_10_), channel_id=1, source_target_pairs={{0,12},{1,13},{2,14},{3,15},{4,0},{5,1},{6,2},{7,3},{8,4},{9,5},{1... | collective-permute-start | bytes 2457608 | tf_op jit(solution)/shard_map/ppermute | solution.py:23
  25.7 27.9 %collective-permute-start.7 = (bf16[400,1024]{1,0:T(8,128)(2,1)}, bf16[400,1024]{1,0:T(8,128)(2,1)S(1)}, u32[]{:S(2)}, u32[]{:S(2)}) collective-permute-start(bf16[400,1024]{1,0:T(8,128)(2,1)} %get-tuple-element.30.refs_10_), channel_id=1, source_target_pairs={{0,4},{1,5},{2,6},{3,7},{4,8},{5,9},{6,10},{7,11},{8,12},{9,13},{1... | collective-permute-start | bytes 2457608 | tf_op jit(solution)/shard_map/ppermute | solution.py:23
  27.3 9.2 %copy-start.2 = (bf16[144,1024]{1,0:T(8,128)(2,1)S(1)}, bf16[144,1024]{1,0:T(8,128)(2,1)}, u32[]{:S(2)}) copy-start(bf16[144,1024]{1,0:T(8,128)(2,1)} %get-tuple-element.22) | copy-start | bytes 884740
  36.3 11.4 %collective-permute-start.10 = (bf16[128,1024]{1,0:T(8,128)(2,1)}, bf16[128,1024]{1,0:T(8,128)(2,1)S(1)}, u32[]{:S(2)}, u32[]{:S(2)}) collective-permute-start(bf16[128,1024]{1,0:T(8,128)(2,1)} %encode.3.refs_11_), channel_id=1, source_target_pairs={{0,12},{1,13},{2,14},{3,15},{4,0},{5,1},{6,2},{7,3},{8,4},{9,5},{1... | collective-permute-start | bytes 786440 | tf_op jit(solution)/shard_map/ppermute | solution.py:23
  36.4 11.3 %copy-start = (bf16[128,1024]{1,0:T(8,128)(2,1)S(1)}, bf16[128,1024]{1,0:T(8,128)(2,1)}, u32[]{:S(2)}) copy-start(bf16[128,1024]{1,0:T(8,128)(2,1)} %encode.3.refs_11_) | copy-start | bytes 786436
  36.6 42.6 %copy-start.1 = (bf16[400,1024]{1,0:T(8,128)(2,1)S(1)}, bf16[400,1024]{1,0:T(8,128)(2,1)}, u32[]{:S(2)}) copy-start(bf16[400,1024]{1,0:T(8,128)(2,1)} %get-tuple-element.30.refs_10_) | copy-start | bytes 2457604
  36.6 20.5 %collective-permute-start.4 = (bf16[4,144,1024]{2,1,0:T(8,128)(2,1)S(1)}, bf16[4,144,1024]{2,1,0:T(8,128)(2,1)S(1)}, u32[]{:S(2)}, u32[]{:S(2)}) collective-permute-start(bf16[4,144,1024]{2,1,0:T(8,128)(2,1)S(1)} %pad_maximum_fusion.refs_0_), channel_id=1, source_target_pairs={{0,3},{1,0},{2,1},{3,2},{4,7},{5,4},{6,5},{7,6},{8,11},{9,8},{10,9... | collective-permute-start | bytes 3538952 | tf_op jit(solution)/shard_map/ppermute | solution.py:23
  39.4 20.5 %collective-permute-start.3 = (bf16[4,144,1024]{2,1,0:T(8,128)(2,1)S(1)}, bf16[4,144,1024]{2,1,0:T(8,128)(2,1)S(1)}, u32[]{:S(2)}, u32[]{:S(2)}) collective-permute-start(bf16[4,144,1024]{2,1,0:T(8,128)(2,1)S(1)} %pad_maximum_fusion.refs_0_), channel_id=1, source_target_pairs={{0,1},{1,2},{2,3},{3,0},{4,5},{5,6},{6,7},{7,4},{8,9},{9,10},{10,1... | collective-permute-start | bytes 3538952 | tf_op jit(solution)/shard_map/ppermute | solution.py:23
  47.7 5.9 %collective-permute-start.9 = (bf16[128,1024]{1,0:T(8,128)(2,1)S(1)}, bf16[128,1024]{1,0:T(8,128)(2,1)S(1)}, u32[]{:S(2)}, u32[]{:S(2)}) collective-permute-start(bf16[128,1024]{1,0:T(8,128)(2,1)S(1)} %copy-done), channel_id=1, source_target_pairs={{0,4},{1,5},{2,6},{3,7},{4,8},{5,9},{6,10},{7,11},{8,12},{9,13},{1... | collective-permute-start | bytes 786440 | tf_op jit(solution)/shard_map/ppermute | solution.py:23
  53.6 19.8 %collective-permute-start.11 = (bf16[400,1024]{1,0:T(8,128)(2,1)S(1)}, bf16[400,1024]{1,0:T(8,128)(2,1)S(1)}, u32[]{:S(2)}, u32[]{:S(2)}) collective-permute-start(bf16[400,1024]{1,0:T(8,128)(2,1)S(1)} %collective-permute-done.7.refs_12_), channel_id=1, source_target_pairs={{0,4},{1,5},{2,6},{3,7},{4,8},{5,9},{6,10},{7,11},{8,12},{9,13},{1... | collective-permute-start | bytes 2457608 | tf_op jit(solution)/shard_map/ppermute | solution.py:23
  57.0 12.1 %collective-permute-start.12 = (bf16[128,1024]{1,0:T(8,128)(2,1)S(1)}, bf16[128,1024]{1,0:T(8,128)(2,1)S(1)}, u32[]{:S(2)}, u32[]{:S(2)}) collective-permute-start(bf16[128,1024]{1,0:T(8,128)(2,1)S(1)} %collective-permute-done.9.refs_13_), channel_id=1, source_target_pairs={{0,4},{1,5},{2,6},{3,7},{4,8},{5,9},{6,10},{7,11},{8,12},{9,13},{1... | collective-permute-start | bytes 786440 | tf_op jit(solution)/shard_map/ppermute | solution.py:23
  57.1 16.2 %collective-permute-start.6 = (bf16[2,144,1024]{2,1,0:T(8,128)(2,1)S(1)}, bf16[2,144,1024]{2,1,0:T(8,128)(2,1)S(1)}, u32[]{:S(2)}, u32[]{:S(2)}) collective-permute-start(bf16[2,144,1024]{2,1,0:T(8,128)(2,1)S(1)} %slice.9), channel_id=1, source_target_pairs={{0,3},{1,0},{2,1},{3,2},{4,7},{5,4},{6,5},{7,6},{8,11},{9,8},{10,9... | collective-permute-start | bytes 1769480 | tf_op jit(solution)/shard_map/ppermute | solution.py:23
  60.0 13.4 %collective-permute-start.5 = (bf16[2,144,1024]{2,1,0:T(8,128)(2,1)S(1)}, bf16[2,144,1024]{2,1,0:T(8,128)(2,1)S(1)}, u32[]{:S(2)}, u32[]{:S(2)}) collective-permute-start(bf16[2,144,1024]{2,1,0:T(8,128)(2,1)S(1)} %slice.8), channel_id=1, source_target_pairs={{0,1},{1,2},{2,3},{3,0},{4,5},{5,6},{6,7},{7,4},{8,9},{9,10},{10,1... | collective-permute-start | bytes 1769480 | tf_op jit(solution)/shard_map/ppermute | solution.py:23
  60.1 13.9 %collective-permute-start.13 = (bf16[4,144,1024]{2,1,0:T(8,128)(2,1)S(1)}, bf16[4,144,1024]{2,1,0:T(8,128)(2,1)S(1)}, u32[]{:S(2)}, u32[]{:S(2)}) collective-permute-start(bf16[4,144,1024]{2,1,0:T(8,128)(2,1)S(1)} %pad_maximum_fusion.refs_0_), channel_id=1, source_target_pairs={{0,16},{1,17},{2,18},{3,19},{4,20},{5,21},{6,22},{7,23},{8,24},{9,... | collective-permute-start | bytes 3538952 | tf_op jit(solution)/shard_map/ppermute | solution.py:23
  69.1 6.7 %collective-permute-start.14 = (bf16[4,144,1024]{2,1,0:T(8,128)(2,1)S(1)}, bf16[4,144,1024]{2,1,0:T(8,128)(2,1)S(1)}, u32[]{:S(2)}, u32[]{:S(2)}) collective-permute-start(bf16[4,144,1024]{2,1,0:T(8,128)(2,1)S(1)} %collective-permute-done.3.refs_1_), channel_id=1, source_target_pairs={{0,16},{1,17},{2,18},{3,19},{4,20},{5,21},{6,22},{7,23},{8,24},{9,... | collective-permute-start | bytes 3538952 | tf_op jit(solution)/shard_map/ppermute | solution.py:23
  73.4 4.2 %collective-permute-start.15 = (bf16[4,144,1024]{2,1,0:T(8,128)(2,1)S(1)}, bf16[4,144,1024]{2,1,0:T(8,128)(2,1)S(1)}, u32[]{:S(2)}, u32[]{:S(2)}) collective-permute-start(bf16[4,144,1024]{2,1,0:T(8,128)(2,1)S(1)} %collective-permute-done.4.refs_2_), channel_id=1, source_target_pairs={{0,16},{1,17},{2,18},{3,19},{4,20},{5,21},{6,22},{7,23},{8,24},{9,... | collective-permute-start | bytes 3538952 | tf_op jit(solution)/shard_map/ppermute | solution.py:23
  73.4 5.0 %collective-permute-start.16 = (bf16[2,144,1024]{2,1,0:T(8,128)(2,1)S(1)}, bf16[2,144,1024]{2,1,0:T(8,128)(2,1)S(1)}, u32[]{:S(2)}, u32[]{:S(2)}) collective-permute-start(bf16[2,144,1024]{2,1,0:T(8,128)(2,1)S(1)} %collective-permute-done.5.refs_3_), channel_id=1, source_target_pairs={{0,16},{1,17},{2,18},{3,19},{4,20},{5,21},{6,22},{7,23},{8,24},{9,... | collective-permute-start | bytes 1769480 | tf_op jit(solution)/shard_map/ppermute | solution.py:23
  73.9 5.3 %collective-permute-start.17 = (bf16[2,144,1024]{2,1,0:T(8,128)(2,1)S(1)}, bf16[2,144,1024]{2,1,0:T(8,128)(2,1)S(1)}, u32[]{:S(2)}, u32[]{:S(2)}) collective-permute-start(bf16[2,144,1024]{2,1,0:T(8,128)(2,1)S(1)} %collective-permute-done.6.refs_4_), channel_id=1, source_target_pairs={{0,16},{1,17},{2,18},{3,19},{4,20},{5,21},{6,22},{7,23},{8,24},{9,... | collective-permute-start | bytes 1769480 | tf_op jit(solution)/shard_map/ppermute | solution.py:23

commit v9 on v6

--- a/solution.py
+++ b/solution.py
@@ -56,17 +56,6 @@
     step = pl.program_id(0)
     seqs = n_cand + len(picks)
 
-    def token_weights(ids, length):
-        high, low = ids >> 7, ids & 127
-        hot = (lax.broadcasted_iota(jnp.int32, (TABLE_ROWS, L), 0) == high).astype(jnp.bfloat16)
-        rows = lax.dot_general(
-            tbl_ref[...].astype(jnp.bfloat16), hot, (((0,), (0,)), ((), ())), preferred_element_type=jnp.float32
-        )
-        mine = lax.broadcasted_iota(jnp.int32, (128, L), 0) == low
-        value = jnp.sum(jnp.where(mine, rows, 0.0), axis=0, keepdims=True)
-        live = lax.broadcasted_iota(jnp.int32, (1, L), 1) < length
-        return jnp.where(live, value, 0.0)
-
     @pl.when(step == 0)
     def _():
         if n_cand:
@@ -74,17 +63,36 @@
         for k, q in enumerate(picks):
             x_ref[L * (n_cand + k) : L * (n_cand + k + 1), :] = rh_ref[q]
         if weights:
+            full = tbl_ref.shape[0] // 1024
+            rest = tbl_ref.shape[0] - full * 1024
+            pieces = [tbl_ref[pl.ds(k * 1024, 1024)].reshape(8, 128) for k in range(full)]
+            end = jnp.concatenate([tbl_ref[pl.ds(full * 1024, rest)], jnp.zeros((1024 - rest,), jnp.float32)])
+            table = jnp.concatenate(pieces + [end.reshape(8, 128)], axis=0).astype(jnp.bfloat16)
+            ids = jnp.concatenate([cid_ref[...]] + [rid_ref[q : q + 1, :] for q in range(4)], axis=1)
+            high, low = ids >> 7, ids & 127
+            hot = lax.broadcasted_iota(jnp.int32, (TABLE_ROWS, 5 * L), 0) == high
+            rows = lax.dot_general(
+                table, hot.astype(jnp.bfloat16), (((0,), (0,)), ((), ())),
+                preferred_element_type=jnp.float32,
+            )
+            mine = lax.broadcasted_iota(jnp.int32, (128, 5 * L), 0) == low
+            value = jnp.sum(jnp.where(mine, rows, 0.0), axis=0, keepdims=True)
+            place = lax.broadcasted_iota(jnp.int32, (1, L), 1)
+
+            def token_weights(k, length):
+                return jnp.where(place < length, value[:, k * L : (k + 1) * L], 0.0)
+
             row = lax.broadcasted_iota(jnp.int32, (16, L), 0)
             co_ref[L:, :] = jnp.zeros((16, D), jnp.bfloat16)
             ro_ref[len(picks) * L :, :] = jnp.zeros((16, D), jnp.bfloat16)
-            w = token_weights(cid_ref[...], clen_ref[0])
+            w = token_weights(0, clen_ref[0])
             count = jnp.full((1, 2 * SLOTS), count_ref[0], jnp.int32)
             slots = jnp.concatenate([pc_ref[...], pr_ref[...], count], axis=1).astype(jnp.float32)
             words = jnp.where(row == 0, w, jnp.where(row == 1, slots, 0.0))
             co_ref[L:, 0:L] = words.astype(jnp.bfloat16)
             block = jnp.zeros((16, L), jnp.float32)
             for q in range(4):
-                block = jnp.where(row == q, token_weights(rid_ref[q : q + 1, :], rlen_ref[q]), block)
+                block = jnp.where(row == q, token_weights(q + 1, rlen_ref[q]), block)
             ro_ref[len(picks) * L :, 0:L] = block.astype(jnp.bfloat16)
 
     w = up.shape[1] // sub
@@ -336,7 +344,6 @@
     cand_hidden, ref_hidden, cand_ids, ref_ids, cand_len, reference_length, idf_table, up_weight,
     up_bias, down_weight, down_bias, norm_gain, norm_bias, pair_cand, pair_ref, pair_count,
 ):
-    table = jnp.pad(idf_table, (0, TABLE_ROWS * 128 - idf_table.shape[0])).reshape(TABLE_ROWS, 128)
     count = pair_count.reshape(1)
     dp, prompt = lax.axis_index("dp"), lax.axis_index("prompt")
     pos = jnp.stack([dp >> 1, dp & 1, prompt >> 2, prompt & 3]).astype(jnp.int32)
@@ -357,7 +364,7 @@
         ref_ids.reshape(4, L),
         pair_cand.reshape(1, SLOTS),
         pair_ref.reshape(1, SLOTS),
-        table,
+        idf_table,
     )
     cand, refs_a = encode((0, 1, 2), cand_hidden.reshape(1, L, D), hidden, words, layer)
     c1 = send(cand, along_first(1))

time: 104 us -> 101 us (0.971); the launches traced: 104 us -> 100 us
  local copies, waits for them, and re-layouts: 1.7 us -> 0.09 us
  Pallas kernels: 34.7 us -> 33.4 us
  blocking collectives: 15.8 us -> 14.6 us
    reshape x1 -> x0, local copies, waits for them, and re-layouts: 1.62 us -> none  [on_device(): jnp.pad(idf_table, (0, TABLE_ROWS * 128 - idf_table.shape[0]))]
    pallas_call x1, Pallas kernels: 8.41 us -> 7.1 us  [score_pairs(): pl.pallas_call(pair_kernel, in_specs=[smem] * 2 + [vmem] * len(blocks), o...]
    all_to_all x1, blocking collectives: 15.8 us -> 14.6 us  [on_device(): got = lax.all_to_all(payload, AXES, 0, 0)]
where the time goes in v9:
time: 101 us; the launch traced here: 100 us
  Pallas kernels  33.4 us (33%)
  starting transfers between devices  28.2 us (28%)
  waiting for transfers between devices  20.7 us (20%)
  blocking collectives  14.6 us (14%)
  between operations  2 us (2%)
  other arithmetic  1.19 us (1%)
    ppermute x18, starting transfers between devices, send(): lax.ppermute(value, AXES, [(number(*a), number(*where(*a))) for a in GRID])  28.2 us
    pallas_call x2, Pallas kernels, encode(): pl.pallas_call(functools.partial(encode_kernel, n_cand, picks, bool(words...  24.6 us
    ppermute x18, waiting for transfers between devices, send(): lax.ppermute(value, AXES, [(number(*a), number(*where(*a))) for a in GRID])  20.7 us
    all_to_all x1, blocking collectives, on_device(): got = lax.all_to_all(payload, AXES, 0, 0)  14.6 us
    pallas_call x1, Pallas kernels, score_pairs(): pl.pallas_call(pair_kernel, in_specs=[smem] * 2 + [vmem] * len(blocks), o...  7.1 us
  transfers between devices with their start and end apart: 18, of which 7 were waited for; matrix products, arithmetic and copies ran while one was open for 1% of the time, Pallas kernels for 9%

profile of v9, /device:TPU:1, one launch (start us, length us, event | category | flops | bytes accessed | tf_op | source)
XLA Modules:
  0.0 100.2 jit_solution(7930236743114664560)
XLA Ops:
  1.9 15.6 %encode.2 = (bf16[144,1024]{1,0:T(8,128)(2,1)}, bf16[400,1024]{1,0:T(8,128)(2,1)}) custom-call(s32[1]{0:T(128)} %bitcast.22.refs_0_, s32[4]{0:T(128)} %bitcast.41, s32[1]{0:T(128)} %bitcast.23.refs_2_, s32[1,128]{1,0:T(1,128)} %bitcast.42, s32[4,128]{1,0:T(4,128)} %bitcast.40, s32[1,32]{1,0:T(1,128)} %bitcast.43, s32[1,32]{1,0:T(1,128)} %bitcast.44, ...), custom_call_target="tpu_custom_call" | custom-call | flops 8589934592 | bytes 17825792 | tf_op jit(solution)/shard_map/encode/pallas_call | solution.py:150
  17.5 4.6 %collective-permute-start.2 = (bf16[144,1024]{1,0:T(8,128)(2,1)}, bf16[144,1024]{1,0:T(8,128)(2,1)S(1)}, u32[]{:S(2)}, u32[]{:S(2)}) collective-permute-start(bf16[144,1024]{1,0:T(8,128)(2,1)} %get-tuple-element.22), channel_id=1, source_target_pairs={{0,96},{1,97},{2,98},{3,99},{4,100},{5,101},{6,102},{7,103},{8,104... | collective-permute-start | bytes 884744 | tf_op jit(solution)/shard_map/ppermute | solution.py:23
  22.1 0.0 collective-permute-start.1
  22.1 0.7 collective-permute-start
  22.8 1.2 %collective-permute-start.8 = (bf16[400,1024]{1,0:T(8,128)(2,1)}, bf16[400,1024]{1,0:T(8,128)(2,1)}, u32[]{:S(2)}, u32[]{:S(2)}) collective-permute-start(bf16[400,1024]{1,0:T(8,128)(2,1)} %get-tuple-element.30.refs_10_), channel_id=1, source_target_pairs={{0,12},{1,13},{2,14},{3,15},{4,0},{5,1},{6,2},{7,3},{8,4},{9,5},{1... | collective-permute-start | bytes 2457608 | tf_op jit(solution)/shard_map/ppermute | solution.py:23
  24.0 1.5 %collective-permute-start.7 = (bf16[400,1024]{1,0:T(8,128)(2,1)}, bf16[400,1024]{1,0:T(8,128)(2,1)}, u32[]{:S(2)}, u32[]{:S(2)}) collective-permute-start(bf16[400,1024]{1,0:T(8,128)(2,1)} %get-tuple-element.30.refs_10_), channel_id=1, source_target_pairs={{0,4},{1,5},{2,6},{3,7},{4,8},{5,9},{6,10},{7,11},{8,12},{9,13},{1... | collective-permute-start | bytes 2457608 | tf_op jit(solution)/shard_map/ppermute | solution.py:23
  25.5 0.1 pad_add_fusion.pos_ref
  25.6 3.7 %collective-permute-done.2 = bf16[144,1024]{1,0:T(8,128)(2,1)S(1)} collective-permute-done((bf16[144,1024]{1,0:T(8,128)(2,1)}, bf16[144,1024]{1,0:T(8,128)(2,1)S(1)}, u32[]{:S(2)}, u32[]{:S(2)}) %collective-permute-start.2) | collective-permute-done | bytes 294944 | tf_op jit(solution)/shard_map/ppermute | solution.py:23
  29.3 0.5 collective-permute-done.1
  29.7 2.9 %collective-permute-done = bf16[144,1024]{1,0:T(8,128)(2,1)S(1)} collective-permute-done((bf16[144,1024]{1,0:T(8,128)(2,1)}, bf16[144,1024]{1,0:T(8,128)(2,1)S(1)}, u32[]{:S(2)}, u32[]{:S(2)}) %collective-permute-start) | collective-permute-done | bytes 294944 | tf_op jit(solution)/shard_map/ppermute | solution.py:23
  32.7 1.1 %pad_maximum_fusion.refs_0_ = bf16[4,144,1024]{2,1,0:T(8,128)(2,1)S(1)} fusion(bf16[1,144,1024]{2,1,0:T(8,128)(2,1)S(1)} %bitcast.28, bf16[1,144,1024]{2,1,0:T(8,128)(2,1)S(1)} %bitcast.29, bf16[1,144,1024]{2,1,0:T(8,128)(2,1)S(1)} %bitcast.30, bf16[1,144,1024]{2,1,0:T(8,128)(2,1)} %bitcast.27), kind=kLoop, calls=%fused_computation | loop fusion | flops 1769472 | bytes 2359296 | tf_op jit(solution)/shard_map/stack | solution.py:376
  33.8 2.8 %collective-permute-start.4 = (bf16[4,144,1024]{2,1,0:T(8,128)(2,1)S(1)}, bf16[4,144,1024]{2,1,0:T(8,128)(2,1)S(1)}, u32[]{:S(2)}, u32[]{:S(2)}) collective-permute-start(bf16[4,144,1024]{2,1,0:T(8,128)(2,1)S(1)} %pad_maximum_fusion.refs_0_), channel_id=1, source_target_pairs={{0,3},{1,0},{2,1},{3,2},{4,7},{5,4},{6,5},{7,6},{8,11},{9,8},{10,9... | collective-permute-start | bytes 3538952 | tf_op jit(solution)/shard_map/ppermute | solution.py:23
  36.6 0.0 collective-permute-start.3
  36.6 9.0 %encode.3.refs_11_ = bf16[128,1024]{1,0:T(8,128)(2,1)} custom-call(bf16[4,128,1024]{2,1,0:T(8,128)(2,1)} %bitcast.26, bf16[1024,4096]{1,0:T(8,128)(2,1)} %refs_1_.1, f32[1,4096]{1,0:T(1,128)} %bitcast.32, bf16[4096,1024]{1,0:T(8,128)(2,1)} %refs_3_.1, f32[1,1024]{1,0:T(1,128)} %bitcast.34, f32[1,1024]{1,0:T(1,128)} %bitcast.36, f32[1,1024]{1,0:T(1,128)} %bitcast.38), custom_call_target="tpu_custom_call" | custom-call | flops 2147483648 | bytes 17825792 | tf_op jit(solution)/shard_map/encode/pallas_call | solution.py:150
  45.6 0.0 copy-start
  45.6 0.0 copy-start.1
  45.6 0.0 collective-permute-done.8.refs_14_
  45.6 0.0 collective-permute-done.7.refs_12_
  45.6 2.5 %collective-permute-start.9 = (bf16[400,1024]{1,0:T(8,128)(2,1)}, bf16[400,1024]{1,0:T(8,128)(2,1)S(1)}, u32[]{:S(2)}, u32[]{:S(2)}) collective-permute-start(bf16[400,1024]{1,0:T(8,128)(2,1)} %collective-permute-done.7.refs_12_), channel_id=1, source_target_pairs={{0,4},{1,5},{2,6},{3,7},{4,8},{5,9},{6,10},{7,11},{8,12},{9,13},{1... | collective-permute-start | bytes 2457608 | tf_op jit(solution)/shard_map/ppermute | solution.py:23
  48.2 0.0 collective-permute-start.11
  48.2 2.7 %collective-permute-start.10 = (bf16[128,1024]{1,0:T(8,128)(2,1)}, bf16[128,1024]{1,0:T(8,128)(2,1)S(1)}, u32[]{:S(2)}, u32[]{:S(2)}) collective-permute-start(bf16[128,1024]{1,0:T(8,128)(2,1)} %encode.3.refs_11_), channel_id=1, source_target_pairs={{0,4},{1,5},{2,6},{3,7},{4,8},{5,9},{6,10},{7,11},{8,12},{9,13},{1... | collective-permute-start | bytes 786440 | tf_op jit(solution)/shard_map/ppermute | solution.py:23
  50.9 0.0 collective-permute-done.4.refs_2_
  50.9 2.7 %collective-permute-start.6 = (bf16[2,144,1024]{2,1,0:T(8,128)(2,1)S(1)}, bf16[2,144,1024]{2,1,0:T(8,128)(2,1)S(1)}, u32[]{:S(2)}, u32[]{:S(2)}) collective-permute-start(bf16[2,144,1024]{2,1,0:T(8,128)(2,1)S(1)} %slice.9), channel_id=1, source_target_pairs={{0,3},{1,0},{2,1},{3,2},{4,7},{5,4},{6,5},{7,6},{8,11},{9,8},{10,9... | collective-permute-start | bytes 1769480 | tf_op jit(solution)/shard_map/ppermute | solution.py:23
  53.6 0.0 collective-permute-done.3.refs_1_
  53.7 0.1 collective-permute-start.5
  53.8 3.9 %collective-permute-done.11.refs_15_ = bf16[128,1024]{1,0:T(8,128)(2,1)S(1)} collective-permute-done((bf16[128,1024]{1,0:T(8,128)(2,1)}, bf16[128,1024]{1,0:T(8,128)(2,1)S(1)}, u32[]{:S(2)}, u32[]{:S(2)}) %collective-permute-start.11) | collective-permute-done | bytes 262176 | tf_op jit(solution)/shard_map/ppermute | solution.py:23
  57.7 1.3 %collective-permute-start.12 = (bf16[4,144,1024]{2,1,0:T(8,128)(2,1)S(1)}, bf16[4,144,1024]{2,1,0:T(8,128)(2,1)S(1)}, u32[]{:S(2)}, u32[]{:S(2)}) collective-permute-start(bf16[4,144,1024]{2,1,0:T(8,128)(2,1)S(1)} %pad_maximum_fusion.refs_0_), channel_id=1, source_target_pairs={{0,16},{1,17},{2,18},{3,19},{4,20},{5,21},{6,22},{7,23},{8,24},{9,... | collective-permute-start | bytes 3538952 | tf_op jit(solution)/shard_map/ppermute | solution.py:23
  58.9 4.5 %collective-permute-done.10.refs_13_ = bf16[128,1024]{1,0:T(8,128)(2,1)S(1)} collective-permute-done((bf16[128,1024]{1,0:T(8,128)(2,1)}, bf16[128,1024]{1,0:T(8,128)(2,1)S(1)}, u32[]{:S(2)}, u32[]{:S(2)}) %collective-permute-start.10) | collective-permute-done | bytes 262176 | tf_op jit(solution)/shard_map/ppermute | solution.py:23
  63.4 3.7 %collective-permute-start.13 = (bf16[4,144,1024]{2,1,0:T(8,128)(2,1)S(1)}, bf16[4,144,1024]{2,1,0:T(8,128)(2,1)S(1)}, u32[]{:S(2)}, u32[]{:S(2)}) collective-permute-start(bf16[4,144,1024]{2,1,0:T(8,128)(2,1)S(1)} %collective-permute-done.3.refs_1_), channel_id=1, source_target_pairs={{0,16},{1,17},{2,18},{3,19},{4,20},{5,21},{6,22},{7,23},{8,24},{9,... | collective-permute-start | bytes 3538952 | tf_op jit(solution)/shard_map/ppermute | solution.py:23
  67.1 0.0 collective-permute-done.9.refs_16_
  67.1 0.0 collective-permute-start.14
  67.1 0.0 collective-permute-done.6.refs_4_
  67.1 0.0 collective-permute-done.5.refs_3_
  67.1 0.1 collective-permute-start.17
  67.2 1.9 %collective-permute-start.15 = (bf16[2,144,1024]{2,1,0:T(8,128)(2,1)S(1)}, bf16[2,144,1024]{2,1,0:T(8,128)(2,1)S(1)}, u32[]{:S(2)}, u32[]{:S(2)}) collective-permute-start(bf16[2,144,1024]{2,1,0:T(8,128)(2,1)S(1)} %collective-permute-done.5.refs_3_), channel_id=1, source_target_pairs={{0,16},{1,17},{2,18},{3,19},{4,20},{5,21},{6,22},{7,23},{8,24},{9,... | collective-permute-start | bytes 1769480 | tf_op jit(solution)/shard_map/ppermute | solution.py:23
  69.1 3.6 %collective-permute-done.17.refs_17_ = bf16[128,1024]{1,0:T(8,128)(2,1)S(1)} collective-permute-done((bf16[128,1024]{1,0:T(8,128)(2,1)S(1)}, bf16[128,1024]{1,0:T(8,128)(2,1)S(1)}, u32[]{:S(2)}, u32[]{:S(2)}) %collective-permute-start.17) | collective-permute-done | bytes 262176 | tf_op jit(solution)/shard_map/ppermute | solution.py:23
  72.7 2.5 %collective-permute-start.16 = (bf16[2,144,1024]{2,1,0:T(8,128)(2,1)S(1)}, bf16[2,144,1024]{2,1,0:T(8,128)(2,1)S(1)}, u32[]{:S(2)}, u32[]{:S(2)}) collective-permute-start(bf16[2,144,1024]{2,1,0:T(8,128)(2,1)S(1)} %collective-permute-done.6.refs_4_), channel_id=1, source_target_pairs={{0,16},{1,17},{2,18},{3,19},{4,20},{5,21},{6,22},{7,23},{8,24},{9,... | collective-permute-start | bytes 1769480 | tf_op jit(solution)/shard_map/ppermute | solution.py:23
  75.2 0.0 collective-permute-done.12.refs_5_
  75.2 0.0 collective-permute-done.13.refs_6_
  75.2 0.0 collective-permute-done.14.refs_7_
  75.2 0.0 collective-permute-done.15.refs_8_
  75.2 1.6 %collective-permute-done.16.refs_9_ = bf16[2,144,1024]{2,1,0:T(8,128)(2,1)S(1)} collective-permute-done((bf16[2,144,1024]{2,1,0:T(8,128)(2,1)S(1)}, bf16[2,144,1024]{2,1,0:T(8,128)(2,1)S(1)}, u32[]{:S(2)}, u32[]{:S(2)}) %collective-permute-start.16) | collective-permute-done | bytes 589856 | tf_op jit(solution)/shard_map/ppermute | solution.py:23
  76.8 0.0 copy-done
  76.8 0.0 copy-done.1
  76.8 7.1 %score_pairs.1 = f32[128,1,128]{2,1,0:T(1,128)S(1)} custom-call(s32[4]{0:T(128)S(1)} %pad_add_fusion.pos_ref, s32[1]{0:T(128)} %bitcast.24.count_ref, bf16[4,144,1024]{2,1,0:T(8,128)(2,1)S(1)} %pad_maximum_fusion.refs_0_, bf16[4,144,1024]{2,1,0:T(8,128)(2,1)S(1)} %collective-permute-done.3.refs_1_, bf16[4,144,1024]{2,1,0:T(8,128)(2,1)S(1)} %collective-permute-done.4.refs_2_, ...), custom_call_target="tpu_custom_call" | custom-call | tf_op jit(solution)/shard_map/score_pairs/pallas_call | solution.py:324
  84.0 14.6 %all_to_all.5.got_ref = f32[128,1,128]{2,1,0:T(1,128)} all-to-all(f32[128,1,128]{2,1,0:T(1,128)S(1)} %score_pairs.1), channel_id=1, replica_groups=mesh['dp'=8,'prompt'=16] {'dp','prompt'}, dimensions={0} | all-to-all | bytes 131072 | tf_op jit(solution)/shard_map/all_to_all | solution.py:394
  98.6 1.6 %finish.1 = (f32[3,1,1,32]{3,2,1,0:T(1,128)}, f32[1,3]{1,0:T(1,128)}) custom-call(f32[128,1,128]{2,1,0:T(1,128)} %all_to_all.5.got_ref), custom_call_target="tpu_custom_call" | custom-call | tf_op jit(solution)/shard_map/finish/pallas_call | solution.py:395
  (2 shorter events, 0.1 us)
Async XLA Ops:
  17.5 11.7 %collective-permute-start.2 = (bf16[144,1024]{1,0:T(8,128)(2,1)}, bf16[144,1024]{1,0:T(8,128)(2,1)S(1)}, u32[]{:S(2)}, u32[]{:S(2)}) collective-permute-start(bf16[144,1024]{1,0:T(8,128)(2,1)} %get-tuple-element.22), channel_id=1, source_target_pairs={{0,96},{1,97},{2,98},{3,99},{4,100},{5,101},{6,102},{7,103},{8,104... | collective-permute-start | bytes 884744 | tf_op jit(solution)/shard_map/ppermute | solution.py:23
  22.1 7.6 %collective-permute-start.1 = (bf16[144,1024]{1,0:T(8,128)(2,1)}, bf16[144,1024]{1,0:T(8,128)(2,1)S(1)}, u32[]{:S(2)}, u32[]{:S(2)}) collective-permute-start(bf16[144,1024]{1,0:T(8,128)(2,1)} %get-tuple-element.22), channel_id=1, source_target_pairs={{0,64},{1,65},{2,66},{3,67},{4,68},{5,69},{6,70},{7,71},{8,72},{9,... | collective-permute-start | bytes 884744 | tf_op jit(solution)/shard_map/ppermute | solution.py:23
  22.1 10.6 %collective-permute-start = (bf16[144,1024]{1,0:T(8,128)(2,1)}, bf16[144,1024]{1,0:T(8,128)(2,1)S(1)}, u32[]{:S(2)}, u32[]{:S(2)}) collective-permute-start(bf16[144,1024]{1,0:T(8,128)(2,1)} %get-tuple-element.22), channel_id=1, source_target_pairs={{0,32},{1,33},{2,34},{3,35},{4,36},{5,37},{6,38},{7,39},{8,40},{9,... | collective-permute-start | bytes 884744 | tf_op jit(solution)/shard_map/ppermute | solution.py:23
  22.8 22.8 %collective-permute-start.8 = (bf16[400,1024]{1,0:T(8,128)(2,1)}, bf16[400,1024]{1,0:T(8,128)(2,1)}, u32[]{:S(2)}, u32[]{:S(2)}) collective-permute-start(bf16[400,1024]{1,0:T(8,128)(2,1)} %get-tuple-element.30.refs_10_), channel_id=1, source_target_pairs={{0,12},{1,13},{2,14},{3,15},{4,0},{5,1},{6,2},{7,3},{8,4},{9,5},{1... | collective-permute-start | bytes 2457608 | tf_op jit(solution)/shard_map/ppermute | solution.py:23
  24.0 21.6 %collective-permute-start.7 = (bf16[400,1024]{1,0:T(8,128)(2,1)}, bf16[400,1024]{1,0:T(8,128)(2,1)}, u32[]{:S(2)}, u32[]{:S(2)}) collective-permute-start(bf16[400,1024]{1,0:T(8,128)(2,1)} %get-tuple-element.30.refs_10_), channel_id=1, source_target_pairs={{0,4},{1,5},{2,6},{3,7},{4,8},{5,9},{6,10},{7,11},{8,12},{9,13},{1... | collective-permute-start | bytes 2457608 | tf_op jit(solution)/shard_map/ppermute | solution.py:23
  33.8 17.1 %collective-permute-start.4 = (bf16[4,144,1024]{2,1,0:T(8,128)(2,1)S(1)}, bf16[4,144,1024]{2,1,0:T(8,128)(2,1)S(1)}, u32[]{:S(2)}, u32[]{:S(2)}) collective-permute-start(bf16[4,144,1024]{2,1,0:T(8,128)(2,1)S(1)} %pad_maximum_fusion.refs_0_), channel_id=1, source_target_pairs={{0,3},{1,0},{2,1},{3,2},{4,7},{5,4},{6,5},{7,6},{8,11},{9,8},{10,9... | collective-permute-start | bytes 3538952 | tf_op jit(solution)/shard_map/ppermute | solution.py:23
  36.6 17.1 %collective-permute-start.3 = (bf16[4,144,1024]{2,1,0:T(8,128)(2,1)S(1)}, bf16[4,144,1024]{2,1,0:T(8,128)(2,1)S(1)}, u32[]{:S(2)}, u32[]{:S(2)}) collective-permute-start(bf16[4,144,1024]{2,1,0:T(8,128)(2,1)S(1)} %pad_maximum_fusion.refs_0_), channel_id=1, source_target_pairs={{0,1},{1,2},{2,3},{3,0},{4,5},{5,6},{6,7},{7,4},{8,9},{9,10},{10,1... | collective-permute-start | bytes 3538952 | tf_op jit(solution)/shard_map/ppermute | solution.py:23
  45.6 31.2 %copy-start = (bf16[128,1024]{1,0:T(8,128)(2,1)S(1)}, bf16[128,1024]{1,0:T(8,128)(2,1)}, u32[]{:S(2)}) copy-start(bf16[128,1024]{1,0:T(8,128)(2,1)} %encode.3.refs_11_) | copy-start | bytes 786436
  45.6 31.2 %copy-start.1 = (bf16[400,1024]{1,0:T(8,128)(2,1)S(1)}, bf16[400,1024]{1,0:T(8,128)(2,1)}, u32[]{:S(2)}) copy-start(bf16[400,1024]{1,0:T(8,128)(2,1)} %get-tuple-element.30.refs_10_) | copy-start | bytes 2457604
  45.6 21.5 %collective-permute-start.9 = (bf16[400,1024]{1,0:T(8,128)(2,1)}, bf16[400,1024]{1,0:T(8,128)(2,1)S(1)}, u32[]{:S(2)}, u32[]{:S(2)}) collective-permute-start(bf16[400,1024]{1,0:T(8,128)(2,1)} %collective-permute-done.7.refs_12_), channel_id=1, source_target_pairs={{0,4},{1,5},{2,6},{3,7},{4,8},{5,9},{6,10},{7,11},{8,12},{9,13},{1... | collective-permute-start | bytes 2457608 | tf_op jit(solution)/shard_map/ppermute | solution.py:23
  48.2 9.5 %collective-permute-start.11 = (bf16[128,1024]{1,0:T(8,128)(2,1)}, bf16[128,1024]{1,0:T(8,128)(2,1)S(1)}, u32[]{:S(2)}, u32[]{:S(2)}) collective-permute-start(bf16[128,1024]{1,0:T(8,128)(2,1)} %encode.3.refs_11_), channel_id=1, source_target_pairs={{0,12},{1,13},{2,14},{3,15},{4,0},{5,1},{6,2},{7,3},{8,4},{9,5},{1... | collective-permute-start | bytes 786440 | tf_op jit(solution)/shard_map/ppermute | solution.py:23
  48.2 15.2 %collective-permute-start.10 = (bf16[128,1024]{1,0:T(8,128)(2,1)}, bf16[128,1024]{1,0:T(8,128)(2,1)S(1)}, u32[]{:S(2)}, u32[]{:S(2)}) collective-permute-start(bf16[128,1024]{1,0:T(8,128)(2,1)} %encode.3.refs_11_), channel_id=1, source_target_pairs={{0,4},{1,5},{2,6},{3,7},{4,8},{5,9},{6,10},{7,11},{8,12},{9,13},{1... | collective-permute-start | bytes 786440 | tf_op jit(solution)/shard_map/ppermute | solution.py:23
  50.9 16.2 %collective-permute-start.6 = (bf16[2,144,1024]{2,1,0:T(8,128)(2,1)S(1)}, bf16[2,144,1024]{2,1,0:T(8,128)(2,1)S(1)}, u32[]{:S(2)}, u32[]{:S(2)}) collective-permute-start(bf16[2,144,1024]{2,1,0:T(8,128)(2,1)S(1)} %slice.9), channel_id=1, source_target_pairs={{0,3},{1,0},{2,1},{3,2},{4,7},{5,4},{6,5},{7,6},{8,11},{9,8},{10,9... | collective-permute-start | bytes 1769480 | tf_op jit(solution)/shard_map/ppermute | solution.py:23
  53.7 13.4 %collective-permute-start.5 = (bf16[2,144,1024]{2,1,0:T(8,128)(2,1)S(1)}, bf16[2,144,1024]{2,1,0:T(8,128)(2,1)S(1)}, u32[]{:S(2)}, u32[]{:S(2)}) collective-permute-start(bf16[2,144,1024]{2,1,0:T(8,128)(2,1)S(1)} %slice.8), channel_id=1, source_target_pairs={{0,1},{1,2},{2,3},{3,0},{4,5},{5,6},{6,7},{7,4},{8,9},{9,10},{10,1... | collective-permute-start | bytes 1769480 | tf_op jit(solution)/shard_map/ppermute | solution.py:23
  57.7 17.5 %collective-permute-start.12 = (bf16[4,144,1024]{2,1,0:T(8,128)(2,1)S(1)}, bf16[4,144,1024]{2,1,0:T(8,128)(2,1)S(1)}, u32[]{:S(2)}, u32[]{:S(2)}) collective-permute-start(bf16[4,144,1024]{2,1,0:T(8,128)(2,1)S(1)} %pad_maximum_fusion.refs_0_), channel_id=1, source_target_pairs={{0,16},{1,17},{2,18},{3,19},{4,20},{5,21},{6,22},{7,23},{8,24},{9,... | collective-permute-start | bytes 3538952 | tf_op jit(solution)/shard_map/ppermute | solution.py:23
  63.4 11.8 %collective-permute-start.13 = (bf16[4,144,1024]{2,1,0:T(8,128)(2,1)S(1)}, bf16[4,144,1024]{2,1,0:T(8,128)(2,1)S(1)}, u32[]{:S(2)}, u32[]{:S(2)}) collective-permute-start(bf16[4,144,1024]{2,1,0:T(8,128)(2,1)S(1)} %collective-permute-done.3.refs_1_), channel_id=1, source_target_pairs={{0,16},{1,17},{2,18},{3,19},{4,20},{5,21},{6,22},{7,23},{8,24},{9,... | collective-permute-start | bytes 3538952 | tf_op jit(solution)/shard_map/ppermute | solution.py:23
  67.1 8.1 %collective-permute-start.14 = (bf16[4,144,1024]{2,1,0:T(8,128)(2,1)S(1)}, bf16[4,144,1024]{2,1,0:T(8,128)(2,1)S(1)}, u32[]{:S(2)}, u32[]{:S(2)}) collective-permute-start(bf16[4,144,1024]{2,1,0:T(8,128)(2,1)S(1)} %collective-permute-done.4.refs_2_), channel_id=1, source_target_pairs={{0,16},{1,17},{2,18},{3,19},{4,20},{5,21},{6,22},{7,23},{8,24},{9,... | collective-permute-start | bytes 3538952 | tf_op jit(solution)/shard_map/ppermute | solution.py:23
  67.1 5.6 %collective-permute-start.17 = (bf16[128,1024]{1,0:T(8,128)(2,1)S(1)}, bf16[128,1024]{1,0:T(8,128)(2,1)S(1)}, u32[]{:S(2)}, u32[]{:S(2)}) collective-permute-start(bf16[128,1024]{1,0:T(8,128)(2,1)S(1)} %collective-permute-done.10.refs_13_), channel_id=1, source_target_pairs={{0,4},{1,5},{2,6},{3,7},{4,8},{5,9},{6,10},{7,11},{8,12},{9,13},{1... | collective-permute-start | bytes 786440 | tf_op jit(solution)/shard_map/ppermute | solution.py:23
  67.2 8.0 %collective-permute-start.15 = (bf16[2,144,1024]{2,1,0:T(8,128)(2,1)S(1)}, bf16[2,144,1024]{2,1,0:T(8,128)(2,1)S(1)}, u32[]{:S(2)}, u32[]{:S(2)}) collective-permute-start(bf16[2,144,1024]{2,1,0:T(8,128)(2,1)S(1)} %collective-permute-done.5.refs_3_), channel_id=1, source_target_pairs={{0,16},{1,17},{2,18},{3,19},{4,20},{5,21},{6,22},{7,23},{8,24},{9,... | collective-permute-start | bytes 1769480 | tf_op jit(solution)/shard_map/ppermute | solution.py:23
  72.7 4.1 %collective-permute-start.16 = (bf16[2,144,1024]{2,1,0:T(8,128)(2,1)S(1)}, bf16[2,144,1024]{2,1,0:T(8,128)(2,1)S(1)}, u32[]{:S(2)}, u32[]{:S(2)}) collective-permute-start(bf16[2,144,1024]{2,1,0:T(8,128)(2,1)S(1)} %collective-permute-done.6.refs_4_), channel_id=1, source_target_pairs={{0,16},{1,17},{2,18},{3,19},{4,20},{5,21},{6,22},{7,23},{8,24},{9,... | collective-permute-start | bytes 1769480 | tf_op jit(solution)/shard_map/ppermute | solution.py:23
